TPU v7x, 512 devices: a whole 4x4x16 slice. The times are simulated.
512 devices in a mesh: feat: 16 (over z), img: 32 (over x, y, core).
Axes of the slice: x: 4, y: 4, z: 16, core: 2. Of those that a mesh axis runs over, the one named last changes fastest.
Arguments:
- features: bfloat16 [1792, 61440], P('img', 'feat'), may hold values from -6 to 6
- proj_in: bfloat16 [61440, 768], P('feat', 'img'), may hold values from -0.0234375 to 0.0234375
- proj_out: bfloat16 [768, 512], P('feat'), may hold values from -0.21875 to 0.21875
- centres: bfloat16 [262144, 512], P(('feat', 'img')), may hold values from -0.25 to 0.25
- labels: int32 [1792], P('img'), may hold values from 0 to 262143
Outputs:
- centre_grad: float32 [262144, 512], P(('feat', 'img'))
- emb_grad: float32 [1792, 512], P('img', 'feat')
Inputs may be any that keep to these rules, and one draw needn't show every extreme that they name: `labels`: each image's identity is among the sampled centres, at this position.
All inputs are finite; a program needn't handle non-finite values.
Results may differ from a plain program's by a relative error of at most 0.006.
Values may be sent and summed in bfloat16 or wider, within the bound.
No kernel may reach another device: no remote copies, remote signals or barrier semaphores. Data moves between devices by JAX's collectives and lax.ppermute only.
A program may use at most 64 MiB of HBM per device.

v0:
```python
import jax
import jax.numpy as jnp
from jax import lax
from jax.sharding import PartitionSpec as P

norm_eps = 1e-06
scale_logit = 64.0
margin_angle = 0.5
sine_floor = 0.04


def per_device(features, proj_in, proj_out, centres, labels):
    emb_width = proj_out.shape[1]
    partial_hidden = jnp.dot(
        features,
        lax.all_gather(proj_in, "img", axis=1, tiled=True),
        preferred_element_type=jnp.float32,
    )
    hidden = lax.psum(partial_hidden, "feat").astype(jnp.bfloat16)
    embed = jnp.dot(
        hidden,
        lax.all_gather(proj_out, "feat", axis=0, tiled=True),
        preferred_element_type=jnp.float32,
    )
    inverse = lax.rsqrt(jnp.sum(embed * embed, axis=1) + norm_eps)
    unit = embed * inverse[:, None]
    unit_low = unit.astype(jnp.bfloat16)
    all_units, all_labels = (
        lax.all_gather(unit_low, "img", axis=0, tiled=True),
        lax.all_gather(labels, "img", axis=0, tiled=True),
    )
    cen_rows = centres.shape[0]
    wide = centres.astype(jnp.float32)
    cinv = lax.rsqrt(jnp.sum(wide * wide, axis=1) + norm_eps)
    unit_centre = wide * cinv[:, None]
    centre_low = unit_centre.astype(jnp.bfloat16)
    cosine = jnp.dot(all_units, centre_low.T, preferred_element_type=jnp.float32)
    begin = lax.axis_index(("feat", "img")) * cen_rows
    position = begin + jnp.arange(cen_rows, dtype=jnp.int32)
    target = all_labels[:, None] == position[None, :]
    cos_m = jnp.cos(jnp.float32(margin_angle))
    sin_m = jnp.sin(jnp.float32(margin_angle))
    inner = 1.0 - cosine * cosine
    sine = jnp.sqrt(jnp.maximum(inner, sine_floor))
    logit = jnp.where(target, scale_logit * (cosine * cos_m - sine * sin_m), scale_logit * cosine)
    exps = jnp.exp(logit)
    total = lax.psum(jnp.sum(exps, axis=1), ("feat", "img"))
    dlogit = exps / total[:, None] - target.astype(jnp.float32)
    slope = cos_m + jnp.where(inner > sine_floor, sin_m * cosine / sine, 0.0)
    dcos = (dlogit * scale_logit * jnp.where(target, slope, 1.0)).astype(jnp.bfloat16)
    gunit = jnp.dot(dcos.T, all_units, preferred_element_type=jnp.float32)
    centre_grad = cinv[:, None] * (
        gunit - unit_centre * jnp.sum(unit_centre * gunit, axis=1, keepdims=True)
    )
    dunit_terms = jnp.dot(dcos, centre_low, preferred_element_type=jnp.float32)
    slice_width = emb_width // lax.axis_size("feat")
    col_start = lax.axis_index("feat") * slice_width
    row_sums = lax.psum_scatter(dunit_terms, "img", scatter_dimension=0, tiled=True)
    dunit = lax.psum(row_sums, "feat")
    full_grad = inverse[:, None] * (dunit - unit * jnp.sum(unit * dunit, axis=1, keepdims=True))
    emb_grad = lax.dynamic_slice_in_dim(full_grad, col_start, slice_width, 1)
    return (centre_grad, emb_grad)


def solution(mesh):
    return jax.shard_map(
        per_device,
        mesh=mesh,
        in_specs=(
            P("img", "feat"),
            P("feat", "img"),
            P("feat", None),
            P(("feat", "img"), None),
            P("img"),
        ),
        out_specs=(P(("feat", "img"), None), P("img", "feat")),
        check_vma=False,
    )
```

profile of v0, /device:TPU:6, one launch (start us, length us, event | category | flops | bytes accessed | tf_op | source)
XLA Modules:
  0.0 562.6 jit_solution(8354672069626509758)
XLA Ops:
  7.2 0.7 all-gather.3.cloned.1.call-update
  8.0 40.2 %all_gather.14 = bf16[768,512]{1,0:T(8,128)(2,1)S(1)} all-gather(bf16[48,512]{1,0:T(8,128)(2,1)} %param.7), channel_id=1, replica_groups=mesh['feat'=16,'img'=32] {'feat'}, dimensions={0}, use_global_device_ids=true | all-gather | bytes 835584 | tf_op jit(solution)/shard_map/all_gather | solution.py:22
  48.2 30.2 %all-gather.3.cloned.1.call-done = bf16[3840,768]{0,1:T(8,128)(2,1)} async-done(((bf16[3840,24]{0,1:T(8,128)(2,1)}), bf16[3840,768]{0,1:T(8,128)(2,1)}) %all-gather.3.cloned.1.call-update) | async-done | bytes 5898256 | tf_op jit(solution)/shard_map/all_gather | solution.py:16
  78.4 4.6 fusion.21
  83.0 58.5 %all-reduce.5 = bf16[56,768]{1,0:T(8,128)(2,1)S(1)} all-reduce(f32[56,768]{1,0:T(8,128)S(1)} %fusion.21), channel_id=1, replica_groups=mesh['feat'=16,'img'=32] {'feat'}, use_global_device_ids=true, to_apply=%region_1.0 | all-reduce | flops 43008 | bytes 258048 | tf_op jit(solution)/shard_map/psum | solution.py:19
  141.5 0.3 multiply_reduce_fusion.1
  141.8 0.7 fusion.20
  142.6 0.2 copy.7
  142.9 1.3 dynamic-slice
  144.8 0.3 dynamic-update-slice
  145.0 14.7 %all-reduce = s32[1792]{0:T(1024)S(1)} all-reduce(s32[1792]{0:T(1024)S(1)} %dynamic-update-slice), channel_id=1, replica_groups=mesh['feat'=16,'img'=32] {'img'}, use_global_device_ids=true, to_apply=%add | all-reduce | flops 1792 | bytes 14336
  159.9 37.4 %all-gather.5.cloned.1.call-done = bf16[1792,512]{1,0:T(8,128)(2,1)} async-done(((bf16[56,512]{1,0:T(8,128)(2,1)}), bf16[1792,512]{1,0:T(8,128)(2,1)}) %all-gather.5.cloned.1.call-update) | async-done | bytes 1835024 | tf_op jit(solution)/shard_map/all_gather | solution.py:29
  197.3 6.0 %fusion.5 = (f32[1792]{0:T(1024)S(1)}, f32[1792,512]{0,1:T(8,128)}) fusion(s32[1792]{0:T(1024)S(1)} %all-reduce, s32[512]{0:T(512)S(1)} %iota_add_fusion, bf16[1792,512]{1,0:T(8,128)(2,1)} %all-gather.5.cloned.1.call-done, bf16[512,512]{0,1:T(8,128)(2,1)S(1)} %copy.7, f32[512]{0:T(512)S(1)} %add_rsqrt_fusion), kind=kOutput, calls=%fused_computation.10 | convolution fusion | flops 950401280 | bytes 6047744 | tf_op jit(solution)/shard_map/dot_general | solution.py:37
  203.4 104.1 %psum.22 = f32[1792]{0:T(1024)S(1)} all-reduce(f32[1792]{0:T(1024)S(1)} %get-tuple-element.8), channel_id=1, replica_groups=mesh['feat'=16,'img'=32] {'feat','img'}, use_global_device_ids=true, to_apply=%region_4.5 | all-reduce | flops 1792 | bytes 14336 | tf_op jit(solution)/shard_map/psum | solution.py:47
  307.5 5.5 fusion.4
  313.0 3.0 fusion.13
  316.0 3.6 fusion.9
  319.7 95.7 %reduce-scatter.2.cloned.1.call-done = f32[56,512]{1,0:T(8,128)} async-done(((f32[1792,512]{1,0:T(8,128)}), f32[56,512]{1,0:T(8,128)}) %reduce-scatter.2.cloned.1.call-update) | async-done | bytes 114704 | tf_op jit(solution)/shard_map/reduce_scatter | solution.py:58
  415.4 1.4 fusion.11
  416.8 1.3 copy.8
  418.1 135.4 %all-reduce.4.cloned.1.call-done = f32[56,512]{1,0:T(8,128)} async-done(((f32[56,512]{1,0:T(8,128)}), f32[56,512]{1,0:T(8,128)}) %all-reduce.4.cloned.1.call-update) | async-done | bytes 114704 | tf_op jit(solution)/shard_map/psum | solution.py:59
  553.5 1.0 multiply_reduce_fusion
  554.5 0.9 fusion.19
  555.4 0.7 copy.9
  (18 shorter events, 0.4 us)
Async XLA Ops:
  7.2 71.2 %copy-start = (bf16[56,3840]{1,0:T(8,128)(2,1)S(1)}, bf16[56,3840]{1,0:T(8,128)(2,1)}, u32[]{:S(2)}) copy-start(bf16[56,3840]{1,0:T(8,128)(2,1)} %param.5) | copy-start | bytes 1290244
  7.2 71.2 %all-gather.3.cloned.1.call-start = ((), (), s32[]{:S(2)}) async-start(), calls=%async_computation.1 | async-start | bytes 6082560 | tf_op jit(solution)/shard_map/all_gather | solution.py:16
  7.9 189.4 %all-gather.5.cloned.1.call-start = ((), (), s32[]{:S(2)}) async-start(), calls=%async_computation.2 | async-start | bytes 1892352 | tf_op jit(solution)/shard_map/all_gather | solution.py:29
  48.2 94.5 %copy-start.1 = (bf16[512,512]{1,0:T(8,128)(2,1)S(1)}, bf16[512,512]{1,0:T(8,128)(2,1)}, u32[]{:S(2)}) copy-start(bf16[512,512]{1,0:T(8,128)(2,1)} %param.8) | copy-start | bytes 1572868
  48.2 96.6 %copy-start.2 = (s32[56]{0:T(128)S(1)}, s32[56]{0:T(128)}, u32[]{:S(2)}) copy-start(s32[56]{0:T(128)} %param.9) | copy-start | bytes 676
  142.6 272.8 %reduce-scatter.2.cloned.1.call-start = ((), (), s32[]{:S(2)}) async-start(), calls=%async_computation.3 | async-start | bytes 3784704 | tf_op jit(solution)/shard_map/reduce_scatter | solution.py:58
  316.0 237.5 %all-reduce.4.cloned.1.call-start = ((), (), s32[]{:S(2)}) async-start(), calls=%async_computation.4 | async-start | bytes 229376 | tf_op jit(solution)/shard_map/psum | solution.py:59
Sparse Core Ops, SparseCore 0:
  11.2 67.1 all-gather.2
  142.7 54.6 all-gather.4
  316.1 99.2 reduce-scatter.1
  417.5 135.9 all-reduce.3
where the time goes:
time: 563 us
  waiting for transfers between devices  299 us (53%)
  blocking collectives  218 us (39%)
  matrix products  17.5 us (3%)
  between operations  14.5 us (3%)
  other arithmetic  9.65 us (2%)
    psum x1, waiting for transfers between devices, per_device(): dunit = lax.psum(row_sums, 'feat')  135 us
    psum x1, blocking collectives, per_device(): total = lax.psum(jnp.sum(exps, axis=1), ('feat', 'img'))  104 us
    reduce_scatter x1, waiting for transfers between devices, per_device(): lax.psum_scatter(dunit_terms, 'img', scatter_dimension=0, tiled=True)  95.7 us
    psum x1, blocking collectives, per_device(): hidden = lax.psum(partial_hidden, 'feat').astype(jnp.bfloat16)  58.5 us
    all_gather x1, blocking collectives, per_device(): lax.all_gather(proj_out, 'feat', axis=0, tiled=True)  40.2 us
    all_gather x1, waiting for transfers between devices, per_device(): lax.all_gather(unit_low, 'img', axis=0, tiled=True)  37.4 us
    all_gather x1, waiting for transfers between devices, per_device(): lax.all_gather(proj_in, 'img', axis=1, tiled=True)  30.2 us
    unnamed x1, blocking collectives  14.7 us
  transfers between devices with their start and end apart: 4, of which 4 were waited for; matrix products, arithmetic and copies ran while one was open for 1% of the time, Pallas kernels for 0%

commit v1 on v0

v1 whole, which is shorter than its diff:
```python
import jax
import jax.numpy as jnp
import numpy as np
from jax import lax
from jax.sharding import Mesh, PartitionSpec as P

norm_eps = 1e-06
scale_logit = 64.0
margin_angle = 0.5
sine_floor = 0.04

NZ, NX, NY, NC = 16, 4, 4, 2
XY = ("x", "y")
SWAP = [(0, 1), (1, 0)]
f32 = jnp.float32
bf16 = jnp.bfloat16


def exchange(blocks, axis):
    return lax.all_to_all(blocks, axis, 0, 0)


def spread(block, axis, count):
    return exchange(jnp.broadcast_to(block[None], (count,) + block.shape), axis)


def partner(block):
    return lax.ppermute(block, "c", SWAP)


def exact_dot(left, right):
    return jnp.dot(left, right.astype(f32), precision=lax.Precision.HIGHEST, preferred_element_type=f32)


def per_device(features, proj_in, proj_out, centres, labels):
    rows, feats = features.shape
    cols = proj_in.shape[1]
    emb = proj_out.shape[1]
    cen = centres.shape[0]
    images = NX * NY * rows
    zi, xi, yi, ci = (lax.axis_index(a) for a in ("z", "x", "y", "c"))

    wide_rows = spread(features, "x", NX).reshape(NX * rows, feats)
    own_cols = spread(proj_in.T, "y", NY).reshape(NY * cols, feats)
    other_cols = partner(own_cols)
    out_rows = spread(proj_out, "z", NZ)
    out_rows = lax.dynamic_slice_in_dim(out_rows, NX * xi, NX, 0)
    own_out = lax.dynamic_slice_in_dim(out_rows, cols * ci, cols, 1).reshape(NY * cols, emb)
    other_out = lax.dynamic_slice_in_dim(out_rows, cols * (1 - ci), cols, 1).reshape(NY * cols, emb)

    all_labels = spread(labels, XY, NX * NY).reshape(images, 1)
    wide = centres.astype(f32)
    cinv = lax.rsqrt(jnp.sum(wide * wide, axis=1) + norm_eps)
    unit_centre = wide * cinv[:, None]
    own_low = unit_centre.astype(bf16)
    low = jnp.concatenate([own_low, partner(own_low)], axis=0)
    seat = ((zi * NX + xi) * NY + yi) * NC
    step = jnp.arange(cen, dtype=jnp.int32)
    position = jnp.concatenate([(seat + ci) * cen + step, (seat + 1 - ci) * cen + step])
    target = all_labels == position[None, :]

    def times(weights, cols_of):
        return lax.dot_general(weights, cols_of, (((1,), (1,)), ((), ())), preferred_element_type=f32)

    part = exact_dot(times(wide_rows, own_cols), own_out) + exact_dot(times(wide_rows, other_cols), other_out)
    part = jnp.sum(exchange(part.reshape(NX, rows, emb), "x"), axis=0)
    lanes = emb // 4
    piece = part.reshape(rows, 4, lanes).transpose(1, 0, 2).reshape(NZ, rows // 4, lanes)
    piece = jnp.sum(exchange(piece, "z"), axis=0)
    embed = spread(piece, "z", NZ).reshape(4, rows, lanes).transpose(1, 0, 2).reshape(rows, emb)
    inverse = lax.rsqrt(jnp.sum(embed * embed, axis=1) + norm_eps)
    unit = embed * inverse[:, None]
    units = spread(unit.astype(bf16), XY, NX * NY).reshape(images, emb)

    chosen = jnp.dot(target.astype(bf16), low, preferred_element_type=f32).astype(bf16)
    chosen = jnp.sum(exchange(chosen.reshape(NX * NY, rows, emb), XY).astype(f32), axis=0)

    cos_m = jnp.cos(f32(margin_angle))
    sin_m = jnp.sin(f32(margin_angle))
    cosine = lax.dot_general(units, low, (((1,), (1,)), ((), ())), preferred_element_type=f32)
    inner = 1.0 - cosine * cosine
    sine = jnp.sqrt(jnp.maximum(inner, sine_floor))
    logit = jnp.where(target, scale_logit * (cosine * cos_m - sine * sin_m), scale_logit * cosine)
    exps = jnp.exp(logit)
    slope = cos_m + jnp.where(inner > sine_floor, sin_m * cosine / sine, 0.0)
    rest = jnp.where(target, 0.0, exps)
    rest_sum = jnp.sum(rest, axis=1)
    rest_cos = jnp.sum(rest * cosine, axis=1)
    hit = jnp.sum(jnp.where(target, exps, 0.0), axis=1)
    hit_slope = jnp.sum(jnp.where(target, slope, 0.0), axis=1)
    hit_turn = jnp.sum(jnp.where(target, slope * cosine, 0.0), axis=1)

    sums = jnp.stack([rest_sum, hit, rest_cos, hit_slope, hit_turn], axis=1)
    owned = sums.reshape(NX * NY, rows, 5).transpose(0, 2, 1)
    owned = jnp.pad(owned, ((0, 0), (0, 3), (0, 128 - rows)))
    totals = jnp.pad((rest_sum + hit).reshape(images // 128, 128), ((0, 8 - images // 128), (0, 0)))
    pack = jnp.concatenate([jnp.broadcast_to(totals[None], (NX * NY, 8, 128)), owned], axis=1)
    pack = jnp.sum(exchange(pack, XY), axis=0)
    pack = jnp.sum(spread(pack, "z", NZ), axis=0)
    total = pack[: images // 128].reshape(images, 1)
    own_rest, own_hit, own_cos, own_slope, own_turn = (pack[8 + k, :rows] for k in range(5))

    pull = jnp.dot(rest.astype(bf16), low, preferred_element_type=f32).astype(bf16)
    pull = jnp.sum(exchange(pull.reshape(NX * NY, rows, emb), XY).astype(f32), axis=0)
    width = emb // NZ

    def by_column(block):
        block = block.astype(bf16).reshape(4, rows // 4, NZ, width)
        return block.transpose(2, 1, 0, 3).reshape(NZ, rows // 4, 4 * width)

    both = jnp.concatenate([by_column(pull), by_column(chosen)], axis=1)
    both = jnp.sum(exchange(both, "z").astype(f32), axis=0)

    def by_row(block):
        return block.reshape(rows // 4, 4, width).transpose(1, 0, 2).reshape(rows, width)

    pull, chosen = by_row(both[: rows // 4]), by_row(both[rows // 4 :])

    weight = scale_logit * hit_slope[:, None] * (hit[:, None] / total - 1.0)
    dcos = jnp.where(target, weight, scale_logit * (rest / total)).astype(bf16)
    gunit = lax.dot_general(dcos, units, (((0,), (0,)), ((), ())), preferred_element_type=f32)
    gunit = gunit[:cen] + partner(gunit[cen:])
    centre_grad = cinv[:, None] * (gunit - unit_centre * jnp.sum(unit_centre * gunit, axis=1, keepdims=True))

    own_scale = scale_logit / (own_rest + own_hit)
    dunit = own_scale[:, None] * (pull - (own_rest * own_slope)[:, None] * chosen)
    along = own_scale * (own_cos - own_rest * own_turn)
    unit_cols = lax.dynamic_slice_in_dim(unit, zi * width, width, 1)
    emb_grad = inverse[:, None] * (dunit - unit_cols * along[:, None])
    return (centre_grad, emb_grad)


def solution(mesh):
    fine = Mesh(np.asarray(mesh.devices).reshape(NZ, NX, NY, NC), ("z", "x", "y", "c"))
    img = ("x", "y", "c")
    every = ("z", "x", "y", "c")
    return jax.shard_map(
        per_device,
        mesh=fine,
        in_specs=(P(img, "z"), P("z", img), P("z", None), P(every, None), P(img)),
        out_specs=(P(every, None), P(img, "z")),
        check_vma=False,
    )
```

time: 563 us -> 271 us (0.48)
  waiting for transfers between devices: 299 us -> 83.2 us
  blocking collectives: 218 us -> 73 us
  starting transfers between devices: 0.16 us -> 60.6 us
  between operations: 14.5 us -> 1.09 us
  local copies, waits for them, and re-layouts: 3.74 us -> 16 us
  matrix products: 17.5 us -> 25.4 us
    psum x2 -> x0, blocking collectives: 163 us -> none  [the longest x1 104 us: per_device(): total = lax.psum(jnp.sum(exps, axis=1), ('feat', 'img'))]
    psum x1 -> x0, waiting for transfers between devices: 135 us -> none  [per_device(): dunit = lax.psum(row_sums, 'feat')]
    reduce_scatter x1 -> x0, waiting for transfers between devices: 95.7 us -> none  [per_device(): lax.psum_scatter(dunit_terms, 'img', scatter_dimension=0, tiled=True)]
    all_to_all x0 -> x9, waiting for transfers between devices: none -> 81.6 us  [exchange(): return lax.all_to_all(blocks, axis, 0, 0)]
    all_to_all x0 -> x4, blocking collectives: none -> 73 us  [exchange(): return lax.all_to_all(blocks, axis, 0, 0)]
    all_gather x2 -> x0, waiting for transfers between devices: 67.7 us -> none  [the longest x1 37.4 us: per_device(): lax.all_gather(unit_low, 'img', axis=0, tiled=True)]
    all_to_all x0 -> x9, starting transfers between devices: none -> 54.8 us  [exchange(): return lax.all_to_all(blocks, axis, 0, 0)]
    all_gather x1 -> x0, blocking collectives: 40.2 us -> none  [per_device(): lax.all_gather(proj_out, 'feat', axis=0, tiled=True)]
  transfers between devices with their start and end apart: 4 -> 12, of which waited for: 4 -> 11; matrix products, arithmetic and copies ran while one was open for 1% -> 13% of each run, Pallas kernels for 0% -> 0%
where the time goes in v1:
time: 271 us; the launch traced here: 269 us
  waiting for transfers between devices  83.2 us (31%)
  blocking collectives  73 us (27%)
  starting transfers between devices  60.6 us (22%)
  matrix products  25.4 us (9%)
  local copies, waits for them, and re-layouts  16 us (6%)
  other arithmetic  9.83 us (4%)
    all_to_all x9, waiting for transfers between devices, exchange(): return lax.all_to_all(blocks, axis, 0, 0)  81.6 us
    all_to_all x4, blocking collectives, exchange(): return lax.all_to_all(blocks, axis, 0, 0)  73 us
    all_to_all x9, starting transfers between devices, exchange(): return lax.all_to_all(blocks, axis, 0, 0)  54.8 us
    dot_general x1, matrix products, per_device(): lax.dot_general(units, low, (((1,), (1,)), ((), ())), preferred_element_t...  7.31 us
    broadcast_in_dim x7, local copies, waits for them, and re-layouts, spread(): return exchange(jnp.broadcast_to(block[None], (count,) + block.shape), axis)  5.96 us
    dot_general x1, matrix products, per_device(): lax.dot_general(dcos, units, (((0,), (0,)), ((), ())), preferred_element_...  5.79 us
    ppermute x3, starting transfers between devices, partner(): return lax.ppermute(block, 'c', SWAP)  5.75 us
    dot_general x1, matrix products, per_device(): jnp.dot(rest.astype(bf16), low, preferred_element_type=f32).astype(bf16)  5.47 us
  transfers between devices with their start and end apart: 12, of which 11 were waited for; matrix products, arithmetic and copies ran while one was open for 13% of the time, Pallas kernels for 0%

profile of v1, /device:TPU:6, one launch (start us, length us, event | category | flops | bytes accessed | tf_op | source)
XLA Modules:
  0.0 269.1 jit_solution(8652484359553641693)
XLA Ops:
  1.6 16.2 %all_to_all.66 = bf16[4,24,3840]{2,1,0:T(8,128)(2,1)S(1)} all-to-all(bf16[4,24,3840]{2,1,0:T(8,128)(2,1)S(1)} %broadcast_in_dim.32), channel_id=1, replica_groups=mesh['z'=16,'x'=4,'y'=4,'c'=2] {'y'}, dimensions={0} | all-to-all | bytes 1474560 | tf_op jit(solution)/shard_map/all_to_all | solution.py:20
  18.9 23.7 %all_to_all.67 = bf16[4,56,3840]{2,1,0:T(8,128)(2,1)S(1)} all-to-all(bf16[4,56,3840]{2,1,0:T(8,128)(2,1)S(1)} %broadcast_in_dim.31), channel_id=1, replica_groups=mesh['z'=16,'x'=4,'y'=4,'c'=2] {'x'}, dimensions={0} | all-to-all | bytes 3440640 | tf_op jit(solution)/shard_map/all_to_all | solution.py:20
  43.5 15.2 %all-to-all-start.3 = ((bf16[16,48,512]{2,1,0:T(8,128)(2,1)}), bf16[16,48,512]{2,1,0:T(8,128)(2,1)}, u32[]{:S(2)}, u32[]{:S(2)}) async-start(bf16[16,48,512]{2,1,0:T(8,128)(2,1)} %broadcast_in_dim.33), calls=%async_computation.3 | async-start | bytes 1572864 | tf_op jit(solution)/shard_map/all_to_all | solution.py:20
  64.8 29.5 %all-to-all-done.3 = bf16[16,48,512]{2,1,0:T(8,128)(2,1)} async-done(((bf16[16,48,512]{2,1,0:T(8,128)(2,1)}), bf16[16,48,512]{2,1,0:T(8,128)(2,1)}, u32[]{:S(2)}, u32[]{:S(2)}) %all-to-all-start.3) | async-done | bytes 786464 | tf_op jit(solution)/shard_map/all_to_all | solution.py:20
  97.0 10.4 %all_to_all.68 = f32[4,56,512]{2,1,0:T(8,128)S(1)} all-to-all(f32[4,56,512]{2,1,0:T(8,128)S(1)} %bitcast.56), channel_id=1, replica_groups=mesh['z'=16,'x'=4,'y'=4,'c'=2] {'x'}, dimensions={0} | all-to-all | bytes 917504 | tf_op jit(solution)/shard_map/all_to_all | solution.py:20
  107.6 22.8 %all_to_all.69 = f32[16,14,128]{2,1,0:T(8,128)S(1)} all-to-all(f32[16,14,128]{2,1,0:T(8,128)S(1)} %reshape.194), channel_id=1, replica_groups=mesh['z'=16,'x'=4,'y'=4,'c'=2] {'z'}, dimensions={0} | all-to-all | bytes 229376 | tf_op jit(solution)/shard_map/all_to_all | solution.py:20
  131.1 3.5 %all-to-all-start.6 = ((f32[16,14,128]{2,1,0:T(8,128)}), f32[16,14,128]{2,1,0:T(8,128)S(1)}, u32[]{:S(2)}, u32[]{:S(2)}) async-start(f32[16,14,128]{2,1,0:T(8,128)} %broadcast_in_dim.34), calls=%async_computation.6 | async-start | bytes 262144 | tf_op jit(solution)/shard_map/all_to_all | solution.py:20
  135.0 12.8 %all-to-all-done.6 = f32[16,14,128]{2,1,0:T(8,128)S(1)} async-done(((f32[16,14,128]{2,1,0:T(8,128)}), f32[16,14,128]{2,1,0:T(8,128)S(1)}, u32[]{:S(2)}, u32[]{:S(2)}) %all-to-all-start.6) | async-done | bytes 114720 | tf_op jit(solution)/shard_map/all_to_all | solution.py:20
  148.4 5.4 %all-to-all-start = ((s32[16,1,56]{2,1,0:T(1,128)}), s32[16,1,56]{2,1,0:T(1,128)S(1)}, u32[]{:S(2)}, u32[]{:S(2)}) async-start(s32[16,1,56]{2,1,0:T(1,128)} %broadcast_in_dim.29), calls=%async_computation | async-start | bytes 16384 | tf_op jit(solution)/shard_map/all_to_all | solution.py:20
  154.7 4.6 %all-to-all-done = s32[16,1,56]{2,1,0:T(1,128)S(1)} async-done(((s32[16,1,56]{2,1,0:T(1,128)}), s32[16,1,56]{2,1,0:T(1,128)S(1)}, u32[]{:S(2)}, u32[]{:S(2)}) %all-to-all-start) | async-done | bytes 3616 | tf_op jit(solution)/shard_map/all_to_all | solution.py:20
  160.3 5.6 %all-to-all-start.7 = ((bf16[16,56,512]{2,1,0:T(8,128)(2,1)}), bf16[16,56,512]{2,1,0:T(8,128)(2,1)S(1)}, u32[]{:S(2)}, u32[]{:S(2)}) async-start(bf16[16,56,512]{2,1,0:T(8,128)(2,1)} %broadcast_in_dim.35), calls=%async_computation.7 | async-start | bytes 1835008 | tf_op jit(solution)/shard_map/all_to_all | solution.py:20
  171.8 4.2 %all-to-all-done.7 = bf16[16,56,512]{2,1,0:T(8,128)(2,1)S(1)} async-done(((bf16[16,56,512]{2,1,0:T(8,128)(2,1)}), bf16[16,56,512]{2,1,0:T(8,128)(2,1)S(1)}, u32[]{:S(2)}, u32[]{:S(2)}) %all-to-all-start.7) | async-done | bytes 917536 | tf_op jit(solution)/shard_map/all_to_all | solution.py:20
  176.0 5.6 %all-to-all-start.11 = ((bf16[16,56,512]{2,1,0:T(8,128)(2,1)}), bf16[16,56,512]{2,1,0:T(8,128)(2,1)S(1)}, u32[]{:S(2)}, u32[]{:S(2)}) async-start(bf16[16,56,512]{2,1,0:T(8,128)(2,1)} %bitcast.15), calls=%async_computation.11 | async-start | bytes 1835008 | tf_op jit(solution)/shard_map/all_to_all | solution.py:20
  181.7 7.3 %fusion.5 = (f32[896]{0:T(1024)S(1)}, f32[896]{0:T(1024)S(1)}, f32[896]{0:T(1024)S(1)}, f32[896]{0:T(1024)S(1)}, f32[896]{0:T(1024)S(1)}, /*index=5*/f32[896,1024]{1,0:T(8,128)}) fusion(s32[1024]{0:T(1024)S(1)} %pad_add_fusion, s32[896]{0:T(1024)S(1)} %eq.15, bf16[896,512]{1,0:T(8,128)(2,1)S(1)} %bitcast.57, ...), kind=kOutput, calls=%fused_computation.11 | convolution fusion | flops 965471872 | bytes 5661696 | tf_op jit(solution)/shard_map/dot_general | solution.py:80
  190.2 2.9 %all-to-all-done.11 = bf16[16,56,512]{2,1,0:T(8,128)(2,1)S(1)} async-done(((bf16[16,56,512]{2,1,0:T(8,128)(2,1)}), bf16[16,56,512]{2,1,0:T(8,128)(2,1)S(1)}, u32[]{:S(2)}, u32[]{:S(2)}) %all-to-all-start.11) | async-done | bytes 917536 | tf_op jit(solution)/shard_map/all_to_all | solution.py:20
  193.1 5.6 %all-to-all-start.8 = ((f32[16,16,128]{2,1,0:T(8,128)}), f32[16,16,128]{2,1,0:T(8,128)S(1)}, u32[]{:S(2)}, u32[]{:S(2)}) async-start(f32[16,16,128]{2,1,0:T(8,128)} %select_maximum_fusion), calls=%async_computation.8 | async-start | bytes 262144 | tf_op jit(solution)/shard_map/all_to_all | solution.py:20
  199.9 4.6 %all-to-all-done.8 = f32[16,16,128]{2,1,0:T(8,128)S(1)} async-done(((f32[16,16,128]{2,1,0:T(8,128)}), f32[16,16,128]{2,1,0:T(8,128)S(1)}, u32[]{:S(2)}, u32[]{:S(2)}) %all-to-all-start.8) | async-done | bytes 131104 | tf_op jit(solution)/shard_map/all_to_all | solution.py:20
  205.2 3.9 %all-to-all-start.9 = ((f32[16,16,128]{2,1,0:T(8,128)}), f32[16,16,128]{2,1,0:T(8,128)S(1)}, u32[]{:S(2)}, u32[]{:S(2)}) async-start(f32[16,16,128]{2,1,0:T(8,128)} %broadcast_in_dim.38), calls=%async_computation.9 | async-start | bytes 262144 | tf_op jit(solution)/shard_map/all_to_all | solution.py:20
  209.1 5.5 %fusion.18 = bf16[896,512]{1,0:T(8,128)(2,1)} fusion(s32[1024]{0:T(1024)S(1)} %pad_add_fusion, s32[896]{0:T(1024)S(1)} %eq.15, bf16[512,512]{0,1:T(8,128)(2,1)S(1)} %collective-permute-done.1, bf16[512,512]{0,1:T(8,128)(2,1)S(1)} %fusion.26, f32[896,1024]{1,0:T(8,128)} %get-tuple-element.25), kind=kOutput, calls=%fused_computation.26 | convolution fusion | flops 953090048 | bytes 5643776 | tf_op jit(solution)/shard_map/dot_general | solution.py:103
  214.6 7.6 %all-to-all-done.9 = f32[16,16,128]{2,1,0:T(8,128)S(1)} async-done(((f32[16,16,128]{2,1,0:T(8,128)}), f32[16,16,128]{2,1,0:T(8,128)S(1)}, u32[]{:S(2)}, u32[]{:S(2)}) %all-to-all-start.9) | async-done | bytes 131104 | tf_op jit(solution)/shard_map/all_to_all | solution.py:20
  222.2 5.6 %all-to-all-start.10 = ((bf16[16,56,512]{2,1,0:T(8,128)(2,1)}), bf16[16,56,512]{2,1,0:T(8,128)(2,1)S(1)}, u32[]{:S(2)}, u32[]{:S(2)}) async-start(bf16[16,56,512]{2,1,0:T(8,128)(2,1)} %bitcast.13), calls=%async_computation.10 | async-start | bytes 1835008 | tf_op jit(solution)/shard_map/all_to_all | solution.py:20
  228.5 5.8 %fusion.16 = f32[1024,512]{0,1:T(8,128)S(1)} fusion(bf16[896,512]{1,0:T(8,128)(2,1)} %bitcast.58, f32[896]{0:T(1024)S(1)} %slice_bitcast_fusion, bf16[896]{0:T(1024)(128)(2,1)S(1)} %add_multiply_fusion, s32[1024]{0:T(1024)} %copy-done.5, s32[896]{0:T(1024)} %copy-done.4, f32[896,1024]{1,0:T(8,128)} %get-tuple-element.25), kind=kOutput, calls=%fused_computation.25 | convolution fusion | flops 952369152 | bytes 6697728 | tf_op jit(solution)/shard_map/dot_general | solution.py:121
  241.6 4.4 %all-to-all-start.12 = ((bf16[16,28,128]{2,1,0:T(8,128)(2,1)}), bf16[16,28,128]{2,1,0:T(8,128)(2,1)S(1)}, u32[]{:S(2)}, u32[]{:S(2)}) async-start(bf16[16,28,128]{2,1,0:T(8,128)(2,1)} %copy.40), calls=%async_computation.12 | async-start | bytes 262144 | tf_op jit(solution)/shard_map/all_to_all | solution.py:20
  246.1 14.7 %all-to-all-done.12 = bf16[16,28,128]{2,1,0:T(8,128)(2,1)S(1)} async-done(((bf16[16,28,128]{2,1,0:T(8,128)(2,1)}), bf16[16,28,128]{2,1,0:T(8,128)(2,1)S(1)}, u32[]{:S(2)}, u32[]{:S(2)}) %all-to-all-start.12) | async-done | bytes 114720 | tf_op jit(solution)/shard_map/all_to_all | solution.py:20
  (96 shorter events, 40.7 us)
Async XLA Ops:
  1.6 41.0 %copy-start.2 = (bf16[48,512]{1,0:T(8,128)(2,1)S(1)}, bf16[48,512]{1,0:T(8,128)(2,1)}, u32[]{:S(2)}) copy-start(bf16[48,512]{1,0:T(8,128)(2,1)} %param.7) | copy-start | bytes 147460
  43.5 50.8 %all-to-all-start.3 = ((bf16[16,48,512]{2,1,0:T(8,128)(2,1)}), bf16[16,48,512]{2,1,0:T(8,128)(2,1)}, u32[]{:S(2)}, u32[]{:S(2)}) async-start(bf16[16,48,512]{2,1,0:T(8,128)(2,1)} %broadcast_in_dim.33), calls=%async_computation.3 | async-start | bytes 1572864 | tf_op jit(solution)/shard_map/all_to_all | solution.py:20
  58.8 4.2 %collective-permute-start = (bf16[96,3840]{1,0:T(8,128)(2,1)S(1)}, bf16[96,3840]{1,0:T(8,128)(2,1)}, u32[]{:S(2)}, u32[]{:S(2)}) collective-permute-start(bf16[96,3840]{1,0:T(8,128)(2,1)S(1)} %bitcast.54), channel_id=1, source_target_pairs={{0,1},{1,0},{2,3},{3,2},{4,5},{5,4},{6,7},{7,6},{8,9},{9,8},{10,11... | collective-permute-start | bytes 2211848 | tf_op jit(solution)/shard_map/ppermute | solution.py:28
  62.0 72.6 %copy-start.1 = (bf16[512,512]{1,0:T(8,128)(2,1)S(1)}, bf16[512,512]{1,0:T(8,128)(2,1)}, u32[]{:S(2)}) copy-start(bf16[512,512]{1,0:T(8,128)(2,1)} %param.8) | copy-start | bytes 1572868
  64.8 83.0 %copy-start.8 = (s32[56]{0:T(128)S(1)}, s32[56]{0:T(128)}, u32[]{:S(2)}) copy-start(s32[56]{0:T(128)} %param.9) | copy-start | bytes 676
  131.1 16.7 %all-to-all-start.6 = ((f32[16,14,128]{2,1,0:T(8,128)}), f32[16,14,128]{2,1,0:T(8,128)S(1)}, u32[]{:S(2)}, u32[]{:S(2)}) async-start(f32[16,14,128]{2,1,0:T(8,128)} %broadcast_in_dim.34), calls=%async_computation.6 | async-start | bytes 262144 | tf_op jit(solution)/shard_map/all_to_all | solution.py:20
  148.4 10.9 %all-to-all-start = ((s32[16,1,56]{2,1,0:T(1,128)}), s32[16,1,56]{2,1,0:T(1,128)S(1)}, u32[]{:S(2)}, u32[]{:S(2)}) async-start(s32[16,1,56]{2,1,0:T(1,128)} %broadcast_in_dim.29), calls=%async_computation | async-start | bytes 16384 | tf_op jit(solution)/shard_map/all_to_all | solution.py:20
  153.9 6.3 %copy-start.6 = (f32[56]{0:T(128)}, f32[56]{0:T(128)S(1)}, u32[]{:S(2)}) copy-start(f32[56]{0:T(128)S(1)} %add_rsqrt_fusion.1) | copy-start | bytes 676
  160.3 15.8 %all-to-all-start.7 = ((bf16[16,56,512]{2,1,0:T(8,128)(2,1)}), bf16[16,56,512]{2,1,0:T(8,128)(2,1)S(1)}, u32[]{:S(2)}, u32[]{:S(2)}) async-start(bf16[16,56,512]{2,1,0:T(8,128)(2,1)} %broadcast_in_dim.35), calls=%async_computation.7 | async-start | bytes 1835008 | tf_op jit(solution)/shard_map/all_to_all | solution.py:20
  165.9 3.8 %collective-permute-start.1 = (bf16[512,512]{0,1:T(8,128)(2,1)S(1)}, bf16[512,512]{0,1:T(8,128)(2,1)S(1)}, u32[]{:S(2)}, u32[]{:S(2)}) collective-permute-start(bf16[512,512]{0,1:T(8,128)(2,1)S(1)} %fusion.26), channel_id=1, source_target_pairs={{0,1},{1,0},{2,3},{3,2},{4,5},{5,4},{6,7},{7,6},{8,9},{9,8},{10,11... | collective-permute-start | bytes 1572872 | tf_op jit(solution)/shard_map/ppermute | solution.py:28
  167.9 41.2 %copy-start.5 = (s32[1024]{0:T(1024)}, s32[1024]{0:T(1024)S(1)}, u32[]{:S(2)}) copy-start(s32[1024]{0:T(1024)S(1)} %pad_add_fusion) | copy-start | bytes 12292
  169.2 39.9 %copy-start.4 = (s32[896]{0:T(1024)}, s32[896]{0:T(1024)S(1)}, u32[]{:S(2)}) copy-start(s32[896]{0:T(1024)S(1)} %eq.15) | copy-start | bytes 10756
  176.0 13.0 %copy-start = (bf16[16,56,512]{2,1,0:T(8,128)(2,1)}, bf16[16,56,512]{2,1,0:T(8,128)(2,1)S(1)}, u32[]{:S(2)}) copy-start(bf16[16,56,512]{2,1,0:T(8,128)(2,1)S(1)} %all-to-all-done.7) | copy-start | bytes 2752516
  176.0 17.1 %all-to-all-start.11 = ((bf16[16,56,512]{2,1,0:T(8,128)(2,1)}), bf16[16,56,512]{2,1,0:T(8,128)(2,1)S(1)}, u32[]{:S(2)}, u32[]{:S(2)}) async-start(bf16[16,56,512]{2,1,0:T(8,128)(2,1)} %bitcast.15), calls=%async_computation.11 | async-start | bytes 1835008 | tf_op jit(solution)/shard_map/all_to_all | solution.py:20
  189.0 25.6 %copy-start.3 = (f32[896]{0:T(1024)}, f32[896]{0:T(1024)S(1)}, u32[]{:S(2)}) copy-start(f32[896]{0:T(1024)S(1)} %get-tuple-element.15) | copy-start | bytes 10756
  193.1 11.4 %all-to-all-start.8 = ((f32[16,16,128]{2,1,0:T(8,128)}), f32[16,16,128]{2,1,0:T(8,128)S(1)}, u32[]{:S(2)}, u32[]{:S(2)}) async-start(f32[16,16,128]{2,1,0:T(8,128)} %select_maximum_fusion), calls=%async_computation.8 | async-start | bytes 262144 | tf_op jit(solution)/shard_map/all_to_all | solution.py:20
  205.2 17.0 %all-to-all-start.9 = ((f32[16,16,128]{2,1,0:T(8,128)}), f32[16,16,128]{2,1,0:T(8,128)S(1)}, u32[]{:S(2)}, u32[]{:S(2)}) async-start(f32[16,16,128]{2,1,0:T(8,128)} %broadcast_in_dim.38), calls=%async_computation.9 | async-start | bytes 262144 | tf_op jit(solution)/shard_map/all_to_all | solution.py:20
  222.2 15.8 %all-to-all-start.10 = ((bf16[16,56,512]{2,1,0:T(8,128)(2,1)}), bf16[16,56,512]{2,1,0:T(8,128)(2,1)S(1)}, u32[]{:S(2)}, u32[]{:S(2)}) async-start(bf16[16,56,512]{2,1,0:T(8,128)(2,1)} %bitcast.13), calls=%async_computation.10 | async-start | bytes 1835008 | tf_op jit(solution)/shard_map/all_to_all | solution.py:20
  234.3 26.7 %copy-start.7 = (f32[56]{0:T(128)S(1)}, f32[56]{0:T(128)}, u32[]{:S(2)}) copy-start(f32[56]{0:T(128)} %copy-done.6) | copy-start | bytes 676
  235.4 27.2 %collective-permute-start.2 = (f32[512,512]{0,1:T(8,128)}, f32[512,512]{0,1:T(8,128)}, u32[]{:S(2)}, u32[]{:S(2)}) collective-permute-start(f32[512,512]{0,1:T(8,128)} %slice.42), channel_id=1, source_target_pairs={{0,1},{1,0},{2,3},{3,2},{4,5},{5,4},{6,7},{7,6},{8,9},{9,8},{10,11... | collective-permute-start | bytes 3145736 | tf_op jit(solution)/shard_map/ppermute | solution.py:28
  241.6 19.2 %all-to-all-start.12 = ((bf16[16,28,128]{2,1,0:T(8,128)(2,1)}), bf16[16,28,128]{2,1,0:T(8,128)(2,1)S(1)}, u32[]{:S(2)}, u32[]{:S(2)}) async-start(bf16[16,28,128]{2,1,0:T(8,128)(2,1)} %copy.40), calls=%async_computation.12 | async-start | bytes 262144 | tf_op jit(solution)/shard_map/all_to_all | solution.py:20

commit v2 on v1

v2 whole, which is shorter than its diff:
```python
import jax
import jax.numpy as jnp
import numpy as np
from jax import lax
from jax.experimental import pallas as pl
from jax.experimental.pallas import tpu as pltpu
from jax.sharding import Mesh, PartitionSpec as P


norm_eps = 1e-06
scale_logit = 64.0
margin_angle = 0.5
sine_floor = 0.04

NZ, NX, NY, NC = 16, 4, 4, 2
XY = ("x", "y")
SWAP = [(0, 1), (1, 0)]
f32 = jnp.float32
bf16 = jnp.bfloat16


def exchange(blocks, axis):
    return lax.all_to_all(blocks, axis, 0, 0)


def spread(block, axis, count):
    return exchange(jnp.broadcast_to(block[None], (count,) + block.shape), axis)


def partner(block):
    return lax.ppermute(block, "c", SWAP)


def shift(block, axis, by):
    return lax.ppermute(block, axis, [(i, (i + by) % 4) for i in range(4)])


def hidden_kernel(seat, mine, left, right, far_a, far_b, own_cols, other_cols, out):
    x, y, c = seat[0], seat[1], seat[2]
    rows = mine.shape[0]
    cols = own_cols.shape[0] // NY
    far = jnp.concatenate([far_a[...], far_b[...]], axis=0)
    zero = jnp.zeros((NY * cols, 64 - rows), f32)

    def times(weights, block):
        return lax.dot_general(weights, block, (((1,), (1,)), ((), ())), preferred_element_type=f32)

    for off, block in ((0, mine[...]), (3, left[...]), (1, right[...]), (2, far)):
        own, other = times(own_cols[...], block), times(other_cols[...], block)
        first, second = jnp.where(c == 0, own, other), jnp.where(c == 0, other, own)
        both = jnp.concatenate([first, zero, second, zero], axis=1)
        for k, y_off in enumerate((0, 3, 1, 2)):
            out[lax.rem(x + off, NX), lax.rem(y + y_off, NY)] = both[k * cols : (k + 1) * cols]


def partial_hidden(seat, blocks, own_cols, other_cols, cols):
    vmem = pl.BlockSpec(memory_space=pltpu.VMEM)
    return pl.pallas_call(
        hidden_kernel,
        out_shape=jax.ShapeDtypeStruct((NX, NY, cols, 128), f32),
        in_specs=[pl.BlockSpec(memory_space=pltpu.SMEM)] + [vmem] * 7,
        out_specs=vmem,
        cost_estimate=pl.CostEstimate(flops=330_000_000, bytes_accessed=3_400_000, transcendentals=0),
    )(seat, *blocks, own_cols, other_cols)


def centre_kernel(centres, own, received, out):
    wide = centres[...].astype(f32)
    cinv = lax.rsqrt(jnp.sum(wide * wide, axis=1, keepdims=True) + norm_eps)
    unit_centre = wide * cinv
    gunit = own[...] + received[...]
    out[...] = cinv * (gunit - unit_centre * jnp.sum(unit_centre * gunit, axis=1, keepdims=True))


def centre_gradient(centres, own, received):
    rows, emb = centres.shape
    block = pl.BlockSpec((rows // 4, emb), lambda i: (i, 0))
    return pl.pallas_call(
        centre_kernel,
        out_shape=jax.ShapeDtypeStruct((rows, emb), f32),
        grid=(4,),
        in_specs=[block] * 3,
        out_specs=block,
        cost_estimate=pl.CostEstimate(flops=3_000_000, bytes_accessed=3_700_000, transcendentals=512),
    )(centres, own, received)


def split_pair(value):
    high = lax.reduce_precision(value, 8, 7)
    return high.astype(bf16), (value - high).astype(bf16)


def step_of(features, proj_in, proj_out, centres, labels):
    rows, _ = features.shape
    cols = proj_in.shape[1]
    emb = proj_out.shape[1]
    cen = centres.shape[0]
    images = NX * NY * rows
    lanes = emb // 4
    zi, xi, yi, ci = (lax.axis_index(a) for a in ("z", "x", "y", "c"))

    out_part = lax.dynamic_slice_in_dim(proj_out, yi * lanes, lanes, 1)
    out_part = spread(out_part, "z", NZ).reshape(NZ * proj_out.shape[0], lanes)
    from_left = shift(features, "x", 1)
    from_right = shift(features, "x", 3)
    cols_in = proj_in.T
    own_cols = [cols_in]
    for by in (1, 3, 2):
        own_cols.append(shift(cols_in, "y", by))
    own_cols = jnp.concatenate(own_cols, axis=0)
    far_a = shift(from_left[:32], "x", 1)
    far_b = shift(from_right[32:], "x", 3)
    other_cols = partner(own_cols)
    seat = jnp.stack([xi, yi, ci]).astype(jnp.int32)
    part = partial_hidden(seat, (features, from_left, from_right, far_a, far_b), own_cols, other_cols, cols)

    all_labels = spread(labels, XY, NX * NY).reshape(images, 1)
    wide = centres.astype(f32)
    cinv = lax.rsqrt(jnp.sum(wide * wide, axis=1) + norm_eps)
    unit_centre = wide * cinv[:, None]
    own_low = unit_centre.astype(bf16)
    low = jnp.concatenate([own_low, partner(own_low)], axis=0)
    chip = ((zi * NX + xi) * NY + yi) * NC
    step = jnp.arange(cen, dtype=jnp.int32)
    position = jnp.concatenate([(chip + ci) * cen + step, (chip + 1 - ci) * cen + step])
    target = all_labels == position[None, :]

    part = exchange(part, "x").reshape(NZ, cols, 128)
    hidden = jnp.sum(exchange(part, "z"), axis=0).astype(bf16)
    hidden = spread(hidden, "z", NZ).reshape(NZ * cols, 128)
    whole = jnp.stack([out_part, shift(out_part, "y", 1), shift(out_part, "y", 3), shift(out_part, "y", 2)])
    order = jnp.stack([lax.rem(yi * 0 + k + 4 - yi, 4) for k in range(4)])
    order = jnp.where(order == 3, 1, jnp.where(order == 1, 2, jnp.where(order == 2, 3, 0)))
    whole = jnp.take(whole, order, axis=0).transpose(1, 0, 2).reshape(NZ, NC, cols, emb)

    def over_rows(left, right):
        return lax.dot_general(left, right, (((0,), (0,)), ((), ())), preferred_element_type=f32)

    embed = over_rows(hidden[:, :rows], whole[:, 0].reshape(NZ * cols, emb))
    embed = embed + over_rows(hidden[:, 64 : 64 + rows], whole[:, 1].reshape(NZ * cols, emb))
    inverse = lax.rsqrt(jnp.sum(embed * embed, axis=1) + norm_eps)
    unit = embed * inverse[:, None]
    units = spread(unit.astype(bf16), XY, NX * NY).reshape(images, emb)

    chosen = jnp.dot(target.astype(bf16), low, preferred_element_type=f32).astype(bf16)
    chosen, units = lax.optimization_barrier((chosen, units))
    chosen = exchange(chosen.reshape(NX * NY, rows, emb), XY)
    chosen = jnp.sum(chosen.astype(f32), axis=0)

    cos_m = jnp.cos(f32(margin_angle))
    sin_m = jnp.sin(f32(margin_angle))
    cosine = lax.dot_general(units, low, (((1,), (1,)), ((), ())), preferred_element_type=f32)
    inner = 1.0 - cosine * cosine
    sine = jnp.sqrt(jnp.maximum(inner, sine_floor))
    logit = jnp.where(target, scale_logit * (cosine * cos_m - sine * sin_m), scale_logit * cosine)
    exps = jnp.exp(logit)
    slope = cos_m + jnp.where(inner > sine_floor, sin_m * cosine / sine, 0.0)
    rest = jnp.where(target, 0.0, exps)
    rest_sum = jnp.sum(rest, axis=1)
    rest_cos = jnp.sum(rest * cosine, axis=1)
    hit = jnp.sum(jnp.where(target, exps, 0.0), axis=1)
    hit_slope = jnp.sum(jnp.where(target, slope, 0.0), axis=1)
    hit_turn = jnp.sum(jnp.where(target, slope * cosine, 0.0), axis=1)

    pull = jnp.dot(rest.astype(bf16), low, preferred_element_type=f32).astype(bf16)
    pull = exchange(pull.reshape(NX * NY, rows, emb), XY)

    sums = jnp.stack([rest_sum, hit, rest_cos, hit_slope, hit_turn]).reshape(5, images // 128, 128)
    sums = lax.psum(lax.psum(sums, "x"), "y").reshape(5, images)
    owned = lax.dynamic_slice_in_dim(sums, (xi * NY + yi) * rows, rows, 1)
    owned = jnp.pad(owned, ((0, 0), (0, 128 - rows)))
    totals = (sums[0] + sums[1]).reshape(images // 128, 128)

    width = emb // NZ

    def by_column(block):
        block = block.astype(bf16).reshape(4, rows // 4, NZ, width)
        return block.transpose(2, 1, 0, 3).reshape(NZ, rows // 4, 4 * width)

    pull = jnp.sum(pull.astype(f32), axis=0)
    common = jnp.concatenate(split_pair(totals) + split_pair(owned), axis=0)
    common = jnp.broadcast_to(common[None], (NZ,) + common.shape)
    pack = jnp.concatenate([by_column(pull), by_column(chosen), common], axis=1)
    pack = exchange(pack, "z")
    pack = jnp.sum(pack.astype(f32), axis=0)

    def by_row(block):
        return block.reshape(rows // 4, 4, width).transpose(1, 0, 2).reshape(rows, width)

    quarter, tall = rows // 4, images // 128
    pull, chosen = by_row(pack[:quarter]), by_row(pack[quarter : 2 * quarter])
    common = pack[2 * quarter :]
    total = (common[:tall] + common[tall : 2 * tall]).reshape(images, 1)
    owned = common[2 * tall : 2 * tall + 5, :rows] + common[2 * tall + 5 :, :rows]
    own_rest, own_hit, own_cos, own_slope, own_turn = (owned[k] for k in range(5))

    cosine_t = lax.dot_general(low, units, (((1,), (1,)), ((), ())), preferred_element_type=f32)
    target_t = position[:, None] == all_labels.reshape(1, images)
    rest_t = jnp.where(target_t, 0.0, jnp.exp(scale_logit * cosine_t)).astype(bf16)
    rest_t, target_t = lax.optimization_barrier((rest_t, target_t.astype(bf16)))
    weight = scale_logit * hit_slope[:, None] * (hit[:, None] / total - 1.0)
    scaled = (units.astype(f32) * (scale_logit / total)).astype(bf16)
    aimed = (units.astype(f32) * weight).astype(bf16)

    def gradient_of(part):
        left = jnp.dot(rest_t[part], scaled, preferred_element_type=f32)
        return left + jnp.dot(target_t[part], aimed, preferred_element_type=f32)

    received = partner(gradient_of(slice(cen, None)))
    centre_grad = centre_gradient(centres, gradient_of(slice(0, cen)), received)

    own_scale = scale_logit / (own_rest + own_hit)
    dunit = own_scale[:, None] * (pull - (own_rest * own_slope)[:, None] * chosen)
    along = own_scale * (own_cos - own_rest * own_turn)
    unit_cols = lax.dynamic_slice_in_dim(unit, zi * width, width, 1)
    emb_grad = inverse[:, None] * (dunit - unit_cols * along[:, None])
    return (centre_grad, emb_grad)


def solution(mesh):
    fine = Mesh(np.asarray(mesh.devices).reshape(NZ, NX, NY, NC), ("z", "x", "y", "c"))
    img = ("x", "y", "c")
    every = ("z", "x", "y", "c")
    return jax.shard_map(
        step_of,
        mesh=fine,
        in_specs=(P(img, "z"), P("z", img), P("z", None), P(every, None), P(img)),
        out_specs=(P(every, None), P(img, "z")),
        check_vma=False,
    )
```

time: 271 us -> 269 us (level); the launches traced: 269 us -> 264 us
  starting transfers between devices: 60.6 us -> 108 us
  blocking collectives: 73 us -> 35.7 us
  waiting for transfers between devices: 83.2 us -> 72.8 us
  Pallas kernels: 0 us -> 8.34 us
  local copies, waits for them, and re-layouts: 16 us -> 10.2 us
  other arithmetic: 9.83 us -> 4.75 us
    all_to_all x4 -> x0, blocking collectives: 73 us -> none  [exchange(): return lax.all_to_all(blocks, axis, 0, 0)]
    psum x0 -> x2, blocking collectives: none -> 35.7 us  [step_of(): sums = lax.psum(lax.psum(sums, 'x'), 'y').reshape(5, images)]
    all_to_all x9, waiting for transfers between devices: 81.6 us -> 46 us  [exchange(): return lax.all_to_all(blocks, axis, 0, 0)]
    ppermute x0 -> x10, starting transfers between devices: none -> 32.4 us  [shift(): return lax.ppermute(block, axis, [(i, (i + by) % 4) for i in range(4)])]
    ppermute x0 -> x10, waiting for transfers between devices: none -> 26.4 us  [shift(): return lax.ppermute(block, axis, [(i, (i + by) % 4) for i in range(4)])]
    all_to_all x9, starting transfers between devices: 54.8 us -> 69.3 us  [exchange(): return lax.all_to_all(blocks, axis, 0, 0)]
    pallas_call x0 -> x2, Pallas kernels: none -> 8.34 us  [the longest x1 4.32 us: partial_hidden(): pl.pallas_call(hidden_kernel, out_shape=jax.ShapeDtypeStruct((NX, NY, col...]
    mul x5 -> x4, other arithmetic: 4.11 us -> 0.13 us  [the longest x1 0.11 us: step_of(): emb_grad = inverse[:, None] * (dunit - unit_cols * along[:, None])]
  transfers between devices with their start and end apart: 12 -> 22, of which waited for: 11 -> 13; matrix products, arithmetic and copies ran while one was open for 13% -> 7% of each run, Pallas kernels for 0% -> 2%
where the time goes in v2:
time: 269 us; the launch traced here: 264 us
  starting transfers between devices  108 us (40%)
  waiting for transfers between devices  72.8 us (27%)
  blocking collectives  35.7 us (13%)
  matrix products  23.4 us (9%)
  local copies, waits for them, and re-layouts  10.2 us (4%)
  Pallas kernels  8.34 us (3%)
  other arithmetic  4.75 us (2%)
    all_to_all x9, starting transfers between devices, exchange(): return lax.all_to_all(blocks, axis, 0, 0)  69.3 us
    all_to_all x9, waiting for transfers between devices, exchange(): return lax.all_to_all(blocks, axis, 0, 0)  46 us
    psum x2, blocking collectives, step_of(): sums = lax.psum(lax.psum(sums, 'x'), 'y').reshape(5, images)  35.7 us
    ppermute x10, starting transfers between devices, shift(): return lax.ppermute(block, axis, [(i, (i + by) % 4) for i in range(4)])  32.4 us
    ppermute x10, waiting for transfers between devices, shift(): return lax.ppermute(block, axis, [(i, (i + by) % 4) for i in range(4)])  26.4 us
    dot_general x1, matrix products, step_of(): lax.dot_general(units, low, (((1,), (1,)), ((), ())), preferred_element_t...  5.98 us
    ppermute x3, starting transfers between devices, partner(): return lax.ppermute(block, 'c', SWAP)  5.93 us
  transfers between devices with their start and end apart: 22, of which 13 were waited for; matrix products, arithmetic and copies ran while one was open for 7% of the time, Pallas kernels for 2%

profile of v2, /device:TPU:6, one launch (start us, length us, event | category | flops | bytes accessed | tf_op | source)
XLA Modules:
  0.0 264.1 jit_solution(12565515550417334424)
XLA Ops:
  7.9 3.9 %collective-permute-start.7 = (bf16[24,3840]{1,0:T(8,128)(2,1)}, bf16[24,3840]{1,0:T(8,128)(2,1)S(1)}, u32[]{:S(2)}, u32[]{:S(2)}) collective-permute-start(bf16[24,3840]{1,0:T(8,128)(2,1)} %bitcast.95), channel_id=1, source_target_pairs={{0,4},{2,6},{4,0},{6,2},{1,5},{3,7},{5,1},{7,3},{8,12},{10,14},{12... | collective-permute-start | bytes 552968 | tf_op jit(solution)/shard_map/ppermute | solution.py:35
  12.5 4.9 %collective-permute-done.7 = bf16[24,3840]{1,0:T(8,128)(2,1)S(1)} collective-permute-done((bf16[24,3840]{1,0:T(8,128)(2,1)}, bf16[24,3840]{1,0:T(8,128)(2,1)S(1)}, u32[]{:S(2)}, u32[]{:S(2)}) %collective-permute-start.7) | collective-permute-done | bytes 184352 | tf_op jit(solution)/shard_map/ppermute | solution.py:35
  21.0 15.2 %all-to-all-start.4 = ((bf16[16,48,128]{2,1,0:T(8,128)(2,1)}), bf16[16,48,128]{2,1,0:T(8,128)(2,1)S(1)}, u32[]{:S(2)}, u32[]{:S(2)}) async-start(bf16[16,48,128]{2,1,0:T(8,128)(2,1)} %broadcast_in_dim.89), calls=%async_computation.4 | async-start | bytes 393216 | tf_op jit(solution)/shard_map/all_to_all | solution.py:23
  42.1 8.3 %collective-permute-done.1.left = bf16[56,3840]{1,0:T(8,128)(2,1)S(1)} collective-permute-done((bf16[56,3840]{1,0:T(8,128)(2,1)}, bf16[56,3840]{1,0:T(8,128)(2,1)S(1)}, u32[]{:S(2)}, u32[]{:S(2)}) %collective-permute-start.1) | collective-permute-done | bytes 430112 | tf_op jit(solution)/shard_map/ppermute | solution.py:35
  58.3 6.1 %collective-permute-done.4.far_b = bf16[24,3840]{1,0:T(8,128)(2,1)S(1)} collective-permute-done((bf16[24,3840]{1,0:T(8,128)(2,1)}, bf16[24,3840]{1,0:T(8,128)(2,1)S(1)}, u32[]{:S(2)}, u32[]{:S(2)}) %collective-permute-start.4) | collective-permute-done | bytes 184352 | tf_op jit(solution)/shard_map/ppermute | solution.py:35
  66.0 4.3 %shard_map.68 = f32[4,4,24,128]{3,2,1,0:T(8,128)} custom-call(s32[3]{0:T(128)} %pad_add_fusion.1.seat, bf16[56,3840]{1,0:T(8,128)(2,1)} %mine.1, bf16[56,3840]{1,0:T(8,128)(2,1)} %copy-done.3, bf16[56,3840]{1,0:T(8,128)(2,1)} %copy-done.4, bf16[32,3840]{1,0:T(8,128)(2,1)} %copy-done.7, bf16[24,3840]{1,0:T(8,128)(2,1)} %copy-done.8, ...), custom_call_target="tpu_custom_call" | custom-call | flops 330000000 | bytes 3400000 | tf_op jit(solution)/shard_map/pallas_call | solution.py:58
  70.3 4.5 %all-to-all-start.1 = ((f32[4,4,24,128]{3,2,1,0:T(8,128)}), f32[4,4,24,128]{3,2,1,0:T(8,128)}, u32[]{:S(2)}, u32[]{:S(2)}) async-start(f32[4,4,24,128]{3,2,1,0:T(8,128)} %shard_map.68), calls=%async_computation.1 | async-start | bytes 393216 | tf_op jit(solution)/shard_map/all_to_all | solution.py:23
  74.8 4.4 %all-to-all-done.1 = f32[4,4,24,128]{3,2,1,0:T(8,128)} async-done(((f32[4,4,24,128]{3,2,1,0:T(8,128)}), f32[4,4,24,128]{3,2,1,0:T(8,128)}, u32[]{:S(2)}, u32[]{:S(2)}) %all-to-all-start.1) | async-done | bytes 196640 | tf_op jit(solution)/shard_map/all_to_all | solution.py:23
  79.2 11.7 %all-to-all-start.2 = ((f32[16,24,128]{2,1,0:T(8,128)}), f32[16,24,128]{2,1,0:T(8,128)S(1)}, u32[]{:S(2)}, u32[]{:S(2)}) async-start(f32[16,24,128]{2,1,0:T(8,128)} %bitcast.4), calls=%async_computation.2 | async-start | bytes 393216 | tf_op jit(solution)/shard_map/all_to_all | solution.py:23
  102.1 5.3 %collective-permute-done.11 = bf16[768,128]{1,0:T(8,128)(2,1)S(1)} collective-permute-done((bf16[768,128]{1,0:T(8,128)(2,1)S(1)}, bf16[768,128]{1,0:T(8,128)(2,1)S(1)}, u32[]{:S(2)}, u32[]{:S(2)}) %collective-permute-start.11) | collective-permute-done | bytes 196640 | tf_op jit(solution)/shard_map/ppermute | solution.py:35
  108.9 12.0 %all-to-all-start.3 = ((bf16[16,24,128]{2,1,0:T(8,128)(2,1)}), bf16[16,24,128]{2,1,0:T(8,128)(2,1)S(1)}, u32[]{:S(2)}, u32[]{:S(2)}) async-start(bf16[16,24,128]{2,1,0:T(8,128)(2,1)} %broadcast_in_dim.84), calls=%async_computation.3 | async-start | bytes 196608 | tf_op jit(solution)/shard_map/all_to_all | solution.py:23
  122.0 11.9 %all-to-all-done.3 = bf16[16,24,128]{2,1,0:T(8,128)(2,1)S(1)} async-done(((bf16[16,24,128]{2,1,0:T(8,128)(2,1)}), bf16[16,24,128]{2,1,0:T(8,128)(2,1)S(1)}, u32[]{:S(2)}, u32[]{:S(2)}) %all-to-all-start.3) | async-done | bytes 98336 | tf_op jit(solution)/shard_map/all_to_all | solution.py:23
  134.5 5.4 %all-to-all-start = ((s32[16,1,56]{2,1,0:T(1,128)}), s32[16,1,56]{2,1,0:T(1,128)S(1)}, u32[]{:S(2)}, u32[]{:S(2)}) async-start(s32[16,1,56]{2,1,0:T(1,128)} %broadcast_in_dim.82), calls=%async_computation | async-start | bytes 16384 | tf_op jit(solution)/shard_map/all_to_all | solution.py:23
  140.6 4.8 %all-to-all-done = s32[16,1,56]{2,1,0:T(1,128)S(1)} async-done(((s32[16,1,56]{2,1,0:T(1,128)}), s32[16,1,56]{2,1,0:T(1,128)S(1)}, u32[]{:S(2)}, u32[]{:S(2)}) %all-to-all-start) | async-done | bytes 3616 | tf_op jit(solution)/shard_map/all_to_all | solution.py:23
  146.4 5.6 %all-to-all-start.5 = ((bf16[16,56,512]{2,1,0:T(8,128)(2,1)}), bf16[16,56,512]{2,1,0:T(8,128)(2,1)S(1)}, u32[]{:S(2)}, u32[]{:S(2)}) async-start(bf16[16,56,512]{2,1,0:T(8,128)(2,1)} %broadcast_in_dim.94), calls=%async_computation.5 | async-start | bytes 1835008 | tf_op jit(solution)/shard_map/all_to_all | solution.py:23
  158.1 4.1 %all-to-all-done.5 = bf16[16,56,512]{2,1,0:T(8,128)(2,1)S(1)} async-done(((bf16[16,56,512]{2,1,0:T(8,128)(2,1)}), bf16[16,56,512]{2,1,0:T(8,128)(2,1)S(1)}, u32[]{:S(2)}, u32[]{:S(2)}) %all-to-all-start.5) | async-done | bytes 917536 | tf_op jit(solution)/shard_map/all_to_all | solution.py:23
  162.2 6.0 %fusion.6 = (f32[896]{0:T(1024)S(1)}, f32[896]{0:T(1024)S(1)}, f32[896]{0:T(1024)S(1)}, f32[896]{0:T(1024)S(1)}, f32[896]{0:T(1024)S(1)}, /*index=5*/f32[896,1024]{1,0:T(8,128)S(1)}) fusion(s32[1024]{0:T(1024)S(1)} %pad_add_fusion, s32[896]{0:T(1024)S(1)} %eq.71, bf16[896,512]{1,0:T(8,128)(2,1)S(1)} %bitcast.73, ...), kind=kOutput, calls=%fused_computation.14 | convolution fusion | flops 965471872 | bytes 5661696 | tf_op jit(solution)/shard_map/dot_general | solution.py:152
  171.6 5.6 %all-to-all-start.6 = ((bf16[16,56,512]{2,1,0:T(8,128)(2,1)}), bf16[16,56,512]{2,1,0:T(8,128)(2,1)S(1)}, u32[]{:S(2)}, u32[]{:S(2)}) async-start(bf16[16,56,512]{2,1,0:T(8,128)(2,1)} %bitcast.24), calls=%async_computation.6 | async-start | bytes 1835008 | tf_op jit(solution)/shard_map/all_to_all | solution.py:23
  177.3 11.5 %all-to-all-done.6 = bf16[16,56,512]{2,1,0:T(8,128)(2,1)S(1)} async-done(((bf16[16,56,512]{2,1,0:T(8,128)(2,1)}), bf16[16,56,512]{2,1,0:T(8,128)(2,1)S(1)}, u32[]{:S(2)}, u32[]{:S(2)}) %all-to-all-start.6) | async-done | bytes 917536 | tf_op jit(solution)/shard_map/all_to_all | solution.py:23
  188.8 5.6 %all-to-all-start.7 = ((bf16[16,56,512]{2,1,0:T(8,128)(2,1)}), bf16[16,56,512]{2,1,0:T(8,128)(2,1)S(1)}, u32[]{:S(2)}, u32[]{:S(2)}) async-start(bf16[16,56,512]{2,1,0:T(8,128)(2,1)} %bitcast.81), calls=%async_computation.7 | async-start | bytes 1835008 | tf_op jit(solution)/shard_map/all_to_all | solution.py:23
  194.4 18.8 %psum.14 = f32[5,7,128]{2,1,0:T(8,128)S(1)} all-reduce(f32[5,7,128]{2,1,0:T(8,128)S(1)} %constant_dynamic-update-slice_fusion), channel_id=1, replica_groups=mesh['z'=16,'x'=4,'y'=4,'c'=2] {'x'}, use_global_device_ids=true, to_apply=%region_10.11 | all-reduce | flops 4480 | bytes 35840 | tf_op jit(solution)/shard_map/psum | solution.py:169
  213.2 16.9 %psum.15 = f32[5,7,128]{2,1,0:T(8,128)S(1)} all-reduce(f32[5,7,128]{2,1,0:T(8,128)S(1)} %psum.14), channel_id=1, replica_groups=mesh['z'=16,'x'=4,'y'=4,'c'=2] {'y'}, use_global_device_ids=true, to_apply=%region_11.12 | all-reduce | flops 4480 | bytes 35840 | tf_op jit(solution)/shard_map/psum | solution.py:169
  240.1 9.4 %all-to-all-done.8 = bf16[16,52,128]{2,1,0:T(8,128)(2,1)S(1)} async-done(((bf16[16,52,128]{2,1,0:T(8,128)(2,1)}), bf16[16,52,128]{2,1,0:T(8,128)(2,1)S(1)}, u32[]{:S(2)}, u32[]{:S(2)}) %all-to-all-start.8) | async-done | bytes 213024 | tf_op jit(solution)/shard_map/all_to_all | solution.py:23
  260.1 4.0 %shard_map.69 = f32[512,512]{1,0:T(8,128)} custom-call(bf16[512,512]{1,0:T(8,128)(2,1)} %centres.1, f32[512,512]{1,0:T(8,128)} %convolution_add_fusion.1.own, f32[512,512]{1,0:T(8,128)} %collective-permute-done.12.received), custom_call_target="tpu_custom_call" | custom-call | flops 3000000 | bytes 3700000 | tf_op jit(solution)/shard_map/pallas_call | solution.py:78
  (120 shorter events, 72.8 us)
Async XLA Ops:
  0.6 90.4 %copy-start.1 = (bf16[512,512]{1,0:T(8,128)(2,1)S(1)}, bf16[512,512]{1,0:T(8,128)(2,1)}, u32[]{:S(2)}) copy-start(bf16[512,512]{1,0:T(8,128)(2,1)} %centres.1) | copy-start | bytes 1572868
  0.7 11.1 %collective-permute-start.5 = (bf16[24,3840]{1,0:T(8,128)(2,1)}, bf16[24,3840]{1,0:T(8,128)(2,1)S(1)}, u32[]{:S(2)}, u32[]{:S(2)}) collective-permute-start(bf16[24,3840]{1,0:T(8,128)(2,1)} %bitcast.93), channel_id=1, source_target_pairs={{0,2},{2,4},{4,6},{6,0},{1,3},{3,5},{5,7},{7,1},{8,10},{10,12},{12... | collective-permute-start | bytes 552968 | tf_op jit(solution)/shard_map/ppermute | solution.py:35
  4.3 8.2 %collective-permute-start.6 = (bf16[24,3840]{1,0:T(8,128)(2,1)}, bf16[24,3840]{1,0:T(8,128)(2,1)S(1)}, u32[]{:S(2)}, u32[]{:S(2)}) collective-permute-start(bf16[24,3840]{1,0:T(8,128)(2,1)} %bitcast.94), channel_id=1, source_target_pairs={{0,6},{2,0},{4,2},{6,4},{1,7},{3,1},{5,3},{7,5},{8,14},{10,8},{12,... | collective-permute-start | bytes 552968 | tf_op jit(solution)/shard_map/ppermute | solution.py:35
  7.9 9.5 %collective-permute-start.7 = (bf16[24,3840]{1,0:T(8,128)(2,1)}, bf16[24,3840]{1,0:T(8,128)(2,1)S(1)}, u32[]{:S(2)}, u32[]{:S(2)}) collective-permute-start(bf16[24,3840]{1,0:T(8,128)(2,1)} %bitcast.95), channel_id=1, source_target_pairs={{0,4},{2,6},{4,0},{6,2},{1,5},{3,7},{5,1},{7,3},{8,12},{10,14},{12... | collective-permute-start | bytes 552968 | tf_op jit(solution)/shard_map/ppermute | solution.py:35
  18.3 46.1 %copy-start.2 = (bf16[96,3840]{1,0:T(8,128)(2,1)}, bf16[96,3840]{1,0:T(8,128)(2,1)S(1)}, u32[]{:S(2)}) copy-start(bf16[96,3840]{1,0:T(8,128)(2,1)S(1)} %pad_maximum_fusion.2.own_cols) | copy-start | bytes 2211844
  18.3 46.1 %collective-permute-start.8 = (bf16[96,3840]{1,0:T(8,128)(2,1)S(1)}, bf16[96,3840]{1,0:T(8,128)(2,1)S(1)}, u32[]{:S(2)}, u32[]{:S(2)}) collective-permute-start(bf16[96,3840]{1,0:T(8,128)(2,1)S(1)} %pad_maximum_fusion.2.own_cols), channel_id=1, source_target_pairs={{0,1},{1,0},{2,3},{3,2},{4,5},{5,4},{6,7},{7,6},{8,9},{9,8},{10,11... | collective-permute-start | bytes 2211848 | tf_op jit(solution)/shard_map/ppermute | solution.py:31
  21.0 49.3 %all-to-all-start.4 = ((bf16[16,48,128]{2,1,0:T(8,128)(2,1)}), bf16[16,48,128]{2,1,0:T(8,128)(2,1)S(1)}, u32[]{:S(2)}, u32[]{:S(2)}) async-start(bf16[16,48,128]{2,1,0:T(8,128)(2,1)} %broadcast_in_dim.89), calls=%async_computation.4 | async-start | bytes 393216 | tf_op jit(solution)/shard_map/all_to_all | solution.py:23
  36.2 14.1 %collective-permute-start.1 = (bf16[56,3840]{1,0:T(8,128)(2,1)}, bf16[56,3840]{1,0:T(8,128)(2,1)S(1)}, u32[]{:S(2)}, u32[]{:S(2)}) collective-permute-start(bf16[56,3840]{1,0:T(8,128)(2,1)} %mine.1), channel_id=1, source_target_pairs={{0,8},{8,16},{16,24},{24,0},{1,9},{9,17},{17,25},{25,1},{2,10},{10... | collective-permute-start | bytes 1290248 | tf_op jit(solution)/shard_map/ppermute | solution.py:35
  38.6 16.1 %collective-permute-start.2 = (bf16[56,3840]{1,0:T(8,128)(2,1)}, bf16[56,3840]{1,0:T(8,128)(2,1)S(1)}, u32[]{:S(2)}, u32[]{:S(2)}) collective-permute-start(bf16[56,3840]{1,0:T(8,128)(2,1)} %mine.1), channel_id=1, source_target_pairs={{0,24},{8,0},{16,8},{24,16},{1,25},{9,1},{17,9},{25,17},{2,26},{10... | collective-permute-start | bytes 1290248 | tf_op jit(solution)/shard_map/ppermute | solution.py:35
  51.1 13.3 %collective-permute-start.3 = (bf16[32,3840]{1,0:T(8,128)(2,1)}, bf16[32,3840]{1,0:T(8,128)(2,1)S(1)}, u32[]{:S(2)}, u32[]{:S(2)}) collective-permute-start(bf16[32,3840]{1,0:T(8,128)(2,1)} %slice.101), channel_id=1, source_target_pairs={{0,8},{8,16},{16,24},{24,0},{1,9},{9,17},{17,25},{25,1},{2,10},{10... | collective-permute-start | bytes 737288 | tf_op jit(solution)/shard_map/ppermute | solution.py:35
  55.5 8.9 %collective-permute-start.4 = (bf16[24,3840]{1,0:T(8,128)(2,1)}, bf16[24,3840]{1,0:T(8,128)(2,1)S(1)}, u32[]{:S(2)}, u32[]{:S(2)}) collective-permute-start(bf16[24,3840]{1,0:T(8,128)(2,1)} %slice.102), channel_id=1, source_target_pairs={{0,24},{8,0},{16,8},{24,16},{1,25},{9,1},{17,9},{25,17},{2,26},{10... | collective-permute-start | bytes 552968 | tf_op jit(solution)/shard_map/ppermute | solution.py:35
  70.3 8.9 %all-to-all-start.1 = ((f32[4,4,24,128]{3,2,1,0:T(8,128)}), f32[4,4,24,128]{3,2,1,0:T(8,128)}, u32[]{:S(2)}, u32[]{:S(2)}) async-start(f32[4,4,24,128]{3,2,1,0:T(8,128)} %shard_map.68), calls=%async_computation.1 | async-start | bytes 393216 | tf_op jit(solution)/shard_map/all_to_all | solution.py:23
  79.2 29.0 %all-to-all-start.2 = ((f32[16,24,128]{2,1,0:T(8,128)}), f32[16,24,128]{2,1,0:T(8,128)S(1)}, u32[]{:S(2)}, u32[]{:S(2)}) async-start(f32[16,24,128]{2,1,0:T(8,128)} %bitcast.4), calls=%async_computation.2 | async-start | bytes 393216 | tf_op jit(solution)/shard_map/all_to_all | solution.py:23
  91.2 9.7 %collective-permute-start.9 = (bf16[768,128]{1,0:T(8,128)(2,1)S(1)}, bf16[768,128]{1,0:T(8,128)(2,1)S(1)}, u32[]{:S(2)}, u32[]{:S(2)}) collective-permute-start(bf16[768,128]{1,0:T(8,128)(2,1)S(1)} %bitcast.86), channel_id=1, source_target_pairs={{0,2},{2,4},{4,6},{6,0},{1,3},{3,5},{5,7},{7,1},{8,10},{10,12},{12... | collective-permute-start | bytes 589832 | tf_op jit(solution)/shard_map/ppermute | solution.py:35
  94.5 7.6 %collective-permute-start.10 = (bf16[768,128]{1,0:T(8,128)(2,1)S(1)}, bf16[768,128]{1,0:T(8,128)(2,1)S(1)}, u32[]{:S(2)}, u32[]{:S(2)}) collective-permute-start(bf16[768,128]{1,0:T(8,128)(2,1)S(1)} %bitcast.87), channel_id=1, source_target_pairs={{0,6},{2,0},{4,2},{6,4},{1,7},{3,1},{5,3},{7,5},{8,14},{10,8},{12,... | collective-permute-start | bytes 589832 | tf_op jit(solution)/shard_map/ppermute | solution.py:35
  98.3 9.1 %collective-permute-start.11 = (bf16[768,128]{1,0:T(8,128)(2,1)S(1)}, bf16[768,128]{1,0:T(8,128)(2,1)S(1)}, u32[]{:S(2)}, u32[]{:S(2)}) collective-permute-start(bf16[768,128]{1,0:T(8,128)(2,1)S(1)} %bitcast.88), channel_id=1, source_target_pairs={{0,4},{2,6},{4,0},{6,2},{1,5},{3,7},{5,1},{7,3},{8,12},{10,14},{12... | collective-permute-start | bytes 589832 | tf_op jit(solution)/shard_map/ppermute | solution.py:35
  108.9 25.1 %all-to-all-start.3 = ((bf16[16,24,128]{2,1,0:T(8,128)(2,1)}), bf16[16,24,128]{2,1,0:T(8,128)(2,1)S(1)}, u32[]{:S(2)}, u32[]{:S(2)}) async-start(bf16[16,24,128]{2,1,0:T(8,128)(2,1)} %broadcast_in_dim.84), calls=%async_computation.3 | async-start | bytes 196608 | tf_op jit(solution)/shard_map/all_to_all | solution.py:23
  134.5 10.9 %all-to-all-start = ((s32[16,1,56]{2,1,0:T(1,128)}), s32[16,1,56]{2,1,0:T(1,128)S(1)}, u32[]{:S(2)}, u32[]{:S(2)}) async-start(s32[16,1,56]{2,1,0:T(1,128)} %broadcast_in_dim.82), calls=%async_computation | async-start | bytes 16384 | tf_op jit(solution)/shard_map/all_to_all | solution.py:23
  146.4 15.8 %all-to-all-start.5 = ((bf16[16,56,512]{2,1,0:T(8,128)(2,1)}), bf16[16,56,512]{2,1,0:T(8,128)(2,1)S(1)}, u32[]{:S(2)}, u32[]{:S(2)}) async-start(bf16[16,56,512]{2,1,0:T(8,128)(2,1)} %broadcast_in_dim.94), calls=%async_computation.5 | async-start | bytes 1835008 | tf_op jit(solution)/shard_map/all_to_all | solution.py:23
  152.2 3.8 %collective-permute-start = (bf16[512,512]{1,0:T(8,128)(2,1)S(1)}, bf16[512,512]{1,0:T(8,128)(2,1)S(1)}, u32[]{:S(2)}, u32[]{:S(2)}) collective-permute-start(bf16[512,512]{1,0:T(8,128)(2,1)S(1)} %fusion.25), channel_id=1, source_target_pairs={{0,1},{1,0},{2,3},{3,2},{4,5},{5,4},{6,7},{7,6},{8,9},{9,8},{10,11... | collective-permute-start | bytes 1572872 | tf_op jit(solution)/shard_map/ppermute | solution.py:31
  171.6 17.2 %all-to-all-start.6 = ((bf16[16,56,512]{2,1,0:T(8,128)(2,1)}), bf16[16,56,512]{2,1,0:T(8,128)(2,1)S(1)}, u32[]{:S(2)}, u32[]{:S(2)}) async-start(bf16[16,56,512]{2,1,0:T(8,128)(2,1)} %bitcast.24), calls=%async_computation.6 | async-start | bytes 1835008 | tf_op jit(solution)/shard_map/all_to_all | solution.py:23
  188.8 42.0 %all-to-all-start.7 = ((bf16[16,56,512]{2,1,0:T(8,128)(2,1)}), bf16[16,56,512]{2,1,0:T(8,128)(2,1)S(1)}, u32[]{:S(2)}, u32[]{:S(2)}) async-start(bf16[16,56,512]{2,1,0:T(8,128)(2,1)} %bitcast.81), calls=%async_computation.7 | async-start | bytes 1835008 | tf_op jit(solution)/shard_map/all_to_all | solution.py:23
  232.2 17.3 %all-to-all-start.8 = ((bf16[16,52,128]{2,1,0:T(8,128)(2,1)}), bf16[16,52,128]{2,1,0:T(8,128)(2,1)S(1)}, u32[]{:S(2)}, u32[]{:S(2)}) async-start(bf16[16,52,128]{2,1,0:T(8,128)(2,1)} %pad_maximum_fusion.3), calls=%async_computation.8 | async-start | bytes 458752 | tf_op jit(solution)/shard_map/all_to_all | solution.py:23
  253.6 6.5 %collective-permute-start.12 = (f32[512,512]{1,0:T(8,128)}, f32[512,512]{1,0:T(8,128)}, u32[]{:S(2)}, u32[]{:S(2)}) collective-permute-start(f32[512,512]{1,0:T(8,128)} %convolution_add_fusion), channel_id=1, source_target_pairs={{0,1},{1,0},{2,3},{3,2},{4,5},{5,4},{6,7},{7,6},{8,9},{9,8},{10,11... | collective-permute-start | bytes 3145736 | tf_op jit(solution)/shard_map/ppermute | solution.py:31
  (9 other events, 99.6 us)

commit v3 on v2

--- a/solution.py
+++ b/solution.py
@@ -35,22 +35,25 @@
     return lax.ppermute(block, axis, [(i, (i + by) % 4) for i in range(4)])
 
 
-def hidden_kernel(seat, mine, left, right, far_a, far_b, own_cols, other_cols, out):
+def hidden_kernel(seat, mine, left, right, far, own_cols, other_cols, out, held):
     x, y, c = seat[0], seat[1], seat[2]
-    rows = mine.shape[0]
+    rows, feats = mine.shape
     cols = own_cols.shape[0] // NY
-    far = jnp.concatenate([far_a[...], far_b[...]], axis=0)
-    zero = jnp.zeros((NY * cols, 64 - rows), f32)
-
-    def times(weights, block):
-        return lax.dot_general(weights, block, (((1,), (1,)), ((), ())), preferred_element_type=f32)
-
-    for off, block in ((0, mine[...]), (3, left[...]), (1, right[...]), (2, far)):
-        own, other = times(own_cols[...], block), times(other_cols[...], block)
-        first, second = jnp.where(c == 0, own, other), jnp.where(c == 0, other, own)
-        both = jnp.concatenate([first, zero, second, zero], axis=1)
-        for k, y_off in enumerate((0, 3, 1, 2)):
-            out[lax.rem(x + off, NX), lax.rem(y + y_off, NY)] = both[k * cols : (k + 1) * cols]
+    for k, block in enumerate((mine, left, right, far)):
+        held[k, :rows] = block[...]
+        held[k, rows:] = jnp.zeros((64 - rows, feats), bf16)
+    blocks = held[...].reshape(NX * 64, feats)
+
+    def times(weights):
+        return lax.dot_general(weights, blocks, (((1,), (1,)), ((), ())), preferred_element_type=f32)
+
+    own, other = times(own_cols[...]), times(other_cols[...])
+    first, second = jnp.where(c == 0, own, other), jnp.where(c == 0, other, own)
+    beside = y + 1 - 2 * lax.rem(y, 2)
+    for k, off in enumerate((0, 3, 1, 2)):
+        both = jnp.concatenate([first[:, 64 * k : 64 * k + 64], second[:, 64 * k : 64 * k + 64]], axis=1)
+        for j, at in enumerate((y, beside, 3 - y, 3 - beside)):
+            out[lax.rem(x + off, NX), at] = both[j * cols : (j + 1) * cols]
 
 
 def partial_hidden(seat, blocks, own_cols, other_cols, cols):
@@ -58,8 +61,9 @@
     return pl.pallas_call(
         hidden_kernel,
         out_shape=jax.ShapeDtypeStruct((NX, NY, cols, 128), f32),
-        in_specs=[pl.BlockSpec(memory_space=pltpu.SMEM)] + [vmem] * 7,
+        in_specs=[pl.BlockSpec(memory_space=pltpu.SMEM)] + [vmem] * 6,
         out_specs=vmem,
+        scratch_shapes=[pltpu.VMEM((NX, 64, blocks[0].shape[1]), bf16)],
         cost_estimate=pl.CostEstimate(flops=330_000_000, bytes_accessed=3_400_000, transcendentals=0),
     )(seat, *blocks, own_cols, other_cols)
 
@@ -74,11 +78,10 @@
 
 def centre_gradient(centres, own, received):
     rows, emb = centres.shape
-    block = pl.BlockSpec((rows // 4, emb), lambda i: (i, 0))
+    block = pl.BlockSpec(memory_space=pltpu.VMEM)
     return pl.pallas_call(
         centre_kernel,
         out_shape=jax.ShapeDtypeStruct((rows, emb), f32),
-        grid=(4,),
         in_specs=[block] * 3,
         out_specs=block,
         cost_estimate=pl.CostEstimate(flops=3_000_000, bytes_accessed=3_700_000, transcendentals=512),
@@ -96,25 +99,26 @@
     emb = proj_out.shape[1]
     cen = centres.shape[0]
     images = NX * NY * rows
-    lanes = emb // 4
     zi, xi, yi, ci = (lax.axis_index(a) for a in ("z", "x", "y", "c"))
 
-    out_part = lax.dynamic_slice_in_dim(proj_out, yi * lanes, lanes, 1)
-    out_part = spread(out_part, "z", NZ).reshape(NZ * proj_out.shape[0], lanes)
     from_left = shift(features, "x", 1)
     from_right = shift(features, "x", 3)
-    cols_in = proj_in.T
-    own_cols = [cols_in]
-    for by in (1, 3, 2):
-        own_cols.append(shift(cols_in, "y", by))
-    own_cols = jnp.concatenate(own_cols, axis=0)
-    far_a = shift(from_left[:32], "x", 1)
-    far_b = shift(from_right[32:], "x", 3)
+    own_cols = proj_in.T
+    own_cols = jnp.concatenate([own_cols, lax.ppermute(own_cols, "y", [(0, 1), (1, 0), (2, 3), (3, 2)])], axis=0)
+    own_cols = jnp.concatenate([own_cols, lax.ppermute(own_cols, "y", [(0, 3), (3, 0), (1, 2), (2, 1)])], axis=0)
+    from_far = shift(from_left, "x", 1)
+    whole = spread(proj_out, "z", NZ)
     other_cols = partner(own_cols)
     seat = jnp.stack([xi, yi, ci]).astype(jnp.int32)
-    part = partial_hidden(seat, (features, from_left, from_right, far_a, far_b), own_cols, other_cols, cols)
-
-    all_labels = spread(labels, XY, NX * NY).reshape(images, 1)
+    part = partial_hidden(seat, (features, from_left, from_right, from_far), own_cols, other_cols, cols)
+    part = exchange(part, "x").reshape(NZ, cols, 128)
+
+    part, labels = lax.optimization_barrier((part, labels))
+    all_labels = lax.dynamic_update_slice_in_dim(jnp.zeros(NY * rows, jnp.int32), labels, yi * rows, 0)
+    all_labels = lax.psum(all_labels, "y")
+    all_labels = lax.dynamic_update_slice_in_dim(jnp.zeros(images, jnp.int32), all_labels, xi * NY * rows, 0)
+    all_labels = lax.psum(all_labels, "x")
+    all_labels = all_labels.reshape(images, 1)
     wide = centres.astype(f32)
     cinv = lax.rsqrt(jnp.sum(wide * wide, axis=1) + norm_eps)
     unit_centre = wide * cinv[:, None]
@@ -125,19 +129,14 @@
     position = jnp.concatenate([(chip + ci) * cen + step, (chip + 1 - ci) * cen + step])
     target = all_labels == position[None, :]
 
-    part = exchange(part, "x").reshape(NZ, cols, 128)
     hidden = jnp.sum(exchange(part, "z"), axis=0).astype(bf16)
     hidden = spread(hidden, "z", NZ).reshape(NZ * cols, 128)
-    whole = jnp.stack([out_part, shift(out_part, "y", 1), shift(out_part, "y", 3), shift(out_part, "y", 2)])
-    order = jnp.stack([lax.rem(yi * 0 + k + 4 - yi, 4) for k in range(4)])
-    order = jnp.where(order == 3, 1, jnp.where(order == 1, 2, jnp.where(order == 2, 3, 0)))
-    whole = jnp.take(whole, order, axis=0).transpose(1, 0, 2).reshape(NZ, NC, cols, emb)
 
     def over_rows(left, right):
         return lax.dot_general(left, right, (((0,), (0,)), ((), ())), preferred_element_type=f32)
 
-    embed = over_rows(hidden[:, :rows], whole[:, 0].reshape(NZ * cols, emb))
-    embed = embed + over_rows(hidden[:, 64 : 64 + rows], whole[:, 1].reshape(NZ * cols, emb))
+    embed = over_rows(hidden[:, :rows], whole[:, :cols].reshape(NZ * cols, emb))
+    embed = embed + over_rows(hidden[:, 64 : 64 + rows], whole[:, cols:].reshape(NZ * cols, emb))
     inverse = lax.rsqrt(jnp.sum(embed * embed, axis=1) + norm_eps)
     unit = embed * inverse[:, None]
     units = spread(unit.astype(bf16), XY, NX * NY).reshape(images, emb)
@@ -162,14 +161,22 @@
     hit_slope = jnp.sum(jnp.where(target, slope, 0.0), axis=1)
     hit_turn = jnp.sum(jnp.where(target, slope * cosine, 0.0), axis=1)
 
-    pull = jnp.dot(rest.astype(bf16), low, preferred_element_type=f32).astype(bf16)
-    pull = exchange(pull.reshape(NX * NY, rows, emb), XY)
-
-    sums = jnp.stack([rest_sum, hit, rest_cos, hit_slope, hit_turn]).reshape(5, images // 128, 128)
-    sums = lax.psum(lax.psum(sums, "x"), "y").reshape(5, images)
-    owned = lax.dynamic_slice_in_dim(sums, (xi * NY + yi) * rows, rows, 1)
-    owned = jnp.pad(owned, ((0, 0), (0, 128 - rows)))
-    totals = (sums[0] + sums[1]).reshape(images // 128, 128)
+    pull = jnp.dot(rest.astype(bf16), low, preferred_element_type=f32).astype(bf16).reshape(NX * NY, rows, emb)
+    tall = images // 128
+    totals = jnp.concatenate(split_pair((rest_sum + hit).reshape(tall, 128)), axis=0)
+    totals = jnp.pad(totals, ((0, 16 - 2 * tall), (0, 0))).reshape(4, emb)
+    totals = jnp.broadcast_to(totals[None], (NX * NY, 4, emb))
+    owned = jnp.stack([rest_sum, hit, rest_cos, hit_slope, hit_turn]).reshape(5, NX * NY, rows)
+    owned = jnp.pad(owned.transpose(1, 0, 2), ((0, 0), (0, 0), (0, 64 - rows)))
+    owned = jnp.concatenate(split_pair(owned), axis=1).reshape(NX * NY, 640)
+    owned = jnp.pad(owned, ((0, 0), (0, 4 * emb - 640))).reshape(NX * NY, 4, emb)
+    pull = jnp.concatenate([pull, totals, owned], axis=1)
+    pull = exchange(pull, XY)
+    pull = jnp.sum(pull.astype(f32), axis=0)
+    totals = pull[rows : rows + 4].reshape(16, 128)
+    totals = totals[:tall] + totals[tall : 2 * tall]
+    owned = pull[rows + 4 :].reshape(4 * emb)[:640].reshape(10, 64)
+    owned = jnp.pad(owned[:5] + owned[5:], ((0, 0), (0, 64)))
 
     width = emb // NZ
 
@@ -177,7 +184,7 @@
         block = block.astype(bf16).reshape(4, rows // 4, NZ, width)
         return block.transpose(2, 1, 0, 3).reshape(NZ, rows // 4, 4 * width)
 
-    pull = jnp.sum(pull.astype(f32), axis=0)
+    pull = pull[:rows]
     common = jnp.concatenate(split_pair(totals) + split_pair(owned), axis=0)
     common = jnp.broadcast_to(common[None], (NZ,) + common.shape)
     pack = jnp.concatenate([by_column(pull), by_column(chosen), common], axis=1)
@@ -187,7 +194,7 @@
     def by_row(block):
         return block.reshape(rows // 4, 4, width).transpose(1, 0, 2).reshape(rows, width)
 
-    quarter, tall = rows // 4, images // 128
+    quarter = rows // 4
     pull, chosen = by_row(pack[:quarter]), by_row(pack[quarter : 2 * quarter])
     common = pack[2 * quarter :]
     total = (common[:tall] + common[tall : 2 * tall]).reshape(images, 1)

time: 269 us -> 266 us (0.989)
  starting transfers between devices: 108 us -> 62.4 us
  blocking collectives: 35.7 us -> 58.9 us
  waiting for transfers between devices: 72.8 us -> 92.1 us
  local copies, waits for them, and re-layouts: 10.2 us -> 7.33 us
    all_to_all x0 -> x2, blocking collectives: none -> 41.5 us  [exchange(): return lax.all_to_all(blocks, axis, 0, 0)]
    all_to_all x9 -> x6, starting transfers between devices: 69.3 us -> 37 us  [exchange(): return lax.all_to_all(blocks, axis, 0, 0)]
    all_to_all x9 -> x6, waiting for transfers between devices: 46 us -> 74.2 us  [exchange(): return lax.all_to_all(blocks, axis, 0, 0)]
    ppermute x10 -> x3, starting transfers between devices: 32.4 us -> 10.9 us  [shift(): return lax.ppermute(block, axis, [(i, (i + by) % 4) for i in range(4)])]
    psum x2, blocking collectives: 35.7 us -> 17.4 us  [the longest x1 9.46 us: step_of(): all_labels = lax.psum(all_labels, 'y')]
    ppermute x10 -> x3, waiting for transfers between devices: 26.4 us -> 9.01 us  [shift(): return lax.ppermute(block, axis, [(i, (i + by) % 4) for i in range(4)])]
    ppermute x0 -> x2, waiting for transfers between devices: none -> 8.81 us  [the longest x1 4.99 us: step_of(): lax.ppermute(own_cols, 'y', [(0, 1), (1, 0), (2, 3), (3, 2)])]
    ppermute x0 -> x2, starting transfers between devices: none -> 8.54 us  [the longest x1 4.92 us: step_of(): lax.ppermute(own_cols, 'y', [(0, 3), (3, 0), (1, 2), (2, 1)])]
  transfers between devices with their start and end apart: 22 -> 14, of which waited for: 13 -> 9; matrix products, arithmetic and copies ran while one was open for 7% -> 8% of each run, Pallas kernels for 2% -> 0%
where the time goes in v3:
time: 266 us; the launch traced here: 262 us
  waiting for transfers between devices  92.1 us (35%)
  starting transfers between devices  62.4 us (23%)
  blocking collectives  58.9 us (22%)
  matrix products  25.7 us (10%)
  local copies, waits for them, and re-layouts  7.33 us (3%)
  other arithmetic  7.19 us (3%)
  Pallas kernels  7.04 us (3%)
    all_to_all x6, waiting for transfers between devices, exchange(): return lax.all_to_all(blocks, axis, 0, 0)  74.2 us
    all_to_all x2, blocking collectives, exchange(): return lax.all_to_all(blocks, axis, 0, 0)  41.5 us
    all_to_all x6, starting transfers between devices, exchange(): return lax.all_to_all(blocks, axis, 0, 0)  37 us
    ppermute x3, starting transfers between devices, shift(): return lax.ppermute(block, axis, [(i, (i + by) % 4) for i in range(4)])  10.9 us
    psum x1, blocking collectives, step_of(): all_labels = lax.psum(all_labels, 'y')  9.46 us
    ppermute x3, waiting for transfers between devices, shift(): return lax.ppermute(block, axis, [(i, (i + by) % 4) for i in range(4)])  9.01 us
    psum x1, blocking collectives, step_of(): all_labels = lax.psum(all_labels, 'x')  7.93 us
    dot_general x1, matrix products, step_of(): lax.dot_general(units, low, (((1,), (1,)), ((), ())), preferred_element_t...  7.4 us
  transfers between devices with their start and end apart: 14, of which 9 were waited for; matrix products, arithmetic and copies ran while one was open for 8% of the time, Pallas kernels for 0%

profile of v3, /device:TPU:6, one launch (start us, length us, event | category | flops | bytes accessed | tf_op | source)
XLA Modules:
  0.0 261.8 jit_solution(18179449142633729982)
XLA Ops:
  4.3 5.0 %collective-permute-done.3 = bf16[24,3840]{1,0:T(8,128)(2,1)S(1)} collective-permute-done((bf16[24,3840]{1,0:T(8,128)(2,1)}, bf16[24,3840]{1,0:T(8,128)(2,1)S(1)}, u32[]{:S(2)}, u32[]{:S(2)}) %collective-permute-start.3) | collective-permute-done | bytes 184352 | tf_op jit(solution)/shard_map/ppermute | solution.py:107
  10.2 4.9 %collective-permute-start.4 = (bf16[48,3840]{1,0:T(8,128)(2,1)S(1)}, bf16[48,3840]{1,0:T(8,128)(2,1)S(1)}, u32[]{:S(2)}, u32[]{:S(2)}) collective-permute-start(bf16[48,3840]{1,0:T(8,128)(2,1)S(1)} %pad_maximum_fusion.3), channel_id=1, source_target_pairs={{0,6},{6,0},{2,4},{4,2},{1,7},{7,1},{3,5},{5,3},{8,14},{14,8},{10,... | collective-permute-start | bytes 1105928 | tf_op jit(solution)/shard_map/ppermute | solution.py:108
  15.1 3.9 %collective-permute-start = (bf16[56,3840]{1,0:T(8,128)(2,1)}, bf16[56,3840]{1,0:T(8,128)(2,1)S(1)}, u32[]{:S(2)}, u32[]{:S(2)}) collective-permute-start(bf16[56,3840]{1,0:T(8,128)(2,1)} %mine.1), channel_id=1, source_target_pairs={{0,8},{8,16},{16,24},{24,0},{1,9},{9,17},{17,25},{25,1},{2,10},{10... | collective-permute-start | bytes 1290248 | tf_op jit(solution)/shard_map/ppermute | solution.py:35
  19.0 3.8 %collective-permute-done.4 = bf16[48,3840]{1,0:T(8,128)(2,1)S(1)} collective-permute-done((bf16[48,3840]{1,0:T(8,128)(2,1)S(1)}, bf16[48,3840]{1,0:T(8,128)(2,1)S(1)}, u32[]{:S(2)}, u32[]{:S(2)}) %collective-permute-start.4) | collective-permute-done | bytes 368672 | tf_op jit(solution)/shard_map/ppermute | solution.py:108
  28.7 4.3 %collective-permute-start.2 = (bf16[56,3840]{1,0:T(8,128)(2,1)S(1)}, bf16[56,3840]{1,0:T(8,128)(2,1)S(1)}, u32[]{:S(2)}, u32[]{:S(2)}) collective-permute-start(bf16[56,3840]{1,0:T(8,128)(2,1)S(1)} %collective-permute-done.left), channel_id=1, source_target_pairs={{0,8},{8,16},{16,24},{24,0},{1,9},{9,17},{17,25},{25,1},{2,10},{10... | collective-permute-start | bytes 1290248 | tf_op jit(solution)/shard_map/ppermute | solution.py:35
  33.6 8.0 %collective-permute-done.1.right = bf16[56,3840]{1,0:T(8,128)(2,1)S(1)} collective-permute-done((bf16[56,3840]{1,0:T(8,128)(2,1)}, bf16[56,3840]{1,0:T(8,128)(2,1)S(1)}, u32[]{:S(2)}, u32[]{:S(2)}) %collective-permute-start.1) | collective-permute-done | bytes 430112 | tf_op jit(solution)/shard_map/ppermute | solution.py:35
  44.2 4.0 %shard_map.68 = f32[4,4,24,128]{3,2,1,0:T(8,128)} custom-call(s32[3]{0:T(128)} %pad_add_fusion.1.seat, bf16[56,3840]{1,0:T(8,128)(2,1)} %mine.1, bf16[56,3840]{1,0:T(8,128)(2,1)} %copy-done.3, bf16[56,3840]{1,0:T(8,128)(2,1)} %copy-done.4, bf16[56,3840]{1,0:T(8,128)(2,1)} %copy-done.5, bf16[96,3840]{1,0:T(8,128)(2,1)} %copy-done.1, bf16[96,3840]{1,0:T(8,128)(2,1)} %copy-done.2), custom_call_target="tpu_custom_call" | custom-call | flops 330000000 | bytes 3400000 | tf_op jit(solution)/shard_map/pallas_call | solution.py:61
  48.2 11.2 %all_to_all.40 = f32[4,4,24,128]{3,2,1,0:T(8,128)S(1)} all-to-all(f32[4,4,24,128]{3,2,1,0:T(8,128)} %shard_map.68), channel_id=1, replica_groups=mesh['z'=16,'x'=4,'y'=4,'c'=2] {'x'}, dimensions={0} | all-to-all | bytes 393216 | tf_op jit(solution)/shard_map/all_to_all | solution.py:23
  59.4 30.3 %all_to_all.41 = f32[16,24,128]{2,1,0:T(8,128)S(1)} all-to-all(f32[16,24,128]{2,1,0:T(8,128)S(1)} %bitcast.53), channel_id=1, replica_groups=mesh['z'=16,'x'=4,'y'=4,'c'=2] {'z'}, dimensions={0} | all-to-all | bytes 393216 | tf_op jit(solution)/shard_map/all_to_all | solution.py:23
  90.7 4.4 %all-to-all-start.3 = ((bf16[16,48,512]{2,1,0:T(8,128)(2,1)}), bf16[16,48,512]{2,1,0:T(8,128)(2,1)S(1)}, u32[]{:S(2)}, u32[]{:S(2)}) async-start(bf16[16,48,512]{2,1,0:T(8,128)(2,1)} %broadcast_in_dim.33), calls=%async_computation.3 | async-start | bytes 1572864 | tf_op jit(solution)/shard_map/all_to_all | solution.py:23
  95.3 36.2 %all-to-all-done.3 = bf16[16,48,512]{2,1,0:T(8,128)(2,1)S(1)} async-done(((bf16[16,48,512]{2,1,0:T(8,128)(2,1)}), bf16[16,48,512]{2,1,0:T(8,128)(2,1)S(1)}, u32[]{:S(2)}, u32[]{:S(2)}) %all-to-all-start.3) | async-done | bytes 786464 | tf_op jit(solution)/shard_map/all_to_all | solution.py:23
  132.1 8.5 %all-to-all-start.2 = ((bf16[16,24,128]{2,1,0:T(8,128)(2,1)}), bf16[16,24,128]{2,1,0:T(8,128)(2,1)S(1)}, u32[]{:S(2)}, u32[]{:S(2)}) async-start(bf16[16,24,128]{2,1,0:T(8,128)(2,1)} %broadcast_in_dim.32), calls=%async_computation.2 | async-start | bytes 196608 | tf_op jit(solution)/shard_map/all_to_all | solution.py:23
  140.8 13.1 %all-to-all-done.2 = bf16[16,24,128]{2,1,0:T(8,128)(2,1)S(1)} async-done(((bf16[16,24,128]{2,1,0:T(8,128)(2,1)}), bf16[16,24,128]{2,1,0:T(8,128)(2,1)S(1)}, u32[]{:S(2)}, u32[]{:S(2)}) %all-to-all-start.2) | async-done | bytes 98336 | tf_op jit(solution)/shard_map/all_to_all | solution.py:23
  156.2 7.4 %all-to-all-start.4 = ((bf16[16,56,512]{2,1,0:T(8,128)(2,1)}), bf16[16,56,512]{2,1,0:T(8,128)(2,1)S(1)}, u32[]{:S(2)}, u32[]{:S(2)}) async-start(bf16[16,56,512]{2,1,0:T(8,128)(2,1)} %broadcast_in_dim.34), calls=%async_computation.4 | async-start | bytes 1835008 | tf_op jit(solution)/shard_map/all_to_all | solution.py:23
  166.0 9.5 %psum.14 = s32[224]{0:T(256)S(1)} all-reduce(s32[224]{0:T(256)S(1)} %dynamic_update_slice.6), channel_id=1, replica_groups=mesh['z'=16,'x'=4,'y'=4,'c'=2] {'y'}, use_global_device_ids=true, to_apply=%region_0.0 | all-reduce | flops 224 | bytes 1792 | tf_op jit(solution)/shard_map/psum | solution.py:118
  175.6 7.9 %psum.15 = s32[896]{0:T(1024)S(1)} all-reduce(s32[896]{0:T(1024)S(1)} %dynamic_update_slice.7), channel_id=1, replica_groups=mesh['z'=16,'x'=4,'y'=4,'c'=2] {'x'}, use_global_device_ids=true, to_apply=%region_1.0 | all-reduce | flops 896 | bytes 7168 | tf_op jit(solution)/shard_map/psum | solution.py:120
  185.6 7.4 %fusion.6 = (f32[896]{0:T(1024)S(1)}, f32[896]{0:T(1024)S(1)}, f32[896]{0:T(1024)S(1)}, f32[896]{0:T(1024)S(1)}, f32[896]{0:T(1024)S(1)}, /*index=5*/f32[896,1024]{1,0:T(8,128)}) fusion(s32[1024]{0:T(1024)S(1)} %pad_add_fusion, s32[896]{0:T(1024)S(1)} %psum.15, bf16[896,512]{1,0:T(8,128)(2,1)S(1)} %bitcast.40, ...), kind=kOutput, calls=%fused_computation.13 | convolution fusion | flops 965471872 | bytes 5661696 | tf_op jit(solution)/shard_map/dot_general | solution.py:151
  193.6 6.6 %all-to-all-start.6 = ((bf16[16,56,512]{2,1,0:T(8,128)(2,1)}), bf16[16,56,512]{2,1,0:T(8,128)(2,1)S(1)}, u32[]{:S(2)}, u32[]{:S(2)}) async-start(bf16[16,56,512]{2,1,0:T(8,128)(2,1)} %bitcast.13), calls=%async_computation.6 | async-start | bytes 1835008 | tf_op jit(solution)/shard_map/all_to_all | solution.py:23
  200.4 4.5 %fusion.18 = bf16[896,512]{1,0:T(8,128)(2,1)S(1)} fusion(s32[1024]{0:T(1024)S(1)} %pad_add_fusion, s32[896]{0:T(1024)S(1)} %psum.15, bf16[512,512]{1,0:T(8,128)(2,1)S(1)} %collective-permute-done.6, bf16[512,512]{1,0:T(8,128)(2,1)S(1)} %fusion.25, f32[896,1024]{1,0:T(8,128)} %get-tuple-element.53), kind=kOutput, calls=%fused_computation.31 | convolution fusion | flops 953090048 | bytes 5643776 | tf_op jit(solution)/shard_map/dot_general | solution.py:164
  206.1 4.6 %all-to-all-done.6 = bf16[16,56,512]{2,1,0:T(8,128)(2,1)S(1)} async-done(((bf16[16,56,512]{2,1,0:T(8,128)(2,1)}), bf16[16,56,512]{2,1,0:T(8,128)(2,1)S(1)}, u32[]{:S(2)}, u32[]{:S(2)}) %all-to-all-start.6) | async-done | bytes 917536 | tf_op jit(solution)/shard_map/all_to_all | solution.py:23
  210.7 5.6 %all-to-all-start.5 = ((bf16[16,64,512]{2,1,0:T(8,128)(2,1)}), bf16[16,64,512]{2,1,0:T(8,128)(2,1)S(1)}, u32[]{:S(2)}, u32[]{:S(2)}) async-start(bf16[16,64,512]{2,1,0:T(8,128)(2,1)} %pad_maximum_fusion.1), calls=%async_computation.5 | async-start | bytes 2097152 | tf_op jit(solution)/shard_map/all_to_all | solution.py:23
  216.9 10.4 %all-to-all-done.5 = bf16[16,64,512]{2,1,0:T(8,128)(2,1)S(1)} async-done(((bf16[16,64,512]{2,1,0:T(8,128)(2,1)}), bf16[16,64,512]{2,1,0:T(8,128)(2,1)S(1)}, u32[]{:S(2)}, u32[]{:S(2)}) %all-to-all-start.5) | async-done | bytes 1048608 | tf_op jit(solution)/shard_map/all_to_all | solution.py:23
  228.8 4.6 %all-to-all-start.7 = ((bf16[16,52,128]{2,1,0:T(8,128)(2,1)}), bf16[16,52,128]{2,1,0:T(8,128)(2,1)S(1)}, u32[]{:S(2)}, u32[]{:S(2)}) async-start(bf16[16,52,128]{2,1,0:T(8,128)(2,1)} %pad_maximum_fusion.4), calls=%async_computation.7 | async-start | bytes 458752 | tf_op jit(solution)/shard_map/all_to_all | solution.py:23
  237.4 10.0 %all-to-all-done.7 = bf16[16,52,128]{2,1,0:T(8,128)(2,1)S(1)} async-done(((bf16[16,52,128]{2,1,0:T(8,128)(2,1)}), bf16[16,52,128]{2,1,0:T(8,128)(2,1)S(1)}, u32[]{:S(2)}, u32[]{:S(2)}) %all-to-all-start.7) | async-done | bytes 213024 | tf_op jit(solution)/shard_map/all_to_all | solution.py:23
  (106 shorter events, 44.6 us)
Async XLA Ops:
  0.6 89.1 %copy-start.6 = (bf16[48,512]{1,0:T(8,128)(2,1)S(1)}, bf16[48,512]{1,0:T(8,128)(2,1)}, u32[]{:S(2)}) copy-start(bf16[48,512]{1,0:T(8,128)(2,1)} %param.7) | copy-start | bytes 147460
  0.6 8.6 %collective-permute-start.3 = (bf16[24,3840]{1,0:T(8,128)(2,1)}, bf16[24,3840]{1,0:T(8,128)(2,1)S(1)}, u32[]{:S(2)}, u32[]{:S(2)}) collective-permute-start(bf16[24,3840]{1,0:T(8,128)(2,1)} %bitcast.54), channel_id=1, source_target_pairs={{0,2},{2,0},{4,6},{6,4},{1,3},{3,1},{5,7},{7,5},{8,10},{10,8},{12,... | collective-permute-start | bytes 552968 | tf_op jit(solution)/shard_map/ppermute | solution.py:107
  10.2 12.6 %collective-permute-start.4 = (bf16[48,3840]{1,0:T(8,128)(2,1)S(1)}, bf16[48,3840]{1,0:T(8,128)(2,1)S(1)}, u32[]{:S(2)}, u32[]{:S(2)}) collective-permute-start(bf16[48,3840]{1,0:T(8,128)(2,1)S(1)} %pad_maximum_fusion.3), channel_id=1, source_target_pairs={{0,6},{6,0},{2,4},{4,2},{1,7},{7,1},{3,5},{5,3},{8,14},{14,8},{10,... | collective-permute-start | bytes 1105928 | tf_op jit(solution)/shard_map/ppermute | solution.py:108
  15.1 13.5 %collective-permute-start = (bf16[56,3840]{1,0:T(8,128)(2,1)}, bf16[56,3840]{1,0:T(8,128)(2,1)S(1)}, u32[]{:S(2)}, u32[]{:S(2)}) collective-permute-start(bf16[56,3840]{1,0:T(8,128)(2,1)} %mine.1), channel_id=1, source_target_pairs={{0,8},{8,16},{16,24},{24,0},{1,9},{9,17},{17,25},{25,1},{2,10},{10... | collective-permute-start | bytes 1290248 | tf_op jit(solution)/shard_map/ppermute | solution.py:35
  23.8 18.8 %copy-start.1 = (bf16[96,3840]{1,0:T(8,128)(2,1)}, bf16[96,3840]{1,0:T(8,128)(2,1)S(1)}, u32[]{:S(2)}) copy-start(bf16[96,3840]{1,0:T(8,128)(2,1)S(1)} %pad_maximum_fusion.2.own_cols) | copy-start | bytes 2211844
  23.8 71.3 %copy-start = (bf16[512,512]{1,0:T(8,128)(2,1)S(1)}, bf16[512,512]{1,0:T(8,128)(2,1)}, u32[]{:S(2)}) copy-start(bf16[512,512]{1,0:T(8,128)(2,1)} %centres.1) | copy-start | bytes 1572868
  23.9 18.8 %collective-permute-start.5 = (bf16[96,3840]{1,0:T(8,128)(2,1)S(1)}, bf16[96,3840]{1,0:T(8,128)(2,1)S(1)}, u32[]{:S(2)}, u32[]{:S(2)}) collective-permute-start(bf16[96,3840]{1,0:T(8,128)(2,1)S(1)} %pad_maximum_fusion.2.own_cols), channel_id=1, source_target_pairs={{0,1},{1,0},{2,3},{3,2},{4,5},{5,4},{6,7},{7,6},{8,9},{9,8},{10,11... | collective-permute-start | bytes 2211848 | tf_op jit(solution)/shard_map/ppermute | solution.py:31
  25.9 15.6 %collective-permute-start.1 = (bf16[56,3840]{1,0:T(8,128)(2,1)}, bf16[56,3840]{1,0:T(8,128)(2,1)S(1)}, u32[]{:S(2)}, u32[]{:S(2)}) collective-permute-start(bf16[56,3840]{1,0:T(8,128)(2,1)} %mine.1), channel_id=1, source_target_pairs={{0,24},{8,0},{16,8},{24,16},{1,25},{9,1},{17,9},{25,17},{2,26},{10... | collective-permute-start | bytes 1290248 | tf_op jit(solution)/shard_map/ppermute | solution.py:35
  28.7 13.9 %copy-start.3 = (bf16[56,3840]{1,0:T(8,128)(2,1)}, bf16[56,3840]{1,0:T(8,128)(2,1)S(1)}, u32[]{:S(2)}) copy-start(bf16[56,3840]{1,0:T(8,128)(2,1)S(1)} %collective-permute-done.left) | copy-start | bytes 1290244
  28.7 13.9 %collective-permute-start.2 = (bf16[56,3840]{1,0:T(8,128)(2,1)S(1)}, bf16[56,3840]{1,0:T(8,128)(2,1)S(1)}, u32[]{:S(2)}, u32[]{:S(2)}) collective-permute-start(bf16[56,3840]{1,0:T(8,128)(2,1)S(1)} %collective-permute-done.left), channel_id=1, source_target_pairs={{0,8},{8,16},{16,24},{24,0},{1,9},{9,17},{17,25},{25,1},{2,10},{10... | collective-permute-start | bytes 1290248 | tf_op jit(solution)/shard_map/ppermute | solution.py:35
  41.5 1.1 copy-start.4
  42.6 0.8 copy-start.5
  43.4 0.9 copy-start.2
  90.7 40.8 %all-to-all-start.3 = ((bf16[16,48,512]{2,1,0:T(8,128)(2,1)}), bf16[16,48,512]{2,1,0:T(8,128)(2,1)S(1)}, u32[]{:S(2)}, u32[]{:S(2)}) async-start(bf16[16,48,512]{2,1,0:T(8,128)(2,1)} %broadcast_in_dim.33), calls=%async_computation.3 | async-start | bytes 1572864 | tf_op jit(solution)/shard_map/all_to_all | solution.py:23
  132.1 33.6 %copy-start.8 = (s32[56]{0:T(128)S(1)}, s32[56]{0:T(128)}, u32[]{:S(2)}) copy-start(s32[56]{0:T(128)} %param.9) | copy-start | bytes 676
  132.1 21.7 %all-to-all-start.2 = ((bf16[16,24,128]{2,1,0:T(8,128)(2,1)}), bf16[16,24,128]{2,1,0:T(8,128)(2,1)S(1)}, u32[]{:S(2)}, u32[]{:S(2)}) async-start(bf16[16,24,128]{2,1,0:T(8,128)(2,1)} %broadcast_in_dim.32), calls=%async_computation.2 | async-start | bytes 196608 | tf_op jit(solution)/shard_map/all_to_all | solution.py:23
  156.2 29.4 %all-to-all-start.4 = ((bf16[16,56,512]{2,1,0:T(8,128)(2,1)}), bf16[16,56,512]{2,1,0:T(8,128)(2,1)S(1)}, u32[]{:S(2)}, u32[]{:S(2)}) async-start(bf16[16,56,512]{2,1,0:T(8,128)(2,1)} %broadcast_in_dim.34), calls=%async_computation.4 | async-start | bytes 1835008 | tf_op jit(solution)/shard_map/all_to_all | solution.py:23
  163.7 19.8 %collective-permute-start.6 = (bf16[512,512]{1,0:T(8,128)(2,1)S(1)}, bf16[512,512]{1,0:T(8,128)(2,1)S(1)}, u32[]{:S(2)}, u32[]{:S(2)}) collective-permute-start(bf16[512,512]{1,0:T(8,128)(2,1)S(1)} %fusion.25), channel_id=1, source_target_pairs={{0,1},{1,0},{2,3},{3,2},{4,5},{5,4},{6,7},{7,6},{8,9},{9,8},{10,11... | collective-permute-start | bytes 1572872 | tf_op jit(solution)/shard_map/ppermute | solution.py:31
  183.5 16.9 %copy-start.7 = (bf16[512,512]{1,0:T(8,128)(2,1)}, bf16[512,512]{1,0:T(8,128)(2,1)S(1)}, u32[]{:S(2)}) copy-start(bf16[512,512]{1,0:T(8,128)(2,1)S(1)} %collective-permute-done.6) | copy-start | bytes 1572868
  193.6 17.1 %all-to-all-start.6 = ((bf16[16,56,512]{2,1,0:T(8,128)(2,1)}), bf16[16,56,512]{2,1,0:T(8,128)(2,1)S(1)}, u32[]{:S(2)}, u32[]{:S(2)}) async-start(bf16[16,56,512]{2,1,0:T(8,128)(2,1)} %bitcast.13), calls=%async_computation.6 | async-start | bytes 1835008 | tf_op jit(solution)/shard_map/all_to_all | solution.py:23
  210.7 16.6 %all-to-all-start.5 = ((bf16[16,64,512]{2,1,0:T(8,128)(2,1)}), bf16[16,64,512]{2,1,0:T(8,128)(2,1)S(1)}, u32[]{:S(2)}, u32[]{:S(2)}) async-start(bf16[16,64,512]{2,1,0:T(8,128)(2,1)} %pad_maximum_fusion.1), calls=%async_computation.5 | async-start | bytes 2097152 | tf_op jit(solution)/shard_map/all_to_all | solution.py:23
  228.8 18.6 %all-to-all-start.7 = ((bf16[16,52,128]{2,1,0:T(8,128)(2,1)}), bf16[16,52,128]{2,1,0:T(8,128)(2,1)S(1)}, u32[]{:S(2)}, u32[]{:S(2)}) async-start(bf16[16,52,128]{2,1,0:T(8,128)(2,1)} %pad_maximum_fusion.4), calls=%async_computation.7 | async-start | bytes 458752 | tf_op jit(solution)/shard_map/all_to_all | solution.py:23
  251.5 7.2 %collective-permute-start.7 = (f32[512,512]{1,0:T(8,128)}, f32[512,512]{1,0:T(8,128)}, u32[]{:S(2)}, u32[]{:S(2)}) collective-permute-start(f32[512,512]{1,0:T(8,128)} %convolution_add_fusion), channel_id=1, source_target_pairs={{0,1},{1,0},{2,3},{3,2},{4,5},{5,4},{6,7},{7,6},{8,9},{9,8},{10,11... | collective-permute-start | bytes 3145736 | tf_op jit(solution)/shard_map/ppermute | solution.py:31

commit v4 on v3

--- a/solution.py
+++ b/solution.py
@@ -104,10 +104,10 @@
     from_left = shift(features, "x", 1)
     from_right = shift(features, "x", 3)
     own_cols = proj_in.T
+    own_out = spread(lax.dynamic_slice_in_dim(proj_out, ci * (emb // 2), emb // 2, 1), "z", NZ)
     own_cols = jnp.concatenate([own_cols, lax.ppermute(own_cols, "y", [(0, 1), (1, 0), (2, 3), (3, 2)])], axis=0)
     own_cols = jnp.concatenate([own_cols, lax.ppermute(own_cols, "y", [(0, 3), (3, 0), (1, 2), (2, 1)])], axis=0)
     from_far = shift(from_left, "x", 1)
-    whole = spread(proj_out, "z", NZ)
     other_cols = partner(own_cols)
     seat = jnp.stack([xi, yi, ci]).astype(jnp.int32)
     part = partial_hidden(seat, (features, from_left, from_right, from_far), own_cols, other_cols, cols)
@@ -129,14 +129,19 @@
     position = jnp.concatenate([(chip + ci) * cen + step, (chip + 1 - ci) * cen + step])
     target = all_labels == position[None, :]
 
+    other_out = partner(own_out)
     hidden = jnp.sum(exchange(part, "z"), axis=0).astype(bf16)
     hidden = spread(hidden, "z", NZ).reshape(NZ * cols, 128)
 
     def over_rows(left, right):
         return lax.dot_general(left, right, (((0,), (0,)), ((), ())), preferred_element_type=f32)
 
-    embed = over_rows(hidden[:, :rows], whole[:, :cols].reshape(NZ * cols, emb))
-    embed = embed + over_rows(hidden[:, 64 : 64 + rows], whole[:, cols:].reshape(NZ * cols, emb))
+    def embed_with(out_rows):
+        left = over_rows(hidden[:, :rows], out_rows[:, :cols].reshape(NZ * cols, emb // 2))
+        return left + over_rows(hidden[:, 64 : 64 + rows], out_rows[:, cols:].reshape(NZ * cols, emb // 2))
+
+    own, other = embed_with(own_out), embed_with(other_out)
+    embed = jnp.concatenate([jnp.where(ci == 0, own, other), jnp.where(ci == 0, other, own)], axis=1)
     inverse = lax.rsqrt(jnp.sum(embed * embed, axis=1) + norm_eps)
     unit = embed * inverse[:, None]
     units = spread(unit.astype(bf16), XY, NX * NY).reshape(images, emb)
@@ -161,7 +166,7 @@
     hit_slope = jnp.sum(jnp.where(target, slope, 0.0), axis=1)
     hit_turn = jnp.sum(jnp.where(target, slope * cosine, 0.0), axis=1)
 
-    pull = jnp.dot(rest.astype(bf16), low, preferred_element_type=f32).astype(bf16).reshape(NX * NY, rows, emb)
+    pull = jnp.dot(lax.optimization_barrier(rest.astype(bf16)), low, preferred_element_type=f32).astype(bf16).reshape(NX * NY, rows, emb)
     tall = images // 128
     totals = jnp.concatenate(split_pair((rest_sum + hit).reshape(tall, 128)), axis=0)
     totals = jnp.pad(totals, ((0, 16 - 2 * tall), (0, 0))).reshape(4, emb)
@@ -204,14 +209,14 @@
     cosine_t = lax.dot_general(low, units, (((1,), (1,)), ((), ())), preferred_element_type=f32)
     target_t = position[:, None] == all_labels.reshape(1, images)
     rest_t = jnp.where(target_t, 0.0, jnp.exp(scale_logit * cosine_t)).astype(bf16)
-    rest_t, target_t = lax.optimization_barrier((rest_t, target_t.astype(bf16)))
+    joined = lax.optimization_barrier(jnp.concatenate([rest_t, target_t.astype(bf16)], axis=1))
     weight = scale_logit * hit_slope[:, None] * (hit[:, None] / total - 1.0)
     scaled = (units.astype(f32) * (scale_logit / total)).astype(bf16)
     aimed = (units.astype(f32) * weight).astype(bf16)
+    scaled = lax.optimization_barrier(jnp.concatenate([scaled, aimed], axis=0))
 
     def gradient_of(part):
-        left = jnp.dot(rest_t[part], scaled, preferred_element_type=f32)
-        return left + jnp.dot(target_t[part], aimed, preferred_element_type=f32)
+        return jnp.dot(joined[part], scaled, preferred_element_type=f32)
 
     received = partner(gradient_of(slice(cen, None)))
     centre_grad = centre_gradient(centres, gradient_of(slice(0, cen)), received)

time: 266 us -> 246 us (0.925)
  blocking collectives: 58.9 us -> 17.4 us
  starting transfers between devices: 62.4 us -> 85.3 us
  matrix products: 25.7 us -> 20.7 us
    all_to_all x2 -> x0, blocking collectives: 41.5 us -> none  [exchange(): return lax.all_to_all(blocks, axis, 0, 0)]
    all_to_all x6 -> x8, starting transfers between devices: 37 us -> 58.1 us  [exchange(): return lax.all_to_all(blocks, axis, 0, 0)]
    dot_general x5 -> x3, matrix products: 12 us -> 8.38 us  [the longest x2 5.77 us: gradient_of(): return jnp.dot(joined[part], scaled, preferred_element_type=f32)]
    ppermute x3 -> x4, starting transfers between devices: 5.88 us -> 7.67 us  [partner(): return lax.ppermute(block, 'c', SWAP)]
    all_to_all x6 -> x8, waiting for transfers between devices: 74.2 us -> 73.9 us  [exchange(): return lax.all_to_all(blocks, axis, 0, 0)]
  transfers between devices with their start and end apart: 14 -> 17, of which waited for: 9 -> 10; matrix products, arithmetic and copies ran while one was open for 8% -> 11% of each run, Pallas kernels for 0% -> 0%
where the time goes in v4:
time: 246 us; the launch traced here: 241 us
  waiting for transfers between devices  91.8 us (37%)
  starting transfers between devices  85.3 us (35%)
  matrix products  20.7 us (8%)
  blocking collectives  17.4 us (7%)
  local copies, waits for them, and re-layouts  8.98 us (4%)
  other arithmetic  8.55 us (3%)
  Pallas kernels  7.01 us (3%)
    all_to_all x8, waiting for transfers between devices, exchange(): return lax.all_to_all(blocks, axis, 0, 0)  73.9 us
    all_to_all x8, starting transfers between devices, exchange(): return lax.all_to_all(blocks, axis, 0, 0)  58.1 us
    ppermute x3, starting transfers between devices, shift(): return lax.ppermute(block, axis, [(i, (i + by) % 4) for i in range(4)])  10.9 us
    psum x1, blocking collectives, step_of(): all_labels = lax.psum(all_labels, 'y')  9.21 us
    ppermute x3, waiting for transfers between devices, shift(): return lax.ppermute(block, axis, [(i, (i + by) % 4) for i in range(4)])  9.07 us
    psum x1, blocking collectives, step_of(): all_labels = lax.psum(all_labels, 'x')  8.17 us
    dot_general x1, matrix products, step_of(): lax.dot_general(units, low, (((1,), (1,)), ((), ())), preferred_element_t...  8.04 us
    ppermute x4, starting transfers between devices, partner(): return lax.ppermute(block, 'c', SWAP)  7.67 us
  transfers between devices with their start and end apart: 17, of which 10 were waited for; matrix products, arithmetic and copies ran while one was open for 11% of the time, Pallas kernels for 0%

profile of v4, /device:TPU:6, one launch (start us, length us, event | category | flops | bytes accessed | tf_op | source)
XLA Modules:
  0.0 241.0 jit_solution(10570280925963532906)
XLA Ops:
  4.3 5.0 %collective-permute-done.3 = bf16[24,3840]{1,0:T(8,128)(2,1)S(1)} collective-permute-done((bf16[24,3840]{1,0:T(8,128)(2,1)}, bf16[24,3840]{1,0:T(8,128)(2,1)S(1)}, u32[]{:S(2)}, u32[]{:S(2)}) %collective-permute-start.3) | collective-permute-done | bytes 184352 | tf_op jit(solution)/shard_map/ppermute | solution.py:108
  10.2 4.9 %collective-permute-start.4 = (bf16[48,3840]{1,0:T(8,128)(2,1)S(1)}, bf16[48,3840]{1,0:T(8,128)(2,1)S(1)}, u32[]{:S(2)}, u32[]{:S(2)}) collective-permute-start(bf16[48,3840]{1,0:T(8,128)(2,1)S(1)} %pad_maximum_fusion.5), channel_id=1, source_target_pairs={{0,6},{6,0},{2,4},{4,2},{1,7},{7,1},{3,5},{5,3},{8,14},{14,8},{10,... | collective-permute-start | bytes 1105928 | tf_op jit(solution)/shard_map/ppermute | solution.py:109
  15.2 3.9 %collective-permute-start = (bf16[56,3840]{1,0:T(8,128)(2,1)}, bf16[56,3840]{1,0:T(8,128)(2,1)S(1)}, u32[]{:S(2)}, u32[]{:S(2)}) collective-permute-start(bf16[56,3840]{1,0:T(8,128)(2,1)} %mine.1), channel_id=1, source_target_pairs={{0,8},{8,16},{16,24},{24,0},{1,9},{9,17},{17,25},{25,1},{2,10},{10... | collective-permute-start | bytes 1290248 | tf_op jit(solution)/shard_map/ppermute | solution.py:35
  19.1 3.8 %collective-permute-done.4 = bf16[48,3840]{1,0:T(8,128)(2,1)S(1)} collective-permute-done((bf16[48,3840]{1,0:T(8,128)(2,1)S(1)}, bf16[48,3840]{1,0:T(8,128)(2,1)S(1)}, u32[]{:S(2)}, u32[]{:S(2)}) %collective-permute-start.4) | collective-permute-done | bytes 368672 | tf_op jit(solution)/shard_map/ppermute | solution.py:109
  28.6 4.3 %collective-permute-start.2 = (bf16[56,3840]{1,0:T(8,128)(2,1)S(1)}, bf16[56,3840]{1,0:T(8,128)(2,1)}, u32[]{:S(2)}, u32[]{:S(2)}) collective-permute-start(bf16[56,3840]{1,0:T(8,128)(2,1)S(1)} %collective-permute-done.left), channel_id=1, source_target_pairs={{0,8},{8,16},{16,24},{24,0},{1,9},{9,17},{17,25},{25,1},{2,10},{10... | collective-permute-start | bytes 1290248 | tf_op jit(solution)/shard_map/ppermute | solution.py:35
  33.5 7.9 %collective-permute-done.1.right = bf16[56,3840]{1,0:T(8,128)(2,1)S(1)} collective-permute-done((bf16[56,3840]{1,0:T(8,128)(2,1)}, bf16[56,3840]{1,0:T(8,128)(2,1)S(1)}, u32[]{:S(2)}, u32[]{:S(2)}) %collective-permute-start.1) | collective-permute-done | bytes 430112 | tf_op jit(solution)/shard_map/ppermute | solution.py:35
  43.5 4.0 %shard_map.68 = f32[4,4,24,128]{3,2,1,0:T(8,128)} custom-call(s32[3]{0:T(128)} %pad_add_fusion.1.seat, bf16[56,3840]{1,0:T(8,128)(2,1)} %mine.1, bf16[56,3840]{1,0:T(8,128)(2,1)} %copy-done.8, bf16[56,3840]{1,0:T(8,128)(2,1)} %copy-done.9, bf16[56,3840]{1,0:T(8,128)(2,1)} %collective-permute-done.2.far, bf16[96,3840]{1,0:T(8,128)(2,1)} %copy-done.3, ...), custom_call_target="tpu_custom_call" | custom-call | flops 330000000 | bytes 3400000 | tf_op jit(solution)/shard_map/pallas_call | solution.py:61
  47.4 7.6 %all-to-all-start = ((f32[4,4,24,128]{3,2,1,0:T(8,128)}), f32[4,4,24,128]{3,2,1,0:T(8,128)}, u32[]{:S(2)}, u32[]{:S(2)}) async-start(f32[4,4,24,128]{3,2,1,0:T(8,128)} %shard_map.68), calls=%async_computation | async-start | bytes 393216 | tf_op jit(solution)/shard_map/all_to_all | solution.py:23
  55.0 4.4 %all-to-all-done = f32[4,4,24,128]{3,2,1,0:T(8,128)} async-done(((f32[4,4,24,128]{3,2,1,0:T(8,128)}), f32[4,4,24,128]{3,2,1,0:T(8,128)}, u32[]{:S(2)}, u32[]{:S(2)}) %all-to-all-start) | async-done | bytes 196640 | tf_op jit(solution)/shard_map/all_to_all | solution.py:23
  60.2 15.2 %all-to-all-start.3 = ((bf16[16,48,256]{2,1,0:T(8,128)(2,1)}), bf16[16,48,256]{2,1,0:T(8,128)(2,1)S(1)}, u32[]{:S(2)}, u32[]{:S(2)}) async-start(bf16[16,48,256]{2,1,0:T(8,128)(2,1)} %broadcast_in_dim.33), calls=%async_computation.3 | async-start | bytes 786432 | tf_op jit(solution)/shard_map/all_to_all | solution.py:23
  75.3 21.9 %all-to-all-done.3 = bf16[16,48,256]{2,1,0:T(8,128)(2,1)S(1)} async-done(((bf16[16,48,256]{2,1,0:T(8,128)(2,1)}), bf16[16,48,256]{2,1,0:T(8,128)(2,1)S(1)}, u32[]{:S(2)}, u32[]{:S(2)}) %all-to-all-start.3) | async-done | bytes 393248 | tf_op jit(solution)/shard_map/all_to_all | solution.py:23
  97.3 6.3 %all-to-all-start.1 = ((f32[16,24,128]{2,1,0:T(8,128)}), f32[16,24,128]{2,1,0:T(8,128)S(1)}, u32[]{:S(2)}, u32[]{:S(2)}) async-start(f32[16,24,128]{2,1,0:T(8,128)} %bitcast.4), calls=%async_computation.1 | async-start | bytes 393216 | tf_op jit(solution)/shard_map/all_to_all | solution.py:23
  105.7 13.8 %all-to-all-done.1 = f32[16,24,128]{2,1,0:T(8,128)S(1)} async-done(((f32[16,24,128]{2,1,0:T(8,128)}), f32[16,24,128]{2,1,0:T(8,128)S(1)}, u32[]{:S(2)}, u32[]{:S(2)}) %all-to-all-start.1) | async-done | bytes 196640 | tf_op jit(solution)/shard_map/all_to_all | solution.py:23
  120.2 4.7 %all-to-all-start.2 = ((bf16[16,24,128]{2,1,0:T(8,128)(2,1)}), bf16[16,24,128]{2,1,0:T(8,128)(2,1)S(1)}, u32[]{:S(2)}, u32[]{:S(2)}) async-start(bf16[16,24,128]{2,1,0:T(8,128)(2,1)} %broadcast_in_dim.32), calls=%async_computation.2 | async-start | bytes 196608 | tf_op jit(solution)/shard_map/all_to_all | solution.py:23
  125.0 13.1 %all-to-all-done.2 = bf16[16,24,128]{2,1,0:T(8,128)(2,1)S(1)} async-done(((bf16[16,24,128]{2,1,0:T(8,128)(2,1)}), bf16[16,24,128]{2,1,0:T(8,128)(2,1)S(1)}, u32[]{:S(2)}, u32[]{:S(2)}) %all-to-all-start.2) | async-done | bytes 98336 | tf_op jit(solution)/shard_map/all_to_all | solution.py:23
  140.3 6.9 %all-to-all-start.4 = ((bf16[16,56,512]{2,1,0:T(8,128)(2,1)}), bf16[16,56,512]{2,1,0:T(8,128)(2,1)S(1)}, u32[]{:S(2)}, u32[]{:S(2)}) async-start(bf16[16,56,512]{2,1,0:T(8,128)(2,1)} %broadcast_in_dim.34), calls=%async_computation.4 | async-start | bytes 1835008 | tf_op jit(solution)/shard_map/all_to_all | solution.py:23
  149.6 9.2 %psum.14 = s32[224]{0:T(256)S(1)} all-reduce(s32[224]{0:T(256)S(1)} %dynamic_update_slice.6), channel_id=1, replica_groups=mesh['z'=16,'x'=4,'y'=4,'c'=2] {'y'}, use_global_device_ids=true, to_apply=%region_0.0 | all-reduce | flops 224 | bytes 1792 | tf_op jit(solution)/shard_map/psum | solution.py:118
  159.0 8.2 %psum.15 = s32[896]{0:T(1024)S(1)} all-reduce(s32[896]{0:T(1024)S(1)} %dynamic_update_slice.7), channel_id=1, replica_groups=mesh['z'=16,'x'=4,'y'=4,'c'=2] {'x'}, use_global_device_ids=true, to_apply=%region_1.0 | all-reduce | flops 896 | bytes 7168 | tf_op jit(solution)/shard_map/psum | solution.py:120
  169.3 6.4 %all-to-all-start.6 = ((bf16[16,56,512]{2,1,0:T(8,128)(2,1)}), bf16[16,56,512]{2,1,0:T(8,128)(2,1)S(1)}, u32[]{:S(2)}, u32[]{:S(2)}) async-start(bf16[16,56,512]{2,1,0:T(8,128)(2,1)} %bitcast.15), calls=%async_computation.6 | async-start | bytes 1835008 | tf_op jit(solution)/shard_map/all_to_all | solution.py:23
  175.7 8.0 %fusion.6 = (f32[896]{0:T(1024)S(1)}, f32[896]{0:T(1024)S(1)}, f32[896]{0:T(1024)S(1)}, f32[896]{0:T(1024)S(1)}, f32[896]{0:T(1024)S(1)}, /*index=5*/bf16[896,1024]{1,0:T(8,128)(2,1)}) fusion(s32[1024]{0:T(1024)S(1)} %pad_add_fusion, s32[896]{0:T(1024)S(1)} %psum.15, bf16[896,512]{1,0:T(8,128)(2,1)S(1)} %bitcast.47, bf16[512,512]{1,0:T(8,128)(2,1)} %copy-done.10, ...), kind=kOutput, calls=%fused_computation.13 | convolution fusion | flops 966389376 | bytes 3826688 | tf_op jit(solution)/shard_map/dot_general | solution.py:156
  188.3 7.2 %all-to-all-start.5 = ((bf16[16,64,512]{2,1,0:T(8,128)(2,1)}), bf16[16,64,512]{2,1,0:T(8,128)(2,1)S(1)}, u32[]{:S(2)}, u32[]{:S(2)}) async-start(bf16[16,64,512]{2,1,0:T(8,128)(2,1)} %pad_maximum_fusion.3), calls=%async_computation.5 | async-start | bytes 2097152 | tf_op jit(solution)/shard_map/all_to_all | solution.py:23
  196.2 10.8 %all-to-all-done.5 = bf16[16,64,512]{2,1,0:T(8,128)(2,1)S(1)} async-done(((bf16[16,64,512]{2,1,0:T(8,128)(2,1)}), bf16[16,64,512]{2,1,0:T(8,128)(2,1)S(1)}, u32[]{:S(2)}, u32[]{:S(2)}) %all-to-all-start.5) | async-done | bytes 1048608 | tf_op jit(solution)/shard_map/all_to_all | solution.py:23
  208.6 3.8 %all-to-all-start.7 = ((bf16[16,52,128]{2,1,0:T(8,128)(2,1)}), bf16[16,52,128]{2,1,0:T(8,128)(2,1)S(1)}, u32[]{:S(2)}, u32[]{:S(2)}) async-start(bf16[16,52,128]{2,1,0:T(8,128)(2,1)} %pad_maximum_fusion.6), calls=%async_computation.7 | async-start | bytes 458752 | tf_op jit(solution)/shard_map/all_to_all | solution.py:23
  216.2 9.9 %all-to-all-done.7 = bf16[16,52,128]{2,1,0:T(8,128)(2,1)S(1)} async-done(((bf16[16,52,128]{2,1,0:T(8,128)(2,1)}), bf16[16,52,128]{2,1,0:T(8,128)(2,1)S(1)}, u32[]{:S(2)}, u32[]{:S(2)}) %all-to-all-start.7) | async-done | bytes 213024 | tf_op jit(solution)/shard_map/all_to_all | solution.py:23
  (126 shorter events, 48.4 us)
Async XLA Ops:
  0.6 54.4 %copy-start = (bf16[48,512]{1,0:T(8,128)(2,1)S(1)}, bf16[48,512]{1,0:T(8,128)(2,1)}, u32[]{:S(2)}) copy-start(bf16[48,512]{1,0:T(8,128)(2,1)} %param.7) | copy-start | bytes 147460
  0.6 103.0 %copy-start.2 = (bf16[512,512]{1,0:T(8,128)(2,1)S(1)}, bf16[512,512]{1,0:T(8,128)(2,1)}, u32[]{:S(2)}) copy-start(bf16[512,512]{1,0:T(8,128)(2,1)} %centres.1) | copy-start | bytes 1572868
  0.7 8.6 %collective-permute-start.3 = (bf16[24,3840]{1,0:T(8,128)(2,1)}, bf16[24,3840]{1,0:T(8,128)(2,1)S(1)}, u32[]{:S(2)}, u32[]{:S(2)}) collective-permute-start(bf16[24,3840]{1,0:T(8,128)(2,1)} %bitcast.61), channel_id=1, source_target_pairs={{0,2},{2,0},{4,6},{6,4},{1,3},{3,1},{5,7},{7,5},{8,10},{10,8},{12,... | collective-permute-start | bytes 552968 | tf_op jit(solution)/shard_map/ppermute | solution.py:108
  10.2 12.6 %collective-permute-start.4 = (bf16[48,3840]{1,0:T(8,128)(2,1)S(1)}, bf16[48,3840]{1,0:T(8,128)(2,1)S(1)}, u32[]{:S(2)}, u32[]{:S(2)}) collective-permute-start(bf16[48,3840]{1,0:T(8,128)(2,1)S(1)} %pad_maximum_fusion.5), channel_id=1, source_target_pairs={{0,6},{6,0},{2,4},{4,2},{1,7},{7,1},{3,5},{5,3},{8,14},{14,8},{10,... | collective-permute-start | bytes 1105928 | tf_op jit(solution)/shard_map/ppermute | solution.py:109
  15.2 13.4 %collective-permute-start = (bf16[56,3840]{1,0:T(8,128)(2,1)}, bf16[56,3840]{1,0:T(8,128)(2,1)S(1)}, u32[]{:S(2)}, u32[]{:S(2)}) collective-permute-start(bf16[56,3840]{1,0:T(8,128)(2,1)} %mine.1), channel_id=1, source_target_pairs={{0,8},{8,16},{16,24},{24,0},{1,9},{9,17},{17,25},{25,1},{2,10},{10... | collective-permute-start | bytes 1290248 | tf_op jit(solution)/shard_map/ppermute | solution.py:35
  23.8 18.7 %copy-start.3 = (bf16[96,3840]{1,0:T(8,128)(2,1)}, bf16[96,3840]{1,0:T(8,128)(2,1)S(1)}, u32[]{:S(2)}) copy-start(bf16[96,3840]{1,0:T(8,128)(2,1)S(1)} %pad_maximum_fusion.4.own_cols) | copy-start | bytes 2211844
  23.9 18.7 %collective-permute-start.5 = (bf16[96,3840]{1,0:T(8,128)(2,1)S(1)}, bf16[96,3840]{1,0:T(8,128)(2,1)S(1)}, u32[]{:S(2)}, u32[]{:S(2)}) collective-permute-start(bf16[96,3840]{1,0:T(8,128)(2,1)S(1)} %pad_maximum_fusion.4.own_cols), channel_id=1, source_target_pairs={{0,1},{1,0},{2,3},{3,2},{4,5},{5,4},{6,7},{7,6},{8,9},{9,8},{10,11... | collective-permute-start | bytes 2211848 | tf_op jit(solution)/shard_map/ppermute | solution.py:31
  25.8 15.6 %collective-permute-start.1 = (bf16[56,3840]{1,0:T(8,128)(2,1)}, bf16[56,3840]{1,0:T(8,128)(2,1)S(1)}, u32[]{:S(2)}, u32[]{:S(2)}) collective-permute-start(bf16[56,3840]{1,0:T(8,128)(2,1)} %mine.1), channel_id=1, source_target_pairs={{0,24},{8,0},{16,8},{24,16},{1,25},{9,1},{17,9},{25,17},{2,26},{10... | collective-permute-start | bytes 1290248 | tf_op jit(solution)/shard_map/ppermute | solution.py:35
  28.5 14.0 %copy-start.8 = (bf16[56,3840]{1,0:T(8,128)(2,1)}, bf16[56,3840]{1,0:T(8,128)(2,1)S(1)}, u32[]{:S(2)}) copy-start(bf16[56,3840]{1,0:T(8,128)(2,1)S(1)} %collective-permute-done.left) | copy-start | bytes 1290244
  28.6 14.0 %collective-permute-start.2 = (bf16[56,3840]{1,0:T(8,128)(2,1)S(1)}, bf16[56,3840]{1,0:T(8,128)(2,1)}, u32[]{:S(2)}, u32[]{:S(2)}) collective-permute-start(bf16[56,3840]{1,0:T(8,128)(2,1)S(1)} %collective-permute-done.left), channel_id=1, source_target_pairs={{0,8},{8,16},{16,24},{24,0},{1,9},{9,17},{17,25},{25,1},{2,10},{10... | collective-permute-start | bytes 1290248 | tf_op jit(solution)/shard_map/ppermute | solution.py:35
  47.4 11.9 %all-to-all-start = ((f32[4,4,24,128]{3,2,1,0:T(8,128)}), f32[4,4,24,128]{3,2,1,0:T(8,128)}, u32[]{:S(2)}, u32[]{:S(2)}) async-start(f32[4,4,24,128]{3,2,1,0:T(8,128)} %shard_map.68), calls=%async_computation | async-start | bytes 393216 | tf_op jit(solution)/shard_map/all_to_all | solution.py:23
  60.2 37.1 %all-to-all-start.3 = ((bf16[16,48,256]{2,1,0:T(8,128)(2,1)}), bf16[16,48,256]{2,1,0:T(8,128)(2,1)S(1)}, u32[]{:S(2)}, u32[]{:S(2)}) async-start(bf16[16,48,256]{2,1,0:T(8,128)(2,1)} %broadcast_in_dim.33), calls=%async_computation.3 | async-start | bytes 786432 | tf_op jit(solution)/shard_map/all_to_all | solution.py:23
  97.3 22.3 %all-to-all-start.1 = ((f32[16,24,128]{2,1,0:T(8,128)}), f32[16,24,128]{2,1,0:T(8,128)S(1)}, u32[]{:S(2)}, u32[]{:S(2)}) async-start(f32[16,24,128]{2,1,0:T(8,128)} %bitcast.4), calls=%async_computation.1 | async-start | bytes 393216 | tf_op jit(solution)/shard_map/all_to_all | solution.py:23
  103.8 21.2 %collective-permute-start.7 = (bf16[16,48,256]{2,1,0:T(8,128)(2,1)S(1)}, bf16[16,48,256]{2,1,0:T(8,128)(2,1)S(1)}, u32[]{:S(2)}, u32[]{:S(2)}) collective-permute-start(bf16[16,48,256]{2,1,0:T(8,128)(2,1)S(1)} %all-to-all-done.3), channel_id=1, source_target_pairs={{0,1},{1,0},{2,3},{3,2},{4,5},{5,4},{6,7},{7,6},{8,9},{9,8},{10,11... | collective-permute-start | bytes 1179656 | tf_op jit(solution)/shard_map/ppermute | solution.py:31
  120.2 17.9 %all-to-all-start.2 = ((bf16[16,24,128]{2,1,0:T(8,128)(2,1)}), bf16[16,24,128]{2,1,0:T(8,128)(2,1)S(1)}, u32[]{:S(2)}, u32[]{:S(2)}) async-start(bf16[16,24,128]{2,1,0:T(8,128)(2,1)} %broadcast_in_dim.32), calls=%async_computation.2 | async-start | bytes 196608 | tf_op jit(solution)/shard_map/all_to_all | solution.py:23
  124.9 24.4 %copy-start.13 = (s32[56]{0:T(128)S(1)}, s32[56]{0:T(128)}, u32[]{:S(2)}) copy-start(s32[56]{0:T(128)} %param.9) | copy-start | bytes 676
  140.3 29.0 %all-to-all-start.4 = ((bf16[16,56,512]{2,1,0:T(8,128)(2,1)}), bf16[16,56,512]{2,1,0:T(8,128)(2,1)S(1)}, u32[]{:S(2)}, u32[]{:S(2)}) async-start(bf16[16,56,512]{2,1,0:T(8,128)(2,1)} %broadcast_in_dim.34), calls=%async_computation.4 | async-start | bytes 1835008 | tf_op jit(solution)/shard_map/all_to_all | solution.py:23
  147.4 37.2 %copy-start.6 = (bf16[512,512]{1,0:T(8,128)(2,1)}, bf16[512,512]{1,0:T(8,128)(2,1)S(1)}, u32[]{:S(2)}) copy-start(bf16[512,512]{1,0:T(8,128)(2,1)S(1)} %fusion.21) | copy-start | bytes 1572868
  147.4 19.8 %collective-permute-start.6 = (bf16[512,512]{1,0:T(8,128)(2,1)S(1)}, bf16[512,512]{1,0:T(8,128)(2,1)S(1)}, u32[]{:S(2)}, u32[]{:S(2)}) collective-permute-start(bf16[512,512]{1,0:T(8,128)(2,1)S(1)} %fusion.21), channel_id=1, source_target_pairs={{0,1},{1,0},{2,3},{3,2},{4,5},{5,4},{6,7},{7,6},{8,9},{9,8},{10,11... | collective-permute-start | bytes 1572872 | tf_op jit(solution)/shard_map/ppermute | solution.py:31
  169.3 19.1 %all-to-all-start.6 = ((bf16[16,56,512]{2,1,0:T(8,128)(2,1)}), bf16[16,56,512]{2,1,0:T(8,128)(2,1)S(1)}, u32[]{:S(2)}, u32[]{:S(2)}) async-start(bf16[16,56,512]{2,1,0:T(8,128)(2,1)} %bitcast.15), calls=%async_computation.6 | async-start | bytes 1835008 | tf_op jit(solution)/shard_map/all_to_all | solution.py:23
  188.3 18.7 %all-to-all-start.5 = ((bf16[16,64,512]{2,1,0:T(8,128)(2,1)}), bf16[16,64,512]{2,1,0:T(8,128)(2,1)S(1)}, u32[]{:S(2)}, u32[]{:S(2)}) async-start(bf16[16,64,512]{2,1,0:T(8,128)(2,1)} %pad_maximum_fusion.3), calls=%async_computation.5 | async-start | bytes 2097152 | tf_op jit(solution)/shard_map/all_to_all | solution.py:23
  195.7 17.0 %copy-start.7 = (bf16[512,512]{1,0:T(8,128)(2,1)S(1)}, bf16[512,512]{1,0:T(8,128)(2,1)}, u32[]{:S(2)}) copy-start(bf16[512,512]{1,0:T(8,128)(2,1)} %copy-done.6) | copy-start | bytes 1572868
  208.6 17.5 %all-to-all-start.7 = ((bf16[16,52,128]{2,1,0:T(8,128)(2,1)}), bf16[16,52,128]{2,1,0:T(8,128)(2,1)S(1)}, u32[]{:S(2)}, u32[]{:S(2)}) async-start(bf16[16,52,128]{2,1,0:T(8,128)(2,1)} %pad_maximum_fusion.6), calls=%async_computation.7 | async-start | bytes 458752 | tf_op jit(solution)/shard_map/all_to_all | solution.py:23
  230.6 6.4 %collective-permute-start.8 = (f32[512,512]{1,0:T(8,128)}, f32[512,512]{1,0:T(8,128)S(1)}, u32[]{:S(2)}, u32[]{:S(2)}) collective-permute-start(f32[512,512]{1,0:T(8,128)} %fusion.11), channel_id=1, source_target_pairs={{0,1},{1,0},{2,3},{3,2},{4,5},{5,4},{6,7},{7,6},{8,9},{9,8},{10,11... | collective-permute-start | bytes 3145736 | tf_op jit(solution)/shard_map/ppermute | solution.py:31
  (7 other events, 21.6 us)

commit v5 on v4

--- a/solution.py
+++ b/solution.py
@@ -68,24 +68,39 @@
     )(seat, *blocks, own_cols, other_cols)
 
 
-def centre_kernel(centres, own, received, out):
+def partner_kernel(joined, scaled, out):
+    out[...] = jnp.dot(joined[...], scaled[...], preferred_element_type=f32)
+
+
+def centre_kernel(joined, scaled, centres, received, out, held, arrived):
+    size = out.shape[0]
+    copy = pltpu.make_async_copy(received, held, arrived)
+    pl.when(pl.program_id(0) == 0)(copy.start)
     wide = centres[...].astype(f32)
     cinv = lax.rsqrt(jnp.sum(wide * wide, axis=1, keepdims=True) + norm_eps)
     unit_centre = wide * cinv
-    gunit = own[...] + received[...]
+    gunit = jnp.dot(joined[...], scaled[...], preferred_element_type=f32)
+    pl.when(pl.program_id(0) == 0)(copy.wait)
+    gunit = gunit + held[pl.ds(pl.multiple_of(pl.program_id(0) * size, size), size), :]
     out[...] = cinv * (gunit - unit_centre * jnp.sum(unit_centre * gunit, axis=1, keepdims=True))
 
 
-def centre_gradient(centres, own, received):
-    rows, emb = centres.shape
-    block = pl.BlockSpec(memory_space=pltpu.VMEM)
+STEPS = 4
+
+
+def over_centres(kernel, first, joined, scaled, *rest):
+    rows, emb = joined.shape[0] // NC, scaled.shape[1]
+    whole = pl.BlockSpec(memory_space=pltpu.VMEM)
+    block = pl.BlockSpec((rows // STEPS, emb), lambda i: (i, 0))
     return pl.pallas_call(
-        centre_kernel,
+        kernel,
         out_shape=jax.ShapeDtypeStruct((rows, emb), f32),
-        in_specs=[block] * 3,
+        grid=(STEPS,),
+        in_specs=[pl.BlockSpec((rows // STEPS, joined.shape[1]), lambda i: (i + first, 0)), whole] + [block, pl.BlockSpec(memory_space=pl.ANY)][: len(rest)],
         out_specs=block,
-        cost_estimate=pl.CostEstimate(flops=3_000_000, bytes_accessed=3_700_000, transcendentals=512),
-    )(centres, own, received)
+        scratch_shapes=[pltpu.VMEM((rows, emb), f32), pltpu.SemaphoreType.DMA][: len(rest)],
+        cost_estimate=pl.CostEstimate(flops=940_000_000, bytes_accessed=4_500_000, transcendentals=512),
+    )(joined, scaled, *rest)
 
 
 def split_pair(value):
@@ -111,19 +126,20 @@
     other_cols = partner(own_cols)
     seat = jnp.stack([xi, yi, ci]).astype(jnp.int32)
     part = partial_hidden(seat, (features, from_left, from_right, from_far), own_cols, other_cols, cols)
-    part = exchange(part, "x").reshape(NZ, cols, 128)
-
     part, labels = lax.optimization_barrier((part, labels))
     all_labels = lax.dynamic_update_slice_in_dim(jnp.zeros(NY * rows, jnp.int32), labels, yi * rows, 0)
     all_labels = lax.psum(all_labels, "y")
     all_labels = lax.dynamic_update_slice_in_dim(jnp.zeros(images, jnp.int32), all_labels, xi * NY * rows, 0)
     all_labels = lax.psum(all_labels, "x")
+    part = exchange(part, "x").reshape(NZ, cols, 128)
+
     all_labels = all_labels.reshape(images, 1)
     wide = centres.astype(f32)
     cinv = lax.rsqrt(jnp.sum(wide * wide, axis=1) + norm_eps)
     unit_centre = wide * cinv[:, None]
     own_low = unit_centre.astype(bf16)
-    low = jnp.concatenate([own_low, partner(own_low)], axis=0)
+    low = partner(own_low)
+    low = jnp.concatenate([own_low, low], axis=0)
     chip = ((zi * NX + xi) * NY + yi) * NC
     step = jnp.arange(cen, dtype=jnp.int32)
     position = jnp.concatenate([(chip + ci) * cen + step, (chip + 1 - ci) * cen + step])
@@ -181,7 +197,7 @@
     totals = pull[rows : rows + 4].reshape(16, 128)
     totals = totals[:tall] + totals[tall : 2 * tall]
     owned = pull[rows + 4 :].reshape(4 * emb)[:640].reshape(10, 64)
-    owned = jnp.pad(owned[:5] + owned[5:], ((0, 0), (0, 64)))
+    owned = owned[:5] + owned[5:]
 
     width = emb // NZ
 
@@ -190,7 +206,7 @@
         return block.transpose(2, 1, 0, 3).reshape(NZ, rows // 4, 4 * width)
 
     pull = pull[:rows]
-    common = jnp.concatenate(split_pair(totals) + split_pair(owned), axis=0)
+    common = jnp.concatenate(split_pair(totals) + (jnp.concatenate(split_pair(owned), axis=1),), axis=0)
     common = jnp.broadcast_to(common[None], (NZ,) + common.shape)
     pack = jnp.concatenate([by_column(pull), by_column(chosen), common], axis=1)
     pack = exchange(pack, "z")
@@ -203,7 +219,7 @@
     pull, chosen = by_row(pack[:quarter]), by_row(pack[quarter : 2 * quarter])
     common = pack[2 * quarter :]
     total = (common[:tall] + common[tall : 2 * tall]).reshape(images, 1)
-    owned = common[2 * tall : 2 * tall + 5, :rows] + common[2 * tall + 5 :, :rows]
+    owned = common[2 * tall :, :rows] + common[2 * tall :, 64 : 64 + rows]
     own_rest, own_hit, own_cos, own_slope, own_turn = (owned[k] for k in range(5))
 
     cosine_t = lax.dot_general(low, units, (((1,), (1,)), ((), ())), preferred_element_type=f32)
@@ -215,11 +231,8 @@
     aimed = (units.astype(f32) * weight).astype(bf16)
     scaled = lax.optimization_barrier(jnp.concatenate([scaled, aimed], axis=0))
 
-    def gradient_of(part):
-        return jnp.dot(joined[part], scaled, preferred_element_type=f32)
-
-    received = partner(gradient_of(slice(cen, None)))
-    centre_grad = centre_gradient(centres, gradient_of(slice(0, cen)), received)
+    received = partner(over_centres(partner_kernel, STEPS, joined, scaled))
+    centre_grad = over_centres(centre_kernel, 0, joined, scaled, centres, received)
 
     own_scale = scale_logit / (own_rest + own_hit)
     dunit = own_scale[:, None] * (pull - (own_rest * own_slope)[:, None] * chosen)

time: 246 us -> 249 us (1.012)
  blocking collectives: 17.4 us -> 54.3 us
  waiting for transfers between devices: 91.8 us -> 70.5 us
  starting transfers between devices: 85.3 us -> 70.1 us
  Pallas kernels: 7.01 us -> 15.9 us
  matrix products: 20.7 us -> 13.9 us
  other arithmetic: 8.55 us -> 11.2 us
    all_to_all x0 -> x1, blocking collectives: none -> 36.9 us  [exchange(): return lax.all_to_all(blocks, axis, 0, 0)]
    all_to_all x8 -> x7, waiting for transfers between devices: 73.9 us -> 51.7 us  [exchange(): return lax.all_to_all(blocks, axis, 0, 0)]
    all_to_all x8 -> x7, starting transfers between devices: 58.1 us -> 42.9 us  [exchange(): return lax.all_to_all(blocks, axis, 0, 0)]
    pallas_call x1 -> x2, Pallas kernels: 3.05 us -> 12 us  [over_centres(): pl.pallas_call(kernel, out_shape=jax.ShapeDtypeStruct((rows, emb), f32),...]
    dot_general x2 -> x0, matrix products: 5.77 us -> none  [gradient_of(): return jnp.dot(joined[part], scaled, preferred_element_type=f32)]
  transfers between devices with their start and end apart: 17 -> 16, of which waited for: 10 -> 10; matrix products, arithmetic and copies ran while one was open for 11% -> 9% of each run, Pallas kernels for 0% -> 0%
where the time goes in v5:
time: 249 us; the launch traced here: 245 us
  waiting for transfers between devices  70.5 us (28%)
  starting transfers between devices  70.1 us (28%)
  blocking collectives  54.3 us (22%)
  Pallas kernels  15.9 us (6%)
  matrix products  13.9 us (6%)
  other arithmetic  11.2 us (4%)
  local copies, waits for them, and re-layouts  7.37 us (3%)
    all_to_all x7, waiting for transfers between devices, exchange(): return lax.all_to_all(blocks, axis, 0, 0)  51.7 us
    all_to_all x7, starting transfers between devices, exchange(): return lax.all_to_all(blocks, axis, 0, 0)  42.9 us
    all_to_all x1, blocking collectives, exchange(): return lax.all_to_all(blocks, axis, 0, 0)  36.9 us
    pallas_call x2, Pallas kernels, over_centres(): pl.pallas_call(kernel, out_shape=jax.ShapeDtypeStruct((rows, emb), f32),...  12 us
    ppermute x3, starting transfers between devices, shift(): return lax.ppermute(block, axis, [(i, (i + by) % 4) for i in range(4)])  10.9 us
    psum x1, blocking collectives, step_of(): all_labels = lax.psum(all_labels, 'y')  9.22 us
    ppermute x3, waiting for transfers between devices, shift(): return lax.ppermute(block, axis, [(i, (i + by) % 4) for i in range(4)])  8.99 us
    psum x1, blocking collectives, step_of(): all_labels = lax.psum(all_labels, 'x')  8.17 us
  transfers between devices with their start and end apart: 16, of which 10 were waited for; matrix products, arithmetic and copies ran while one was open for 9% of the time, Pallas kernels for 0%

profile of v5, /device:TPU:6, one launch (start us, length us, event | category | flops | bytes accessed | tf_op | source)
XLA Modules:
  0.0 244.8 jit_solution(5804101150357355198)
XLA Ops:
  4.3 5.0 %collective-permute-done.3 = bf16[24,3840]{1,0:T(8,128)(2,1)S(1)} collective-permute-done((bf16[24,3840]{1,0:T(8,128)(2,1)}, bf16[24,3840]{1,0:T(8,128)(2,1)S(1)}, u32[]{:S(2)}, u32[]{:S(2)}) %collective-permute-start.3) | collective-permute-done | bytes 184352 | tf_op jit(solution)/shard_map/ppermute | solution.py:123
  10.2 4.9 %collective-permute-start.4 = (bf16[48,3840]{1,0:T(8,128)(2,1)S(1)}, bf16[48,3840]{1,0:T(8,128)(2,1)S(1)}, u32[]{:S(2)}, u32[]{:S(2)}) collective-permute-start(bf16[48,3840]{1,0:T(8,128)(2,1)S(1)} %pad_maximum_fusion.5), channel_id=1, source_target_pairs={{0,6},{6,0},{2,4},{4,2},{1,7},{7,1},{3,5},{5,3},{8,14},{14,8},{10,... | collective-permute-start | bytes 1105928 | tf_op jit(solution)/shard_map/ppermute | solution.py:124
  15.2 3.9 %collective-permute-start = (bf16[56,3840]{1,0:T(8,128)(2,1)}, bf16[56,3840]{1,0:T(8,128)(2,1)S(1)}, u32[]{:S(2)}, u32[]{:S(2)}) collective-permute-start(bf16[56,3840]{1,0:T(8,128)(2,1)} %mine.1), channel_id=1, source_target_pairs={{0,8},{8,16},{16,24},{24,0},{1,9},{9,17},{17,25},{25,1},{2,10},{10... | collective-permute-start | bytes 1290248 | tf_op jit(solution)/shard_map/ppermute | solution.py:35
  19.1 3.8 %collective-permute-done.4 = bf16[48,3840]{1,0:T(8,128)(2,1)S(1)} collective-permute-done((bf16[48,3840]{1,0:T(8,128)(2,1)S(1)}, bf16[48,3840]{1,0:T(8,128)(2,1)S(1)}, u32[]{:S(2)}, u32[]{:S(2)}) %collective-permute-start.4) | collective-permute-done | bytes 368672 | tf_op jit(solution)/shard_map/ppermute | solution.py:124
  28.6 4.3 %collective-permute-start.2 = (bf16[56,3840]{1,0:T(8,128)(2,1)S(1)}, bf16[56,3840]{1,0:T(8,128)(2,1)S(1)}, u32[]{:S(2)}, u32[]{:S(2)}) collective-permute-start(bf16[56,3840]{1,0:T(8,128)(2,1)S(1)} %collective-permute-done.left), channel_id=1, source_target_pairs={{0,8},{8,16},{16,24},{24,0},{1,9},{9,17},{17,25},{25,1},{2,10},{10... | collective-permute-start | bytes 1290248 | tf_op jit(solution)/shard_map/ppermute | solution.py:35
  33.5 7.9 %collective-permute-done.1.right = bf16[56,3840]{1,0:T(8,128)(2,1)S(1)} collective-permute-done((bf16[56,3840]{1,0:T(8,128)(2,1)}, bf16[56,3840]{1,0:T(8,128)(2,1)S(1)}, u32[]{:S(2)}, u32[]{:S(2)}) %collective-permute-start.1) | collective-permute-done | bytes 430112 | tf_op jit(solution)/shard_map/ppermute | solution.py:35
  44.1 4.0 %shard_map.68 = f32[4,4,24,128]{3,2,1,0:T(8,128)} custom-call(s32[3]{0:T(128)} %pad_add_fusion.1.seat, bf16[56,3840]{1,0:T(8,128)(2,1)} %mine.1, bf16[56,3840]{1,0:T(8,128)(2,1)} %copy-done.5, bf16[56,3840]{1,0:T(8,128)(2,1)} %copy-done.6, bf16[56,3840]{1,0:T(8,128)(2,1)} %copy-done.7, bf16[96,3840]{1,0:T(8,128)(2,1)} %copy-done.2, bf16[96,3840]{1,0:T(8,128)(2,1)} %copy-done.4), custom_call_target="tpu_custom_call" | custom-call | flops 330000000 | bytes 3400000 | tf_op jit(solution)/shard_map/pallas_call | solution.py:61
  48.1 7.6 %all-to-all-start = ((f32[4,4,24,128]{3,2,1,0:T(8,128)}), f32[4,4,24,128]{3,2,1,0:T(8,128)}, u32[]{:S(2)}, u32[]{:S(2)}) async-start(f32[4,4,24,128]{3,2,1,0:T(8,128)} %shard_map.68), calls=%async_computation | async-start | bytes 393216 | tf_op jit(solution)/shard_map/all_to_all | solution.py:23
  55.7 4.4 %all-to-all-done = f32[4,4,24,128]{3,2,1,0:T(8,128)} async-done(((f32[4,4,24,128]{3,2,1,0:T(8,128)}), f32[4,4,24,128]{3,2,1,0:T(8,128)}, u32[]{:S(2)}, u32[]{:S(2)}) %all-to-all-start) | async-done | bytes 196640 | tf_op jit(solution)/shard_map/all_to_all | solution.py:23
  60.0 36.9 %all_to_all.40 = bf16[16,48,256]{2,1,0:T(8,128)(2,1)S(1)} all-to-all(bf16[16,48,256]{2,1,0:T(8,128)(2,1)S(1)} %broadcast_in_dim.33), channel_id=1, replica_groups=mesh['z'=16,'x'=4,'y'=4,'c'=2] {'z'}, dimensions={0} | all-to-all | bytes 786432 | tf_op jit(solution)/shard_map/all_to_all | solution.py:23
  97.0 6.3 %all-to-all-start.1 = ((f32[16,24,128]{2,1,0:T(8,128)}), f32[16,24,128]{2,1,0:T(8,128)S(1)}, u32[]{:S(2)}, u32[]{:S(2)}) async-start(f32[16,24,128]{2,1,0:T(8,128)} %bitcast.4), calls=%async_computation.1 | async-start | bytes 393216 | tf_op jit(solution)/shard_map/all_to_all | solution.py:23
  105.4 13.8 %all-to-all-done.1 = f32[16,24,128]{2,1,0:T(8,128)S(1)} async-done(((f32[16,24,128]{2,1,0:T(8,128)}), f32[16,24,128]{2,1,0:T(8,128)S(1)}, u32[]{:S(2)}, u32[]{:S(2)}) %all-to-all-start.1) | async-done | bytes 196640 | tf_op jit(solution)/shard_map/all_to_all | solution.py:23
  119.9 4.7 %all-to-all-start.2 = ((bf16[16,24,128]{2,1,0:T(8,128)(2,1)}), bf16[16,24,128]{2,1,0:T(8,128)(2,1)S(1)}, u32[]{:S(2)}, u32[]{:S(2)}) async-start(bf16[16,24,128]{2,1,0:T(8,128)(2,1)} %broadcast_in_dim.32), calls=%async_computation.2 | async-start | bytes 196608 | tf_op jit(solution)/shard_map/all_to_all | solution.py:23
  124.7 13.1 %all-to-all-done.2 = bf16[16,24,128]{2,1,0:T(8,128)(2,1)S(1)} async-done(((bf16[16,24,128]{2,1,0:T(8,128)(2,1)}), bf16[16,24,128]{2,1,0:T(8,128)(2,1)S(1)}, u32[]{:S(2)}, u32[]{:S(2)}) %all-to-all-start.2) | async-done | bytes 98336 | tf_op jit(solution)/shard_map/all_to_all | solution.py:23
  140.6 6.9 %all-to-all-start.4 = ((bf16[16,56,512]{2,1,0:T(8,128)(2,1)}), bf16[16,56,512]{2,1,0:T(8,128)(2,1)S(1)}, u32[]{:S(2)}, u32[]{:S(2)}) async-start(bf16[16,56,512]{2,1,0:T(8,128)(2,1)} %broadcast_in_dim.34), calls=%async_computation.4 | async-start | bytes 1835008 | tf_op jit(solution)/shard_map/all_to_all | solution.py:23
  149.9 9.2 %psum.14 = s32[224]{0:T(256)S(1)} all-reduce(s32[224]{0:T(256)S(1)} %dynamic_update_slice.6), channel_id=1, replica_groups=mesh['z'=16,'x'=4,'y'=4,'c'=2] {'y'}, use_global_device_ids=true, to_apply=%region_0.0 | all-reduce | flops 224 | bytes 1792 | tf_op jit(solution)/shard_map/psum | solution.py:131
  159.3 8.2 %psum.15 = s32[896]{0:T(1024)S(1)} all-reduce(s32[896]{0:T(1024)S(1)} %dynamic_update_slice.7), channel_id=1, replica_groups=mesh['z'=16,'x'=4,'y'=4,'c'=2] {'x'}, use_global_device_ids=true, to_apply=%region_1.0 | all-reduce | flops 896 | bytes 7168 | tf_op jit(solution)/shard_map/psum | solution.py:133
  169.6 6.4 %all-to-all-start.6 = ((bf16[16,56,512]{2,1,0:T(8,128)(2,1)}), bf16[16,56,512]{2,1,0:T(8,128)(2,1)S(1)}, u32[]{:S(2)}, u32[]{:S(2)}) async-start(bf16[16,56,512]{2,1,0:T(8,128)(2,1)} %bitcast.15), calls=%async_computation.6 | async-start | bytes 1835008 | tf_op jit(solution)/shard_map/all_to_all | solution.py:23
  176.1 6.9 %fusion.6 = (f32[896]{0:T(1024)S(1)}, f32[896]{0:T(1024)S(1)}, f32[896]{0:T(1024)S(1)}, f32[896]{0:T(1024)S(1)}, f32[896]{0:T(1024)S(1)}, /*index=5*/bf16[896,1024]{1,0:T(8,128)(2,1)}) fusion(s32[1024]{0:T(1024)S(1)} %pad_add_fusion, s32[896]{0:T(1024)S(1)} %psum.15, bf16[896,512]{1,0:T(8,128)(2,1)S(1)} %bitcast.45, ...), kind=kOutput, calls=%fused_computation.13 | convolution fusion | flops 966389376 | bytes 3826688 | tf_op jit(solution)/shard_map/dot_general | solution.py:172
  187.6 7.2 %all-to-all-start.5 = ((bf16[16,64,512]{2,1,0:T(8,128)(2,1)}), bf16[16,64,512]{2,1,0:T(8,128)(2,1)S(1)}, u32[]{:S(2)}, u32[]{:S(2)}) async-start(bf16[16,64,512]{2,1,0:T(8,128)(2,1)} %pad_maximum_fusion.3), calls=%async_computation.5 | async-start | bytes 2097152 | tf_op jit(solution)/shard_map/all_to_all | solution.py:23
  195.4 10.8 %all-to-all-done.5 = bf16[16,64,512]{2,1,0:T(8,128)(2,1)S(1)} async-done(((bf16[16,64,512]{2,1,0:T(8,128)(2,1)}), bf16[16,64,512]{2,1,0:T(8,128)(2,1)S(1)}, u32[]{:S(2)}, u32[]{:S(2)}) %all-to-all-start.5) | async-done | bytes 1048608 | tf_op jit(solution)/shard_map/all_to_all | solution.py:23
  215.4 9.6 %all-to-all-done.7 = bf16[16,47,128]{2,1,0:T(8,128)(2,1)S(1)} async-done(((bf16[16,47,128]{2,1,0:T(8,128)(2,1)}), bf16[16,47,128]{2,1,0:T(8,128)(2,1)S(1)}, u32[]{:S(2)}, u32[]{:S(2)}) %all-to-all-start.7) | async-done | bytes 192544 | tf_op jit(solution)/shard_map/all_to_all | solution.py:23
  226.9 4.9 %shard_map.69 = f32[512,512]{1,0:T(8,128)} custom-call(bf16[1024,1792]{1,0:T(8,128)(2,1)} %pad_maximum_fusion.joined, bf16[1792,512]{1,0:T(8,128)(2,1)} %pad_maximum_fusion.1.scaled), custom_call_target="tpu_custom_call" | custom-call | flops 940000000 | bytes 4500000 | tf_op jit(solution)/shard_map/pallas_call | solution.py:95
  237.5 7.0 %shard_map.70 = f32[512,512]{1,0:T(8,128)} custom-call(bf16[1024,1792]{1,0:T(8,128)(2,1)} %pad_maximum_fusion.joined, bf16[1792,512]{1,0:T(8,128)(2,1)} %pad_maximum_fusion.1.scaled, bf16[512,512]{1,0:T(8,128)(2,1)} %centres.1, f32[512,512]{1,0:T(8,128)} %copy-done.3), custom_call_target="tpu_custom_call" | custom-call | flops 940000000 | bytes 4500000 | tf_op jit(solution)/shard_map/pallas_call | solution.py:95
  (117 shorter events, 45.4 us)
Async XLA Ops:
  0.6 55.0 %copy-start = (bf16[48,512]{1,0:T(8,128)(2,1)S(1)}, bf16[48,512]{1,0:T(8,128)(2,1)}, u32[]{:S(2)}) copy-start(bf16[48,512]{1,0:T(8,128)(2,1)} %param.7) | copy-start | bytes 147460
  0.6 102.6 %copy-start.1 = (bf16[512,512]{1,0:T(8,128)(2,1)S(1)}, bf16[512,512]{1,0:T(8,128)(2,1)}, u32[]{:S(2)}) copy-start(bf16[512,512]{1,0:T(8,128)(2,1)} %centres.1) | copy-start | bytes 1572868
  0.7 8.6 %collective-permute-start.3 = (bf16[24,3840]{1,0:T(8,128)(2,1)}, bf16[24,3840]{1,0:T(8,128)(2,1)S(1)}, u32[]{:S(2)}, u32[]{:S(2)}) collective-permute-start(bf16[24,3840]{1,0:T(8,128)(2,1)} %bitcast.59), channel_id=1, source_target_pairs={{0,2},{2,0},{4,6},{6,4},{1,3},{3,1},{5,7},{7,5},{8,10},{10,8},{12,... | collective-permute-start | bytes 552968 | tf_op jit(solution)/shard_map/ppermute | solution.py:123
  10.2 12.6 %collective-permute-start.4 = (bf16[48,3840]{1,0:T(8,128)(2,1)S(1)}, bf16[48,3840]{1,0:T(8,128)(2,1)S(1)}, u32[]{:S(2)}, u32[]{:S(2)}) collective-permute-start(bf16[48,3840]{1,0:T(8,128)(2,1)S(1)} %pad_maximum_fusion.5), channel_id=1, source_target_pairs={{0,6},{6,0},{2,4},{4,2},{1,7},{7,1},{3,5},{5,3},{8,14},{14,8},{10,... | collective-permute-start | bytes 1105928 | tf_op jit(solution)/shard_map/ppermute | solution.py:124
  15.2 13.4 %collective-permute-start = (bf16[56,3840]{1,0:T(8,128)(2,1)}, bf16[56,3840]{1,0:T(8,128)(2,1)S(1)}, u32[]{:S(2)}, u32[]{:S(2)}) collective-permute-start(bf16[56,3840]{1,0:T(8,128)(2,1)} %mine.1), channel_id=1, source_target_pairs={{0,8},{8,16},{16,24},{24,0},{1,9},{9,17},{17,25},{25,1},{2,10},{10... | collective-permute-start | bytes 1290248 | tf_op jit(solution)/shard_map/ppermute | solution.py:35
  23.8 18.6 %copy-start.2 = (bf16[96,3840]{1,0:T(8,128)(2,1)}, bf16[96,3840]{1,0:T(8,128)(2,1)S(1)}, u32[]{:S(2)}) copy-start(bf16[96,3840]{1,0:T(8,128)(2,1)S(1)} %pad_maximum_fusion.4.own_cols) | copy-start | bytes 2211844
  23.9 18.6 %collective-permute-start.5 = (bf16[96,3840]{1,0:T(8,128)(2,1)S(1)}, bf16[96,3840]{1,0:T(8,128)(2,1)S(1)}, u32[]{:S(2)}, u32[]{:S(2)}) collective-permute-start(bf16[96,3840]{1,0:T(8,128)(2,1)S(1)} %pad_maximum_fusion.4.own_cols), channel_id=1, source_target_pairs={{0,1},{1,0},{2,3},{3,2},{4,5},{5,4},{6,7},{7,6},{8,9},{9,8},{10,11... | collective-permute-start | bytes 2211848 | tf_op jit(solution)/shard_map/ppermute | solution.py:31
  25.8 15.6 %collective-permute-start.1 = (bf16[56,3840]{1,0:T(8,128)(2,1)}, bf16[56,3840]{1,0:T(8,128)(2,1)S(1)}, u32[]{:S(2)}, u32[]{:S(2)}) collective-permute-start(bf16[56,3840]{1,0:T(8,128)(2,1)} %mine.1), channel_id=1, source_target_pairs={{0,24},{8,0},{16,8},{24,16},{1,25},{9,1},{17,9},{25,17},{2,26},{10... | collective-permute-start | bytes 1290248 | tf_op jit(solution)/shard_map/ppermute | solution.py:35
  28.5 13.9 %copy-start.5 = (bf16[56,3840]{1,0:T(8,128)(2,1)}, bf16[56,3840]{1,0:T(8,128)(2,1)S(1)}, u32[]{:S(2)}) copy-start(bf16[56,3840]{1,0:T(8,128)(2,1)S(1)} %collective-permute-done.left) | copy-start | bytes 1290244
  28.6 13.9 %collective-permute-start.2 = (bf16[56,3840]{1,0:T(8,128)(2,1)S(1)}, bf16[56,3840]{1,0:T(8,128)(2,1)S(1)}, u32[]{:S(2)}, u32[]{:S(2)}) collective-permute-start(bf16[56,3840]{1,0:T(8,128)(2,1)S(1)} %collective-permute-done.left), channel_id=1, source_target_pairs={{0,8},{8,16},{16,24},{24,0},{1,9},{9,17},{17,25},{25,1},{2,10},{10... | collective-permute-start | bytes 1290248 | tf_op jit(solution)/shard_map/ppermute | solution.py:35
  41.4 1.1 copy-start.6
  48.1 11.9 %all-to-all-start = ((f32[4,4,24,128]{3,2,1,0:T(8,128)}), f32[4,4,24,128]{3,2,1,0:T(8,128)}, u32[]{:S(2)}, u32[]{:S(2)}) async-start(f32[4,4,24,128]{3,2,1,0:T(8,128)} %shard_map.68), calls=%async_computation | async-start | bytes 393216 | tf_op jit(solution)/shard_map/all_to_all | solution.py:23
  97.0 22.3 %all-to-all-start.1 = ((f32[16,24,128]{2,1,0:T(8,128)}), f32[16,24,128]{2,1,0:T(8,128)S(1)}, u32[]{:S(2)}, u32[]{:S(2)}) async-start(f32[16,24,128]{2,1,0:T(8,128)} %bitcast.4), calls=%async_computation.1 | async-start | bytes 393216 | tf_op jit(solution)/shard_map/all_to_all | solution.py:23
  103.5 21.2 %collective-permute-start.7 = (bf16[16,48,256]{2,1,0:T(8,128)(2,1)S(1)}, bf16[16,48,256]{2,1,0:T(8,128)(2,1)S(1)}, u32[]{:S(2)}, u32[]{:S(2)}) collective-permute-start(bf16[16,48,256]{2,1,0:T(8,128)(2,1)S(1)} %all_to_all.40), channel_id=1, source_target_pairs={{0,1},{1,0},{2,3},{3,2},{4,5},{5,4},{6,7},{7,6},{8,9},{9,8},{10,11... | collective-permute-start | bytes 1179656 | tf_op jit(solution)/shard_map/ppermute | solution.py:31
  119.9 17.9 %all-to-all-start.2 = ((bf16[16,24,128]{2,1,0:T(8,128)(2,1)}), bf16[16,24,128]{2,1,0:T(8,128)(2,1)S(1)}, u32[]{:S(2)}, u32[]{:S(2)}) async-start(bf16[16,24,128]{2,1,0:T(8,128)(2,1)} %broadcast_in_dim.32), calls=%async_computation.2 | async-start | bytes 196608 | tf_op jit(solution)/shard_map/all_to_all | solution.py:23
  124.6 25.1 %copy-start.10 = (s32[56]{0:T(128)S(1)}, s32[56]{0:T(128)}, u32[]{:S(2)}) copy-start(s32[56]{0:T(128)} %param.9) | copy-start | bytes 676
  140.6 29.0 %all-to-all-start.4 = ((bf16[16,56,512]{2,1,0:T(8,128)(2,1)}), bf16[16,56,512]{2,1,0:T(8,128)(2,1)S(1)}, u32[]{:S(2)}, u32[]{:S(2)}) async-start(bf16[16,56,512]{2,1,0:T(8,128)(2,1)} %broadcast_in_dim.34), calls=%async_computation.4 | async-start | bytes 1835008 | tf_op jit(solution)/shard_map/all_to_all | solution.py:23
  147.7 19.8 %collective-permute-start.6 = (bf16[512,512]{1,0:T(8,128)(2,1)S(1)}, bf16[512,512]{1,0:T(8,128)(2,1)S(1)}, u32[]{:S(2)}, u32[]{:S(2)}) collective-permute-start(bf16[512,512]{1,0:T(8,128)(2,1)S(1)} %fusion.17), channel_id=1, source_target_pairs={{0,1},{1,0},{2,3},{3,2},{4,5},{5,4},{6,7},{7,6},{8,9},{9,8},{10,11... | collective-permute-start | bytes 1572872 | tf_op jit(solution)/shard_map/ppermute | solution.py:31
  167.5 16.3 %copy-start.8 = (bf16[512,512]{1,0:T(8,128)(2,1)}, bf16[512,512]{1,0:T(8,128)(2,1)S(1)}, u32[]{:S(2)}) copy-start(bf16[512,512]{1,0:T(8,128)(2,1)S(1)} %collective-permute-done.6) | copy-start | bytes 1572868
  169.6 18.0 %all-to-all-start.6 = ((bf16[16,56,512]{2,1,0:T(8,128)(2,1)}), bf16[16,56,512]{2,1,0:T(8,128)(2,1)S(1)}, u32[]{:S(2)}, u32[]{:S(2)}) async-start(bf16[16,56,512]{2,1,0:T(8,128)(2,1)} %bitcast.15), calls=%async_computation.6 | async-start | bytes 1835008 | tf_op jit(solution)/shard_map/all_to_all | solution.py:23
  187.6 18.7 %all-to-all-start.5 = ((bf16[16,64,512]{2,1,0:T(8,128)(2,1)}), bf16[16,64,512]{2,1,0:T(8,128)(2,1)S(1)}, u32[]{:S(2)}, u32[]{:S(2)}) async-start(bf16[16,64,512]{2,1,0:T(8,128)(2,1)} %pad_maximum_fusion.3), calls=%async_computation.5 | async-start | bytes 2097152 | tf_op jit(solution)/shard_map/all_to_all | solution.py:23
  206.4 5.6 %copy-start.9 = (bf16[512,512]{1,0:T(8,128)(2,1)S(1)}, bf16[512,512]{1,0:T(8,128)(2,1)}, u32[]{:S(2)}) copy-start(bf16[512,512]{1,0:T(8,128)(2,1)} %copy-done.8) | copy-start | bytes 1572868
  207.9 17.2 %all-to-all-start.7 = ((bf16[16,47,128]{2,1,0:T(8,128)(2,1)}), bf16[16,47,128]{2,1,0:T(8,128)(2,1)S(1)}, u32[]{:S(2)}, u32[]{:S(2)}) async-start(bf16[16,47,128]{2,1,0:T(8,128)(2,1)} %pad_maximum_fusion.6), calls=%async_computation.7 | async-start | bytes 393216 | tf_op jit(solution)/shard_map/all_to_all | solution.py:23
  231.8 4.8 %collective-permute-start.8 = (f32[512,512]{1,0:T(8,128)}, f32[512,512]{1,0:T(8,128)S(1)}, u32[]{:S(2)}, u32[]{:S(2)}) collective-permute-start(f32[512,512]{1,0:T(8,128)} %shard_map.69), channel_id=1, source_target_pairs={{0,1},{1,0},{2,3},{3,2},{4,5},{5,4},{6,7},{7,6},{8,9},{9,8},{10,11... | collective-permute-start | bytes 3145736 | tf_op jit(solution)/shard_map/ppermute | solution.py:31
  (3 other events, 2.6 us)

commit v6 on v4

--- a/solution.py
+++ b/solution.py
@@ -168,20 +168,19 @@
 
     pull = jnp.dot(lax.optimization_barrier(rest.astype(bf16)), low, preferred_element_type=f32).astype(bf16).reshape(NX * NY, rows, emb)
     tall = images // 128
-    totals = jnp.concatenate(split_pair((rest_sum + hit).reshape(tall, 128)), axis=0)
-    totals = jnp.pad(totals, ((0, 16 - 2 * tall), (0, 0))).reshape(4, emb)
-    totals = jnp.broadcast_to(totals[None], (NX * NY, 4, emb))
-    owned = jnp.stack([rest_sum, hit, rest_cos, hit_slope, hit_turn]).reshape(5, NX * NY, rows)
+    shared = jnp.concatenate([rest_sum, hit + rest_sum]).reshape(2 * tall, 128)
+    shared = jnp.concatenate(split_pair(shared), axis=0)
+    owned = jnp.stack([rest_cos, hit_slope, hit_turn]).reshape(3, NX * NY, rows)
     owned = jnp.pad(owned.transpose(1, 0, 2), ((0, 0), (0, 0), (0, 64 - rows)))
-    owned = jnp.concatenate(split_pair(owned), axis=1).reshape(NX * NY, 640)
-    owned = jnp.pad(owned, ((0, 0), (0, 4 * emb - 640))).reshape(NX * NY, 4, emb)
-    pull = jnp.concatenate([pull, totals, owned], axis=1)
+    owned = jnp.pad(jnp.concatenate(split_pair(owned), axis=2), ((0, 0), (0, 1), (0, 0)))
+    shared = jnp.broadcast_to(shared[None], (NX * NY,) + shared.shape)
+    extra = jnp.concatenate([shared, owned], axis=1).reshape(NX * NY, 8, emb)
+    pull = jnp.concatenate([pull, extra], axis=1)
     pull = exchange(pull, XY)
     pull = jnp.sum(pull.astype(f32), axis=0)
-    totals = pull[rows : rows + 4].reshape(16, 128)
-    totals = totals[:tall] + totals[tall : 2 * tall]
-    owned = pull[rows + 4 :].reshape(4 * emb)[:640].reshape(10, 64)
-    owned = jnp.pad(owned[:5] + owned[5:], ((0, 0), (0, 64)))
+    extra = pull[rows:].reshape(32, 128)
+    shared = extra[: 2 * tall] + extra[2 * tall : 4 * tall]
+    owned = extra[4 * tall : 4 * tall + 3, :64] + extra[4 * tall : 4 * tall + 3, 64:]
 
     width = emb // NZ
 
@@ -190,7 +189,7 @@
         return block.transpose(2, 1, 0, 3).reshape(NZ, rows // 4, 4 * width)
 
     pull = pull[:rows]
-    common = jnp.concatenate(split_pair(totals) + split_pair(owned), axis=0)
+    common = jnp.concatenate(split_pair(shared) + (jnp.concatenate(split_pair(owned), axis=1),), axis=0)
     common = jnp.broadcast_to(common[None], (NZ,) + common.shape)
     pack = jnp.concatenate([by_column(pull), by_column(chosen), common], axis=1)
     pack = exchange(pack, "z")
@@ -202,26 +201,26 @@
     quarter = rows // 4
     pull, chosen = by_row(pack[:quarter]), by_row(pack[quarter : 2 * quarter])
     common = pack[2 * quarter :]
-    total = (common[:tall] + common[tall : 2 * tall]).reshape(images, 1)
-    owned = common[2 * tall : 2 * tall + 5, :rows] + common[2 * tall + 5 :, :rows]
-    own_rest, own_hit, own_cos, own_slope, own_turn = (owned[k] for k in range(5))
+    shared = (common[: 2 * tall] + common[2 * tall : 4 * tall]).reshape(2, images)
+    own_rest, own_total = lax.dynamic_slice_in_dim(shared, (xi * NY + yi) * rows, rows, 1)
+    owned = common[4 * tall :, :rows] + common[4 * tall :, 64 : 64 + rows]
+    own_cos, own_slope, own_turn = (owned[k] for k in range(3))
 
     cosine_t = lax.dot_general(low, units, (((1,), (1,)), ((), ())), preferred_element_type=f32)
     target_t = position[:, None] == all_labels.reshape(1, images)
     rest_t = jnp.where(target_t, 0.0, jnp.exp(scale_logit * cosine_t)).astype(bf16)
-    joined = lax.optimization_barrier(jnp.concatenate([rest_t, target_t.astype(bf16)], axis=1))
-    weight = scale_logit * hit_slope[:, None] * (hit[:, None] / total - 1.0)
-    scaled = (units.astype(f32) * (scale_logit / total)).astype(bf16)
-    aimed = (units.astype(f32) * weight).astype(bf16)
-    scaled = lax.optimization_barrier(jnp.concatenate([scaled, aimed], axis=0))
+    rest_t = lax.optimization_barrier(rest_t)
+    scaled = (units.astype(f32) * (scale_logit / shared[1])[:, None]).astype(bf16)
+    at_target = -hit_slope * shared[0]
 
     def gradient_of(part):
-        return jnp.dot(joined[part], scaled, preferred_element_type=f32)
+        mixed = jnp.where(target_t[part], at_target[None, :], rest_t[part].astype(f32)).astype(bf16)
+        return jnp.dot(mixed, scaled, preferred_element_type=f32)
 
     received = partner(gradient_of(slice(cen, None)))
     centre_grad = centre_gradient(centres, gradient_of(slice(0, cen)), received)
 
-    own_scale = scale_logit / (own_rest + own_hit)
+    own_scale = scale_logit / own_total
     dunit = own_scale[:, None] * (pull - (own_rest * own_slope)[:, None] * chosen)
     along = own_scale * (own_cos - own_rest * own_turn)
     unit_cols = lax.dynamic_slice_in_dim(unit, zi * width, width, 1)

time: 246 us -> 250 us (1.016)
  waiting for transfers between devices: 91.8 us -> 98.7 us
    all_to_all x8, waiting for transfers between devices: 73.9 us -> 81 us  [exchange(): return lax.all_to_all(blocks, axis, 0, 0)]
  transfers between devices with their start and end apart: 17 -> 17, of which waited for: 10 -> 11; matrix products, arithmetic and copies ran while one was open for 11% -> 7% of each run, Pallas kernels for 0% -> 0%
where the time goes in v6:
time: 250 us; the launch traced here: 245 us
  waiting for transfers between devices  98.7 us (39%)
  starting transfers between devices  83.9 us (34%)
  matrix products  21.4 us (9%)
  blocking collectives  17.4 us (7%)
  other arithmetic  8.06 us (3%)
  local copies, waits for them, and re-layouts  7.78 us (3%)
  Pallas kernels  7.01 us (3%)
    all_to_all x8, waiting for transfers between devices, exchange(): return lax.all_to_all(blocks, axis, 0, 0)  81 us
    all_to_all x8, starting transfers between devices, exchange(): return lax.all_to_all(blocks, axis, 0, 0)  56.8 us
    ppermute x3, starting transfers between devices, shift(): return lax.ppermute(block, axis, [(i, (i + by) % 4) for i in range(4)])  10.9 us
    psum x1, blocking collectives, step_of(): all_labels = lax.psum(all_labels, 'y')  9.22 us
    ppermute x3, waiting for transfers between devices, shift(): return lax.ppermute(block, axis, [(i, (i + by) % 4) for i in range(4)])  8.94 us
    psum x1, blocking collectives, step_of(): all_labels = lax.psum(all_labels, 'x')  8.17 us
    ppermute x4, starting transfers between devices, partner(): return lax.ppermute(block, 'c', SWAP)  7.67 us
    dot_general x1, matrix products, step_of(): lax.dot_general(units, low, (((1,), (1,)), ((), ())), preferred_element_t...  6.9 us
  transfers between devices with their start and end apart: 17, of which 11 were waited for; matrix products, arithmetic and copies ran while one was open for 7% of the time, Pallas kernels for 0%

profile of v6, /device:TPU:6, one launch (start us, length us, event | category | flops | bytes accessed | tf_op | source)
XLA Modules:
  0.0 245.5 jit_solution(12238453666489802276)
XLA Ops:
  4.3 5.0 %collective-permute-done.3 = bf16[24,3840]{1,0:T(8,128)(2,1)S(1)} collective-permute-done((bf16[24,3840]{1,0:T(8,128)(2,1)}, bf16[24,3840]{1,0:T(8,128)(2,1)S(1)}, u32[]{:S(2)}, u32[]{:S(2)}) %collective-permute-start.3) | collective-permute-done | bytes 184352 | tf_op jit(solution)/shard_map/ppermute | solution.py:108
  10.2 4.9 %collective-permute-start.4 = (bf16[48,3840]{1,0:T(8,128)(2,1)S(1)}, bf16[48,3840]{1,0:T(8,128)(2,1)S(1)}, u32[]{:S(2)}, u32[]{:S(2)}) collective-permute-start(bf16[48,3840]{1,0:T(8,128)(2,1)S(1)} %pad_maximum_fusion.3), channel_id=1, source_target_pairs={{0,6},{6,0},{2,4},{4,2},{1,7},{7,1},{3,5},{5,3},{8,14},{14,8},{10,... | collective-permute-start | bytes 1105928 | tf_op jit(solution)/shard_map/ppermute | solution.py:109
  15.2 3.9 %collective-permute-start = (bf16[56,3840]{1,0:T(8,128)(2,1)}, bf16[56,3840]{1,0:T(8,128)(2,1)S(1)}, u32[]{:S(2)}, u32[]{:S(2)}) collective-permute-start(bf16[56,3840]{1,0:T(8,128)(2,1)} %mine.1), channel_id=1, source_target_pairs={{0,8},{8,16},{16,24},{24,0},{1,9},{9,17},{17,25},{25,1},{2,10},{10... | collective-permute-start | bytes 1290248 | tf_op jit(solution)/shard_map/ppermute | solution.py:35
  28.6 4.3 %collective-permute-start.2 = (bf16[56,3840]{1,0:T(8,128)(2,1)S(1)}, bf16[56,3840]{1,0:T(8,128)(2,1)S(1)}, u32[]{:S(2)}, u32[]{:S(2)}) collective-permute-start(bf16[56,3840]{1,0:T(8,128)(2,1)S(1)} %collective-permute-done.left), channel_id=1, source_target_pairs={{0,8},{8,16},{16,24},{24,0},{1,9},{9,17},{17,25},{25,1},{2,10},{10... | collective-permute-start | bytes 1290248 | tf_op jit(solution)/shard_map/ppermute | solution.py:35
  33.5 7.7 %collective-permute-done.1.right = bf16[56,3840]{1,0:T(8,128)(2,1)S(1)} collective-permute-done((bf16[56,3840]{1,0:T(8,128)(2,1)S(1)}, bf16[56,3840]{1,0:T(8,128)(2,1)S(1)}, u32[]{:S(2)}, u32[]{:S(2)}) %collective-permute-start.1) | collective-permute-done | bytes 430112 | tf_op jit(solution)/shard_map/ppermute | solution.py:35
  44.1 4.0 %shard_map.68 = f32[4,4,24,128]{3,2,1,0:T(8,128)} custom-call(s32[3]{0:T(128)} %pad_add_fusion.1.seat, bf16[56,3840]{1,0:T(8,128)(2,1)} %mine.1, bf16[56,3840]{1,0:T(8,128)(2,1)} %copy-done.6, bf16[56,3840]{1,0:T(8,128)(2,1)} %copy-done.7, bf16[56,3840]{1,0:T(8,128)(2,1)} %copy-done.8, bf16[96,3840]{1,0:T(8,128)(2,1)} %copy-done.2, bf16[96,3840]{1,0:T(8,128)(2,1)} %copy-done.4), custom_call_target="tpu_custom_call" | custom-call | flops 330000000 | bytes 3400000 | tf_op jit(solution)/shard_map/pallas_call | solution.py:61
  48.1 7.7 %all-to-all-start = ((f32[4,4,24,128]{3,2,1,0:T(8,128)}), f32[4,4,24,128]{3,2,1,0:T(8,128)}, u32[]{:S(2)}, u32[]{:S(2)}) async-start(f32[4,4,24,128]{3,2,1,0:T(8,128)} %shard_map.68), calls=%async_computation | async-start | bytes 393216 | tf_op jit(solution)/shard_map/all_to_all | solution.py:23
  55.8 4.4 %all-to-all-done = f32[4,4,24,128]{3,2,1,0:T(8,128)} async-done(((f32[4,4,24,128]{3,2,1,0:T(8,128)}), f32[4,4,24,128]{3,2,1,0:T(8,128)}, u32[]{:S(2)}, u32[]{:S(2)}) %all-to-all-start) | async-done | bytes 196640 | tf_op jit(solution)/shard_map/all_to_all | solution.py:23
  60.9 15.2 %all-to-all-start.3 = ((bf16[16,48,256]{2,1,0:T(8,128)(2,1)}), bf16[16,48,256]{2,1,0:T(8,128)(2,1)S(1)}, u32[]{:S(2)}, u32[]{:S(2)}) async-start(bf16[16,48,256]{2,1,0:T(8,128)(2,1)} %broadcast_in_dim.41), calls=%async_computation.3 | async-start | bytes 786432 | tf_op jit(solution)/shard_map/all_to_all | solution.py:23
  76.1 21.9 %all-to-all-done.3 = bf16[16,48,256]{2,1,0:T(8,128)(2,1)S(1)} async-done(((bf16[16,48,256]{2,1,0:T(8,128)(2,1)}), bf16[16,48,256]{2,1,0:T(8,128)(2,1)S(1)}, u32[]{:S(2)}, u32[]{:S(2)}) %all-to-all-start.3) | async-done | bytes 393248 | tf_op jit(solution)/shard_map/all_to_all | solution.py:23
  98.1 6.3 %all-to-all-start.1 = ((f32[16,24,128]{2,1,0:T(8,128)}), f32[16,24,128]{2,1,0:T(8,128)S(1)}, u32[]{:S(2)}, u32[]{:S(2)}) async-start(f32[16,24,128]{2,1,0:T(8,128)} %bitcast.4), calls=%async_computation.1 | async-start | bytes 393216 | tf_op jit(solution)/shard_map/all_to_all | solution.py:23
  106.5 13.8 %all-to-all-done.1 = f32[16,24,128]{2,1,0:T(8,128)S(1)} async-done(((f32[16,24,128]{2,1,0:T(8,128)}), f32[16,24,128]{2,1,0:T(8,128)S(1)}, u32[]{:S(2)}, u32[]{:S(2)}) %all-to-all-start.1) | async-done | bytes 196640 | tf_op jit(solution)/shard_map/all_to_all | solution.py:23
  121.0 4.7 %all-to-all-start.2 = ((bf16[16,24,128]{2,1,0:T(8,128)(2,1)}), bf16[16,24,128]{2,1,0:T(8,128)(2,1)S(1)}, u32[]{:S(2)}, u32[]{:S(2)}) async-start(bf16[16,24,128]{2,1,0:T(8,128)(2,1)} %broadcast_in_dim.40), calls=%async_computation.2 | async-start | bytes 196608 | tf_op jit(solution)/shard_map/all_to_all | solution.py:23
  125.8 13.1 %all-to-all-done.2 = bf16[16,24,128]{2,1,0:T(8,128)(2,1)S(1)} async-done(((bf16[16,24,128]{2,1,0:T(8,128)(2,1)}), bf16[16,24,128]{2,1,0:T(8,128)(2,1)S(1)}, u32[]{:S(2)}, u32[]{:S(2)}) %all-to-all-start.2) | async-done | bytes 98336 | tf_op jit(solution)/shard_map/all_to_all | solution.py:23
  141.7 6.9 %all-to-all-start.4 = ((bf16[16,56,512]{2,1,0:T(8,128)(2,1)}), bf16[16,56,512]{2,1,0:T(8,128)(2,1)S(1)}, u32[]{:S(2)}, u32[]{:S(2)}) async-start(bf16[16,56,512]{2,1,0:T(8,128)(2,1)} %broadcast_in_dim.42), calls=%async_computation.4 | async-start | bytes 1835008 | tf_op jit(solution)/shard_map/all_to_all | solution.py:23
  151.0 9.2 %psum.14 = s32[224]{0:T(256)S(1)} all-reduce(s32[224]{0:T(256)S(1)} %dynamic_update_slice.6), channel_id=1, replica_groups=mesh['z'=16,'x'=4,'y'=4,'c'=2] {'y'}, use_global_device_ids=true, to_apply=%region_0.0 | all-reduce | flops 224 | bytes 1792 | tf_op jit(solution)/shard_map/psum | solution.py:118
  160.4 8.2 %psum.15 = s32[896]{0:T(1024)S(1)} all-reduce(s32[896]{0:T(1024)S(1)} %dynamic_update_slice.7), channel_id=1, replica_groups=mesh['z'=16,'x'=4,'y'=4,'c'=2] {'x'}, use_global_device_ids=true, to_apply=%region_1.0 | all-reduce | flops 896 | bytes 7168 | tf_op jit(solution)/shard_map/psum | solution.py:120
  170.7 6.9 %fusion.6 = (f32[896]{0:T(1024)S(1)}, f32[896]{0:T(1024)S(1)}, f32[896]{0:T(1024)S(1)}, f32[896]{0:T(1024)S(1)}, f32[896]{0:T(1024)S(1)}, /*index=5*/bf16[896,1024]{1,0:T(8,128)(2,1)}) fusion(s32[1024]{0:T(1024)S(1)} %pad_add_fusion, s32[896]{0:T(1024)S(1)} %psum.15, bf16[896,512]{1,0:T(8,128)(2,1)S(1)} %bitcast.51, ...), kind=kOutput, calls=%fused_computation.16 | convolution fusion | flops 966389376 | bytes 3826688 | tf_op jit(solution)/shard_map/dot_general | solution.py:156
  177.9 6.5 %all-to-all-start.6 = ((bf16[16,56,512]{2,1,0:T(8,128)(2,1)}), bf16[16,56,512]{2,1,0:T(8,128)(2,1)S(1)}, u32[]{:S(2)}, u32[]{:S(2)}) async-start(bf16[16,56,512]{2,1,0:T(8,128)(2,1)} %bitcast.16), calls=%async_computation.6 | async-start | bytes 1835008 | tf_op jit(solution)/shard_map/all_to_all | solution.py:23
  188.4 6.4 %all-to-all-done.6 = bf16[16,56,512]{2,1,0:T(8,128)(2,1)S(1)} async-done(((bf16[16,56,512]{2,1,0:T(8,128)(2,1)}), bf16[16,56,512]{2,1,0:T(8,128)(2,1)S(1)}, u32[]{:S(2)}, u32[]{:S(2)}) %all-to-all-start.6) | async-done | bytes 917536 | tf_op jit(solution)/shard_map/all_to_all | solution.py:23
  194.8 5.6 %all-to-all-start.5 = ((bf16[16,64,512]{2,1,0:T(8,128)(2,1)}), bf16[16,64,512]{2,1,0:T(8,128)(2,1)S(1)}, u32[]{:S(2)}, u32[]{:S(2)}) async-start(bf16[16,64,512]{2,1,0:T(8,128)(2,1)} %pad_maximum_fusion.1), calls=%async_computation.5 | async-start | bytes 2097152 | tf_op jit(solution)/shard_map/all_to_all | solution.py:23
  201.0 10.4 %all-to-all-done.5 = bf16[16,64,512]{2,1,0:T(8,128)(2,1)S(1)} async-done(((bf16[16,64,512]{2,1,0:T(8,128)(2,1)}), bf16[16,64,512]{2,1,0:T(8,128)(2,1)S(1)}, u32[]{:S(2)}, u32[]{:S(2)}) %all-to-all-start.5) | async-done | bytes 1048608 | tf_op jit(solution)/shard_map/all_to_all | solution.py:23
  213.1 3.9 %all-to-all-start.7 = ((bf16[16,59,128]{2,1,0:T(8,128)(2,1)}), bf16[16,59,128]{2,1,0:T(8,128)(2,1)S(1)}, u32[]{:S(2)}, u32[]{:S(2)}) async-start(bf16[16,59,128]{2,1,0:T(8,128)(2,1)} %pad_maximum_fusion.4), calls=%async_computation.7 | async-start | bytes 524288 | tf_op jit(solution)/shard_map/all_to_all | solution.py:23
  220.2 10.9 %all-to-all-done.7 = bf16[16,59,128]{2,1,0:T(8,128)(2,1)S(1)} async-done(((bf16[16,59,128]{2,1,0:T(8,128)(2,1)}), bf16[16,59,128]{2,1,0:T(8,128)(2,1)S(1)}, u32[]{:S(2)}, u32[]{:S(2)}) %all-to-all-start.7) | async-done | bytes 241696 | tf_op jit(solution)/shard_map/all_to_all | solution.py:23
  (117 shorter events, 52.5 us)
Async XLA Ops:
  0.6 55.2 %copy-start = (bf16[48,512]{1,0:T(8,128)(2,1)S(1)}, bf16[48,512]{1,0:T(8,128)(2,1)}, u32[]{:S(2)}) copy-start(bf16[48,512]{1,0:T(8,128)(2,1)} %param.7) | copy-start | bytes 147460
  0.6 25.1 %copy-start.5 = (bf16[56,3840]{1,0:T(8,128)(2,1)S(1)}, bf16[56,3840]{1,0:T(8,128)(2,1)}, u32[]{:S(2)}) copy-start(bf16[56,3840]{1,0:T(8,128)(2,1)} %mine.1) | copy-start | bytes 1290244
  0.7 8.6 %collective-permute-start.3 = (bf16[24,3840]{1,0:T(8,128)(2,1)}, bf16[24,3840]{1,0:T(8,128)(2,1)S(1)}, u32[]{:S(2)}, u32[]{:S(2)}) collective-permute-start(bf16[24,3840]{1,0:T(8,128)(2,1)} %bitcast.62), channel_id=1, source_target_pairs={{0,2},{2,0},{4,6},{6,4},{1,3},{3,1},{5,7},{7,5},{8,10},{10,8},{12,... | collective-permute-start | bytes 552968 | tf_op jit(solution)/shard_map/ppermute | solution.py:108
  10.2 12.6 %collective-permute-start.4 = (bf16[48,3840]{1,0:T(8,128)(2,1)S(1)}, bf16[48,3840]{1,0:T(8,128)(2,1)S(1)}, u32[]{:S(2)}, u32[]{:S(2)}) collective-permute-start(bf16[48,3840]{1,0:T(8,128)(2,1)S(1)} %pad_maximum_fusion.3), channel_id=1, source_target_pairs={{0,6},{6,0},{2,4},{4,2},{1,7},{7,1},{3,5},{5,3},{8,14},{14,8},{10,... | collective-permute-start | bytes 1105928 | tf_op jit(solution)/shard_map/ppermute | solution.py:109
  15.2 13.4 %collective-permute-start = (bf16[56,3840]{1,0:T(8,128)(2,1)}, bf16[56,3840]{1,0:T(8,128)(2,1)S(1)}, u32[]{:S(2)}, u32[]{:S(2)}) collective-permute-start(bf16[56,3840]{1,0:T(8,128)(2,1)} %mine.1), channel_id=1, source_target_pairs={{0,8},{8,16},{16,24},{24,0},{1,9},{9,17},{17,25},{25,1},{2,10},{10... | collective-permute-start | bytes 1290248 | tf_op jit(solution)/shard_map/ppermute | solution.py:35
  23.8 18.6 %copy-start.2 = (bf16[96,3840]{1,0:T(8,128)(2,1)}, bf16[96,3840]{1,0:T(8,128)(2,1)S(1)}, u32[]{:S(2)}) copy-start(bf16[96,3840]{1,0:T(8,128)(2,1)S(1)} %pad_maximum_fusion.2.own_cols) | copy-start | bytes 2211844
  23.9 18.6 %collective-permute-start.5 = (bf16[96,3840]{1,0:T(8,128)(2,1)S(1)}, bf16[96,3840]{1,0:T(8,128)(2,1)S(1)}, u32[]{:S(2)}, u32[]{:S(2)}) collective-permute-start(bf16[96,3840]{1,0:T(8,128)(2,1)S(1)} %pad_maximum_fusion.2.own_cols), channel_id=1, source_target_pairs={{0,1},{1,0},{2,3},{3,2},{4,5},{5,4},{6,7},{7,6},{8,9},{9,8},{10,11... | collective-permute-start | bytes 2211848 | tf_op jit(solution)/shard_map/ppermute | solution.py:31
  25.8 15.4 %collective-permute-start.1 = (bf16[56,3840]{1,0:T(8,128)(2,1)S(1)}, bf16[56,3840]{1,0:T(8,128)(2,1)S(1)}, u32[]{:S(2)}, u32[]{:S(2)}) collective-permute-start(bf16[56,3840]{1,0:T(8,128)(2,1)S(1)} %copy-done.5), channel_id=1, source_target_pairs={{0,24},{8,0},{16,8},{24,16},{1,25},{9,1},{17,9},{25,17},{2,26},{10... | collective-permute-start | bytes 1290248 | tf_op jit(solution)/shard_map/ppermute | solution.py:35
  28.6 13.9 %copy-start.6 = (bf16[56,3840]{1,0:T(8,128)(2,1)}, bf16[56,3840]{1,0:T(8,128)(2,1)S(1)}, u32[]{:S(2)}) copy-start(bf16[56,3840]{1,0:T(8,128)(2,1)S(1)} %collective-permute-done.left) | copy-start | bytes 1290244
  28.6 13.9 %collective-permute-start.2 = (bf16[56,3840]{1,0:T(8,128)(2,1)S(1)}, bf16[56,3840]{1,0:T(8,128)(2,1)S(1)}, u32[]{:S(2)}, u32[]{:S(2)}) collective-permute-start(bf16[56,3840]{1,0:T(8,128)(2,1)S(1)} %collective-permute-done.left), channel_id=1, source_target_pairs={{0,8},{8,16},{16,24},{24,0},{1,9},{9,17},{17,25},{25,1},{2,10},{10... | collective-permute-start | bytes 1290248 | tf_op jit(solution)/shard_map/ppermute | solution.py:35
  48.1 56.3 %copy-start.1 = (bf16[512,512]{1,0:T(8,128)(2,1)S(1)}, bf16[512,512]{1,0:T(8,128)(2,1)}, u32[]{:S(2)}) copy-start(bf16[512,512]{1,0:T(8,128)(2,1)} %centres.1) | copy-start | bytes 1572868
  48.1 12.1 %all-to-all-start = ((f32[4,4,24,128]{3,2,1,0:T(8,128)}), f32[4,4,24,128]{3,2,1,0:T(8,128)}, u32[]{:S(2)}, u32[]{:S(2)}) async-start(f32[4,4,24,128]{3,2,1,0:T(8,128)} %shard_map.68), calls=%async_computation | async-start | bytes 393216 | tf_op jit(solution)/shard_map/all_to_all | solution.py:23
  60.9 37.1 %all-to-all-start.3 = ((bf16[16,48,256]{2,1,0:T(8,128)(2,1)}), bf16[16,48,256]{2,1,0:T(8,128)(2,1)S(1)}, u32[]{:S(2)}, u32[]{:S(2)}) async-start(bf16[16,48,256]{2,1,0:T(8,128)(2,1)} %broadcast_in_dim.41), calls=%async_computation.3 | async-start | bytes 786432 | tf_op jit(solution)/shard_map/all_to_all | solution.py:23
  98.1 22.3 %all-to-all-start.1 = ((f32[16,24,128]{2,1,0:T(8,128)}), f32[16,24,128]{2,1,0:T(8,128)S(1)}, u32[]{:S(2)}, u32[]{:S(2)}) async-start(f32[16,24,128]{2,1,0:T(8,128)} %bitcast.4), calls=%async_computation.1 | async-start | bytes 393216 | tf_op jit(solution)/shard_map/all_to_all | solution.py:23
  104.6 21.2 %collective-permute-start.7 = (bf16[16,48,256]{2,1,0:T(8,128)(2,1)S(1)}, bf16[16,48,256]{2,1,0:T(8,128)(2,1)S(1)}, u32[]{:S(2)}, u32[]{:S(2)}) collective-permute-start(bf16[16,48,256]{2,1,0:T(8,128)(2,1)S(1)} %all-to-all-done.3), channel_id=1, source_target_pairs={{0,1},{1,0},{2,3},{3,2},{4,5},{5,4},{6,7},{7,6},{8,9},{9,8},{10,11... | collective-permute-start | bytes 1179656 | tf_op jit(solution)/shard_map/ppermute | solution.py:31
  121.0 17.9 %all-to-all-start.2 = ((bf16[16,24,128]{2,1,0:T(8,128)(2,1)}), bf16[16,24,128]{2,1,0:T(8,128)(2,1)S(1)}, u32[]{:S(2)}, u32[]{:S(2)}) async-start(bf16[16,24,128]{2,1,0:T(8,128)(2,1)} %broadcast_in_dim.40), calls=%async_computation.2 | async-start | bytes 196608 | tf_op jit(solution)/shard_map/all_to_all | solution.py:23
  140.7 10.1 %copy-start.11 = (s32[56]{0:T(128)S(1)}, s32[56]{0:T(128)}, u32[]{:S(2)}) copy-start(s32[56]{0:T(128)} %param.9) | copy-start | bytes 676
  141.7 29.0 %all-to-all-start.4 = ((bf16[16,56,512]{2,1,0:T(8,128)(2,1)}), bf16[16,56,512]{2,1,0:T(8,128)(2,1)S(1)}, u32[]{:S(2)}, u32[]{:S(2)}) async-start(bf16[16,56,512]{2,1,0:T(8,128)(2,1)} %broadcast_in_dim.42), calls=%async_computation.4 | async-start | bytes 1835008 | tf_op jit(solution)/shard_map/all_to_all | solution.py:23
  148.8 19.8 %collective-permute-start.6 = (bf16[512,512]{1,0:T(8,128)(2,1)S(1)}, bf16[512,512]{1,0:T(8,128)(2,1)S(1)}, u32[]{:S(2)}, u32[]{:S(2)}) collective-permute-start(bf16[512,512]{1,0:T(8,128)(2,1)S(1)} %fusion.14), channel_id=1, source_target_pairs={{0,1},{1,0},{2,3},{3,2},{4,5},{5,4},{6,7},{7,6},{8,9},{9,8},{10,11... | collective-permute-start | bytes 1572872 | tf_op jit(solution)/shard_map/ppermute | solution.py:31
  168.6 16.1 %copy-start.9 = (bf16[512,512]{1,0:T(8,128)(2,1)}, bf16[512,512]{1,0:T(8,128)(2,1)S(1)}, u32[]{:S(2)}) copy-start(bf16[512,512]{1,0:T(8,128)(2,1)S(1)} %collective-permute-done.6) | copy-start | bytes 1572868
  177.9 16.9 %all-to-all-start.6 = ((bf16[16,56,512]{2,1,0:T(8,128)(2,1)}), bf16[16,56,512]{2,1,0:T(8,128)(2,1)S(1)}, u32[]{:S(2)}, u32[]{:S(2)}) async-start(bf16[16,56,512]{2,1,0:T(8,128)(2,1)} %bitcast.16), calls=%async_computation.6 | async-start | bytes 1835008 | tf_op jit(solution)/shard_map/all_to_all | solution.py:23
  194.8 16.6 %all-to-all-start.5 = ((bf16[16,64,512]{2,1,0:T(8,128)(2,1)}), bf16[16,64,512]{2,1,0:T(8,128)(2,1)S(1)}, u32[]{:S(2)}, u32[]{:S(2)}) async-start(bf16[16,64,512]{2,1,0:T(8,128)(2,1)} %pad_maximum_fusion.1), calls=%async_computation.5 | async-start | bytes 2097152 | tf_op jit(solution)/shard_map/all_to_all | solution.py:23
  213.1 18.1 %all-to-all-start.7 = ((bf16[16,59,128]{2,1,0:T(8,128)(2,1)}), bf16[16,59,128]{2,1,0:T(8,128)(2,1)S(1)}, u32[]{:S(2)}, u32[]{:S(2)}) async-start(bf16[16,59,128]{2,1,0:T(8,128)(2,1)} %pad_maximum_fusion.4), calls=%async_computation.7 | async-start | bytes 524288 | tf_op jit(solution)/shard_map/all_to_all | solution.py:23
  234.8 6.7 %collective-permute-start.8 = (f32[512,512]{1,0:T(8,128)}, f32[512,512]{1,0:T(8,128)S(1)}, u32[]{:S(2)}, u32[]{:S(2)}) collective-permute-start(f32[512,512]{1,0:T(8,128)} %fusion.16), channel_id=1, source_target_pairs={{0,1},{1,0},{2,3},{3,2},{4,5},{5,4},{6,7},{7,6},{8,9},{9,8},{10,11... | collective-permute-start | bytes 3145736 | tf_op jit(solution)/shard_map/ppermute | solution.py:31
  (5 other events, 9.9 us)

commit v7 on v4

--- a/solution.py
+++ b/solution.py
@@ -15,6 +15,7 @@
 NZ, NX, NY, NC = 16, 4, 4, 2
 XY = ("x", "y")
 SWAP = [(0, 1), (1, 0)]
+NEAR = [(0, 1), (1, 0), (2, 3), (3, 2)]
 f32 = jnp.float32
 bf16 = jnp.bfloat16
 
@@ -35,7 +36,7 @@
     return lax.ppermute(block, axis, [(i, (i + by) % 4) for i in range(4)])
 
 
-def hidden_kernel(seat, mine, left, right, far, own_cols, other_cols, out, held):
+def hidden_kernel(seat, mine, left, right, far, own_cols, other_cols, out, held, weights):
     x, y, c = seat[0], seat[1], seat[2]
     rows, feats = mine.shape
     cols = own_cols.shape[0] // NY
@@ -44,26 +45,26 @@
         held[k, rows:] = jnp.zeros((64 - rows, feats), bf16)
     blocks = held[...].reshape(NX * 64, feats)
 
-    def times(weights):
-        return lax.dot_general(weights, blocks, (((1,), (1,)), ((), ())), preferred_element_type=f32)
-
-    own, other = times(own_cols[...]), times(other_cols[...])
+    half = own_cols.shape[0]
+    weights[:half], weights[half:] = own_cols[...], other_cols[...]
+    both = lax.dot_general(weights[...], blocks, (((1,), (1,)), ((), ())), preferred_element_type=f32)
+    own, other = both[:half], both[half:]
     first, second = jnp.where(c == 0, own, other), jnp.where(c == 0, other, own)
     beside = y + 1 - 2 * lax.rem(y, 2)
     for k, off in enumerate((0, 3, 1, 2)):
         both = jnp.concatenate([first[:, 64 * k : 64 * k + 64], second[:, 64 * k : 64 * k + 64]], axis=1)
         for j, at in enumerate((y, beside, 3 - y, 3 - beside)):
-            out[lax.rem(x + off, NX), at] = both[j * cols : (j + 1) * cols]
+            out[lax.rem(x + off, NX), at] = both[j * cols : (j + 1) * cols].astype(bf16)
 
 
 def partial_hidden(seat, blocks, own_cols, other_cols, cols):
     vmem = pl.BlockSpec(memory_space=pltpu.VMEM)
     return pl.pallas_call(
         hidden_kernel,
-        out_shape=jax.ShapeDtypeStruct((NX, NY, cols, 128), f32),
+        out_shape=jax.ShapeDtypeStruct((NX, NY, cols, 128), bf16),
         in_specs=[pl.BlockSpec(memory_space=pltpu.SMEM)] + [vmem] * 6,
         out_specs=vmem,
-        scratch_shapes=[pltpu.VMEM((NX, 64, blocks[0].shape[1]), bf16)],
+        scratch_shapes=[pltpu.VMEM((NX, 64, blocks[0].shape[1]), bf16), pltpu.VMEM((2 * NY * cols, blocks[0].shape[1]), bf16)],
         cost_estimate=pl.CostEstimate(flops=330_000_000, bytes_accessed=3_400_000, transcendentals=0),
     )(seat, *blocks, own_cols, other_cols)
 
@@ -99,25 +100,26 @@
     emb = proj_out.shape[1]
     cen = centres.shape[0]
     images = NX * NY * rows
+    lanes = emb // 4
     zi, xi, yi, ci = (lax.axis_index(a) for a in ("z", "x", "y", "c"))
 
     from_left = shift(features, "x", 1)
     from_right = shift(features, "x", 3)
     own_cols = proj_in.T
-    own_out = spread(lax.dynamic_slice_in_dim(proj_out, ci * (emb // 2), emb // 2, 1), "z", NZ)
-    own_cols = jnp.concatenate([own_cols, lax.ppermute(own_cols, "y", [(0, 1), (1, 0), (2, 3), (3, 2)])], axis=0)
+    own_out = spread(lax.dynamic_slice_in_dim(proj_out, ci * (emb // 2) + lax.rem(yi, 2) * lanes, lanes, 1), "z", NZ)
+    own_cols = jnp.concatenate([own_cols, lax.ppermute(own_cols, "y", NEAR)], axis=0)
     own_cols = jnp.concatenate([own_cols, lax.ppermute(own_cols, "y", [(0, 3), (3, 0), (1, 2), (2, 1)])], axis=0)
     from_far = shift(from_left, "x", 1)
     other_cols = partner(own_cols)
     seat = jnp.stack([xi, yi, ci]).astype(jnp.int32)
     part = partial_hidden(seat, (features, from_left, from_right, from_far), own_cols, other_cols, cols)
     part = exchange(part, "x").reshape(NZ, cols, 128)
-
     part, labels = lax.optimization_barrier((part, labels))
     all_labels = lax.dynamic_update_slice_in_dim(jnp.zeros(NY * rows, jnp.int32), labels, yi * rows, 0)
     all_labels = lax.psum(all_labels, "y")
     all_labels = lax.dynamic_update_slice_in_dim(jnp.zeros(images, jnp.int32), all_labels, xi * NY * rows, 0)
     all_labels = lax.psum(all_labels, "x")
+
     all_labels = all_labels.reshape(images, 1)
     wide = centres.astype(f32)
     cinv = lax.rsqrt(jnp.sum(wide * wide, axis=1) + norm_eps)
@@ -129,8 +131,11 @@
     position = jnp.concatenate([(chip + ci) * cen + step, (chip + 1 - ci) * cen + step])
     target = all_labels == position[None, :]
 
+    beside_out = lax.ppermute(own_out, "y", NEAR)
+    even = lax.rem(yi, 2) == 0
+    own_out = jnp.concatenate([jnp.where(even, own_out, beside_out), jnp.where(even, beside_out, own_out)], axis=2)
     other_out = partner(own_out)
-    hidden = jnp.sum(exchange(part, "z"), axis=0).astype(bf16)
+    hidden = jnp.sum(exchange(part, "z").astype(f32), axis=0).astype(bf16)
     hidden = spread(hidden, "z", NZ).reshape(NZ * cols, 128)
 
     def over_rows(left, right):

time: 246 us -> 217 us (0.88)
  the two profiles are of different devices: /device:TPU:6 before, /device:TPU:1 now
where the time goes in v7:
time: 217 us; the launch traced here: 216 us
  starting transfers between devices  102 us (47%)
  waiting for transfers between devices  52.1 us (24%)
  matrix products  20.7 us (10%)
  blocking collectives  15.4 us (7%)
  local copies, waits for them, and re-layouts  8.92 us (4%)
  other arithmetic  8.69 us (4%)
  Pallas kernels  6.44 us (3%)
    all_to_all x8, starting transfers between devices, exchange(): return lax.all_to_all(blocks, axis, 0, 0)  54.8 us
    all_to_all x8, waiting for transfers between devices, exchange(): return lax.all_to_all(blocks, axis, 0, 0)  40.9 us
    ppermute x4, starting transfers between devices, partner(): return lax.ppermute(block, 'c', SWAP)  26.8 us
    psum x1, blocking collectives, step_of(): all_labels = lax.psum(all_labels, 'y')  9.53 us
    ppermute x3, starting transfers between devices, shift(): return lax.ppermute(block, axis, [(i, (i + by) % 4) for i in range(4)])  8.41 us
    ppermute x3, waiting for transfers between devices, shift(): return lax.ppermute(block, axis, [(i, (i + by) % 4) for i in range(4)])  8.11 us
    dot_general x1, matrix products, step_of(): lax.dot_general(units, low, (((1,), (1,)), ((), ())), preferred_element_t...  8.02 us
    ppermute x1, starting transfers between devices, step_of(): lax.ppermute(own_cols, 'y', [(0, 3), (3, 0), (1, 2), (2, 1)])  5.93 us
  transfers between devices with their start and end apart: 18, of which 9 were waited for; matrix products, arithmetic and copies ran while one was open for 13% of the time, Pallas kernels for 2%

profile of v7, /device:TPU:1, one launch (start us, length us, event | category | flops | bytes accessed | tf_op | source)
XLA Modules:
  0.0 215.7 jit_solution(18426264920047460778)
XLA Ops:
  0.6 4.2 %collective-permute-start.3 = (bf16[24,3840]{1,0:T(8,128)(2,1)}, bf16[24,3840]{1,0:T(8,128)(2,1)S(1)}, u32[]{:S(2)}, u32[]{:S(2)}) collective-permute-start(bf16[24,3840]{1,0:T(8,128)(2,1)} %bitcast.61), channel_id=1, source_target_pairs={{0,2},{2,0},{4,6},{6,4},{1,3},{3,1},{5,7},{7,5},{8,10},{10,8},{12,... | collective-permute-start | bytes 552968 | tf_op jit(solution)/shard_map/ppermute | solution.py:110
  8.9 5.9 %collective-permute-start.4 = (bf16[48,3840]{1,0:T(8,128)(2,1)S(1)}, bf16[48,3840]{1,0:T(8,128)(2,1)S(1)}, u32[]{:S(2)}, u32[]{:S(2)}) collective-permute-start(bf16[48,3840]{1,0:T(8,128)(2,1)S(1)} %pad_maximum_fusion.6), channel_id=1, source_target_pairs={{0,6},{6,0},{2,4},{4,2},{1,7},{7,1},{3,5},{5,3},{8,14},{14,8},{10,... | collective-permute-start | bytes 1105928 | tf_op jit(solution)/shard_map/ppermute | solution.py:111
  15.6 14.9 %all-to-all-start.3 = ((bf16[16,48,128]{2,1,0:T(8,128)(2,1)}), bf16[16,48,128]{2,1,0:T(8,128)(2,1)S(1)}, u32[]{:S(2)}, u32[]{:S(2)}) async-start(bf16[16,48,128]{2,1,0:T(8,128)(2,1)} %broadcast_in_dim.33), calls=%async_computation.3 | async-start | bytes 393216 | tf_op jit(solution)/shard_map/all_to_all | solution.py:24
  34.6 4.3 %collective-permute-start.5 = (bf16[96,3840]{1,0:T(8,128)(2,1)S(1)}, bf16[96,3840]{1,0:T(8,128)(2,1)S(1)}, u32[]{:S(2)}, u32[]{:S(2)}) collective-permute-start(bf16[96,3840]{1,0:T(8,128)(2,1)S(1)} %pad_maximum_fusion.4.own_cols), channel_id=1, source_target_pairs={{0,1},{1,0},{2,3},{3,2},{4,5},{5,4},{6,7},{7,6},{8,9},{9,8},{10,11... | collective-permute-start | bytes 2211848 | tf_op jit(solution)/shard_map/ppermute | solution.py:32
  47.7 4.9 %collective-permute-done.1.right = bf16[56,3840]{1,0:T(8,128)(2,1)S(1)} collective-permute-done((bf16[56,3840]{1,0:T(8,128)(2,1)}, bf16[56,3840]{1,0:T(8,128)(2,1)S(1)}, u32[]{:S(2)}, u32[]{:S(2)}) %collective-permute-start.1) | collective-permute-done | bytes 430112 | tf_op jit(solution)/shard_map/ppermute | solution.py:36
  59.2 3.9 %all-to-all-start = ((bf16[4,4,24,128]{3,2,1,0:T(8,128)(2,1)}), bf16[4,4,24,128]{3,2,1,0:T(8,128)(2,1)}, u32[]{:S(2)}, u32[]{:S(2)}) async-start(bf16[4,4,24,128]{3,2,1,0:T(8,128)(2,1)} %shard_map.68), calls=%async_computation | async-start | bytes 196608 | tf_op jit(solution)/shard_map/all_to_all | solution.py:24
  63.1 4.7 %all-to-all-done = bf16[4,4,24,128]{3,2,1,0:T(8,128)(2,1)} async-done(((bf16[4,4,24,128]{3,2,1,0:T(8,128)(2,1)}), bf16[4,4,24,128]{3,2,1,0:T(8,128)(2,1)}, u32[]{:S(2)}, u32[]{:S(2)}) %all-to-all-start) | async-done | bytes 98336 | tf_op jit(solution)/shard_map/all_to_all | solution.py:24
  67.9 10.9 %all-to-all-start.1 = ((bf16[16,24,128]{2,1,0:T(8,128)(2,1)}), bf16[16,24,128]{2,1,0:T(8,128)(2,1)S(1)}, u32[]{:S(2)}, u32[]{:S(2)}) async-start(bf16[16,24,128]{2,1,0:T(8,128)(2,1)} %bitcast.4), calls=%async_computation.1 | async-start | bytes 196608 | tf_op jit(solution)/shard_map/all_to_all | solution.py:24
  78.9 7.4 %collective-permute-start.8 = (bf16[16,48,256]{2,1,0:T(8,128)(2,1)S(1)}, bf16[16,48,256]{2,1,0:T(8,128)(2,1)S(1)}, u32[]{:S(2)}, u32[]{:S(2)}) collective-permute-start(bf16[16,48,256]{2,1,0:T(8,128)(2,1)S(1)} %pad_maximum_fusion.5), channel_id=1, source_target_pairs={{0,1},{1,0},{2,3},{3,2},{4,5},{5,4},{6,7},{7,6},{8,9},{9,8},{10,11... | collective-permute-start | bytes 1179656 | tf_op jit(solution)/shard_map/ppermute | solution.py:32
  86.5 4.2 %all-to-all-done.1 = bf16[16,24,128]{2,1,0:T(8,128)(2,1)S(1)} async-done(((bf16[16,24,128]{2,1,0:T(8,128)(2,1)}), bf16[16,24,128]{2,1,0:T(8,128)(2,1)S(1)}, u32[]{:S(2)}, u32[]{:S(2)}) %all-to-all-start.1) | async-done | bytes 98336 | tf_op jit(solution)/shard_map/all_to_all | solution.py:24
  91.4 7.5 %all-to-all-start.2 = ((bf16[16,24,128]{2,1,0:T(8,128)(2,1)}), bf16[16,24,128]{2,1,0:T(8,128)(2,1)S(1)}, u32[]{:S(2)}, u32[]{:S(2)}) async-start(bf16[16,24,128]{2,1,0:T(8,128)(2,1)} %broadcast_in_dim.32), calls=%async_computation.2 | async-start | bytes 196608 | tf_op jit(solution)/shard_map/all_to_all | solution.py:24
  99.0 11.8 %all-to-all-done.2 = bf16[16,24,128]{2,1,0:T(8,128)(2,1)S(1)} async-done(((bf16[16,24,128]{2,1,0:T(8,128)(2,1)}), bf16[16,24,128]{2,1,0:T(8,128)(2,1)S(1)}, u32[]{:S(2)}, u32[]{:S(2)}) %all-to-all-start.2) | async-done | bytes 98336 | tf_op jit(solution)/shard_map/all_to_all | solution.py:24
  113.0 3.6 %all-to-all-start.4 = ((bf16[16,56,512]{2,1,0:T(8,128)(2,1)}), bf16[16,56,512]{2,1,0:T(8,128)(2,1)S(1)}, u32[]{:S(2)}, u32[]{:S(2)}) async-start(bf16[16,56,512]{2,1,0:T(8,128)(2,1)} %broadcast_in_dim.34), calls=%async_computation.4 | async-start | bytes 1835008 | tf_op jit(solution)/shard_map/all_to_all | solution.py:24
  116.9 5.5 %collective-permute-start.6 = (bf16[512,512]{1,0:T(8,128)(2,1)S(1)}, bf16[512,512]{1,0:T(8,128)(2,1)S(1)}, u32[]{:S(2)}, u32[]{:S(2)}) collective-permute-start(bf16[512,512]{1,0:T(8,128)(2,1)S(1)} %fusion.21), channel_id=1, source_target_pairs={{0,1},{1,0},{2,3},{3,2},{4,5},{5,4},{6,7},{7,6},{8,9},{9,8},{10,11... | collective-permute-start | bytes 1572872 | tf_op jit(solution)/shard_map/ppermute | solution.py:32
  122.7 9.5 %psum.14 = s32[224]{0:T(256)S(1)} all-reduce(s32[224]{0:T(256)S(1)} %dynamic_update_slice.6), channel_id=1, replica_groups=mesh['z'=16,'x'=4,'y'=4,'c'=2] {'y'}, use_global_device_ids=true, to_apply=%region_0.0 | all-reduce | flops 224 | bytes 1792 | tf_op jit(solution)/shard_map/psum | solution.py:119
  132.4 5.9 %psum.15 = s32[896]{0:T(1024)S(1)} all-reduce(s32[896]{0:T(1024)S(1)} %dynamic_update_slice.7), channel_id=1, replica_groups=mesh['z'=16,'x'=4,'y'=4,'c'=2] {'x'}, use_global_device_ids=true, to_apply=%region_1.0 | all-reduce | flops 896 | bytes 7168 | tf_op jit(solution)/shard_map/psum | solution.py:121
  140.4 3.8 %all-to-all-start.6 = ((bf16[16,56,512]{2,1,0:T(8,128)(2,1)}), bf16[16,56,512]{2,1,0:T(8,128)(2,1)S(1)}, u32[]{:S(2)}, u32[]{:S(2)}) async-start(bf16[16,56,512]{2,1,0:T(8,128)(2,1)} %bitcast.15), calls=%async_computation.6 | async-start | bytes 1835008 | tf_op jit(solution)/shard_map/all_to_all | solution.py:24
  144.2 8.0 %fusion.6 = (f32[896]{0:T(1024)S(1)}, f32[896]{0:T(1024)S(1)}, f32[896]{0:T(1024)S(1)}, f32[896]{0:T(1024)S(1)}, f32[896]{0:T(1024)S(1)}, /*index=5*/bf16[896,1024]{1,0:T(8,128)(2,1)}) fusion(s32[1024]{0:T(1024)S(1)} %pad_add_fusion, s32[896]{0:T(1024)S(1)} %psum.15, bf16[896,512]{1,0:T(8,128)(2,1)S(1)} %bitcast.47, bf16[512,512]{1,0:T(8,128)(2,1)} %copy-done.10, ...), kind=kOutput, calls=%fused_computation.13 | convolution fusion | flops 966389376 | bytes 3826688 | tf_op jit(solution)/shard_map/dot_general | solution.py:161
  156.8 6.5 %all-to-all-start.5 = ((bf16[16,64,512]{2,1,0:T(8,128)(2,1)}), bf16[16,64,512]{2,1,0:T(8,128)(2,1)S(1)}, u32[]{:S(2)}, u32[]{:S(2)}) async-start(bf16[16,64,512]{2,1,0:T(8,128)(2,1)} %pad_maximum_fusion.3), calls=%async_computation.5 | async-start | bytes 2097152 | tf_op jit(solution)/shard_map/all_to_all | solution.py:24
  164.0 11.4 %all-to-all-done.5 = bf16[16,64,512]{2,1,0:T(8,128)(2,1)S(1)} async-done(((bf16[16,64,512]{2,1,0:T(8,128)(2,1)}), bf16[16,64,512]{2,1,0:T(8,128)(2,1)S(1)}, u32[]{:S(2)}, u32[]{:S(2)}) %all-to-all-start.5) | async-done | bytes 1048608 | tf_op jit(solution)/shard_map/all_to_all | solution.py:24
  177.0 3.5 %all-to-all-start.7 = ((bf16[16,52,128]{2,1,0:T(8,128)(2,1)}), bf16[16,52,128]{2,1,0:T(8,128)(2,1)S(1)}, u32[]{:S(2)}, u32[]{:S(2)}) async-start(bf16[16,52,128]{2,1,0:T(8,128)(2,1)} %pad_maximum_fusion.7), calls=%async_computation.7 | async-start | bytes 458752 | tf_op jit(solution)/shard_map/all_to_all | solution.py:24
  184.3 8.8 %all-to-all-done.7 = bf16[16,52,128]{2,1,0:T(8,128)(2,1)S(1)} async-done(((bf16[16,52,128]{2,1,0:T(8,128)(2,1)}), bf16[16,52,128]{2,1,0:T(8,128)(2,1)S(1)}, u32[]{:S(2)}, u32[]{:S(2)}) %all-to-all-start.7) | async-done | bytes 213024 | tf_op jit(solution)/shard_map/all_to_all | solution.py:24
  197.6 9.6 %collective-permute-start.9 = (f32[512,512]{1,0:T(8,128)}, f32[512,512]{1,0:T(8,128)S(1)}, u32[]{:S(2)}, u32[]{:S(2)}) collective-permute-start(f32[512,512]{1,0:T(8,128)} %fusion.11), channel_id=1, source_target_pairs={{0,1},{1,0},{2,3},{3,2},{4,5},{5,4},{6,7},{7,6},{8,9},{9,8},{10,11... | collective-permute-start | bytes 3145736 | tf_op jit(solution)/shard_map/ppermute | solution.py:32
  208.1 3.6 %fusion.13.own = f32[512,512]{1,0:T(8,128)} fusion(bf16[1792,512]{1,0:T(8,128)(2,1)S(1)} %pad_maximum_fusion.1, bf16[1024,1792]{0,1:T(8,128)(2,1)} %pad_maximum_fusion), kind=kOutput, calls=%fused_computation.28 | convolution fusion | flops 939524096 | bytes 4718592 | tf_op jit(solution)/shard_map/dot_general | solution.py:224
  (130 shorter events, 49.8 us)
Async XLA Ops:
  0.6 14.2 %copy-start = (bf16[48,512]{1,0:T(8,128)(2,1)S(1)}, bf16[48,512]{1,0:T(8,128)(2,1)}, u32[]{:S(2)}) copy-start(bf16[48,512]{1,0:T(8,128)(2,1)} %param.7) | copy-start | bytes 147460
  0.6 7.3 %collective-permute-start.3 = (bf16[24,3840]{1,0:T(8,128)(2,1)}, bf16[24,3840]{1,0:T(8,128)(2,1)S(1)}, u32[]{:S(2)}, u32[]{:S(2)}) collective-permute-start(bf16[24,3840]{1,0:T(8,128)(2,1)} %bitcast.61), channel_id=1, source_target_pairs={{0,2},{2,0},{4,6},{6,4},{1,3},{3,1},{5,7},{7,5},{8,10},{10,8},{12,... | collective-permute-start | bytes 552968 | tf_op jit(solution)/shard_map/ppermute | solution.py:110
  8.9 24.7 %collective-permute-start.4 = (bf16[48,3840]{1,0:T(8,128)(2,1)S(1)}, bf16[48,3840]{1,0:T(8,128)(2,1)S(1)}, u32[]{:S(2)}, u32[]{:S(2)}) collective-permute-start(bf16[48,3840]{1,0:T(8,128)(2,1)S(1)} %pad_maximum_fusion.6), channel_id=1, source_target_pairs={{0,6},{6,0},{2,4},{4,2},{1,7},{7,1},{3,5},{5,3},{8,14},{14,8},{10,... | collective-permute-start | bytes 1105928 | tf_op jit(solution)/shard_map/ppermute | solution.py:111
  14.9 71.4 %copy-start.2 = (bf16[512,512]{1,0:T(8,128)(2,1)S(1)}, bf16[512,512]{1,0:T(8,128)(2,1)}, u32[]{:S(2)}) copy-start(bf16[512,512]{1,0:T(8,128)(2,1)} %centres.1) | copy-start | bytes 1572868
  15.6 29.5 %all-to-all-start.3 = ((bf16[16,48,128]{2,1,0:T(8,128)(2,1)}), bf16[16,48,128]{2,1,0:T(8,128)(2,1)S(1)}, u32[]{:S(2)}, u32[]{:S(2)}) async-start(bf16[16,48,128]{2,1,0:T(8,128)(2,1)} %broadcast_in_dim.33), calls=%async_computation.3 | async-start | bytes 393216 | tf_op jit(solution)/shard_map/all_to_all | solution.py:24
  30.5 12.7 %collective-permute-start = (bf16[56,3840]{1,0:T(8,128)(2,1)}, bf16[56,3840]{1,0:T(8,128)(2,1)S(1)}, u32[]{:S(2)}, u32[]{:S(2)}) collective-permute-start(bf16[56,3840]{1,0:T(8,128)(2,1)} %mine.1), channel_id=1, source_target_pairs={{0,8},{8,16},{16,24},{24,0},{1,9},{9,17},{17,25},{25,1},{2,10},{10... | collective-permute-start | bytes 1290248 | tf_op jit(solution)/shard_map/ppermute | solution.py:36
  34.6 20.3 %copy-start.3 = (bf16[96,3840]{1,0:T(8,128)(2,1)}, bf16[96,3840]{1,0:T(8,128)(2,1)S(1)}, u32[]{:S(2)}) copy-start(bf16[96,3840]{1,0:T(8,128)(2,1)S(1)} %pad_maximum_fusion.4.own_cols) | copy-start | bytes 2211844
  34.6 20.3 %collective-permute-start.5 = (bf16[96,3840]{1,0:T(8,128)(2,1)S(1)}, bf16[96,3840]{1,0:T(8,128)(2,1)S(1)}, u32[]{:S(2)}, u32[]{:S(2)}) collective-permute-start(bf16[96,3840]{1,0:T(8,128)(2,1)S(1)} %pad_maximum_fusion.4.own_cols), channel_id=1, source_target_pairs={{0,1},{1,0},{2,3},{3,2},{4,5},{5,4},{6,7},{7,6},{8,9},{9,8},{10,11... | collective-permute-start | bytes 2211848 | tf_op jit(solution)/shard_map/ppermute | solution.py:32
  38.9 13.7 %collective-permute-start.1 = (bf16[56,3840]{1,0:T(8,128)(2,1)}, bf16[56,3840]{1,0:T(8,128)(2,1)S(1)}, u32[]{:S(2)}, u32[]{:S(2)}) collective-permute-start(bf16[56,3840]{1,0:T(8,128)(2,1)} %mine.1), channel_id=1, source_target_pairs={{0,24},{8,0},{16,8},{24,16},{1,25},{9,1},{17,9},{25,17},{2,26},{10... | collective-permute-start | bytes 1290248 | tf_op jit(solution)/shard_map/ppermute | solution.py:36
  43.2 11.7 %collective-permute-start.2 = (bf16[56,3840]{1,0:T(8,128)(2,1)S(1)}, bf16[56,3840]{1,0:T(8,128)(2,1)}, u32[]{:S(2)}, u32[]{:S(2)}) collective-permute-start(bf16[56,3840]{1,0:T(8,128)(2,1)S(1)} %collective-permute-done.left), channel_id=1, source_target_pairs={{0,8},{8,16},{16,24},{24,0},{1,9},{9,17},{17,25},{25,1},{2,10},{10... | collective-permute-start | bytes 1290248 | tf_op jit(solution)/shard_map/ppermute | solution.py:36
  45.1 33.6 %collective-permute-start.7 = (bf16[16,48,128]{2,1,0:T(8,128)(2,1)S(1)}, bf16[16,48,128]{2,1,0:T(8,128)(2,1)S(1)}, u32[]{:S(2)}, u32[]{:S(2)}) collective-permute-start(bf16[16,48,128]{2,1,0:T(8,128)(2,1)S(1)} %all-to-all-done.3), channel_id=1, source_target_pairs={{0,2},{2,0},{4,6},{6,4},{1,3},{3,1},{5,7},{7,5},{8,10},{10,8},{12,... | collective-permute-start | bytes 589832 | tf_op jit(solution)/shard_map/ppermute | solution.py:134
  59.2 8.6 %all-to-all-start = ((bf16[4,4,24,128]{3,2,1,0:T(8,128)(2,1)}), bf16[4,4,24,128]{3,2,1,0:T(8,128)(2,1)}, u32[]{:S(2)}, u32[]{:S(2)}) async-start(bf16[4,4,24,128]{3,2,1,0:T(8,128)(2,1)} %shard_map.68), calls=%async_computation | async-start | bytes 196608 | tf_op jit(solution)/shard_map/all_to_all | solution.py:24
  67.9 22.8 %all-to-all-start.1 = ((bf16[16,24,128]{2,1,0:T(8,128)(2,1)}), bf16[16,24,128]{2,1,0:T(8,128)(2,1)S(1)}, u32[]{:S(2)}, u32[]{:S(2)}) async-start(bf16[16,24,128]{2,1,0:T(8,128)(2,1)} %bitcast.4), calls=%async_computation.1 | async-start | bytes 196608 | tf_op jit(solution)/shard_map/all_to_all | solution.py:24
  78.9 20.1 %collective-permute-start.8 = (bf16[16,48,256]{2,1,0:T(8,128)(2,1)S(1)}, bf16[16,48,256]{2,1,0:T(8,128)(2,1)S(1)}, u32[]{:S(2)}, u32[]{:S(2)}) collective-permute-start(bf16[16,48,256]{2,1,0:T(8,128)(2,1)S(1)} %pad_maximum_fusion.5), channel_id=1, source_target_pairs={{0,1},{1,0},{2,3},{3,2},{4,5},{5,4},{6,7},{7,6},{8,9},{9,8},{10,11... | collective-permute-start | bytes 1179656 | tf_op jit(solution)/shard_map/ppermute | solution.py:32
  91.4 19.5 %all-to-all-start.2 = ((bf16[16,24,128]{2,1,0:T(8,128)(2,1)}), bf16[16,24,128]{2,1,0:T(8,128)(2,1)S(1)}, u32[]{:S(2)}, u32[]{:S(2)}) async-start(bf16[16,24,128]{2,1,0:T(8,128)(2,1)} %broadcast_in_dim.32), calls=%async_computation.2 | async-start | bytes 196608 | tf_op jit(solution)/shard_map/all_to_all | solution.py:24
  98.9 23.5 %copy-start.13 = (s32[56]{0:T(128)S(1)}, s32[56]{0:T(128)}, u32[]{:S(2)}) copy-start(s32[56]{0:T(128)} %param.9) | copy-start | bytes 676
  113.0 27.3 %all-to-all-start.4 = ((bf16[16,56,512]{2,1,0:T(8,128)(2,1)}), bf16[16,56,512]{2,1,0:T(8,128)(2,1)S(1)}, u32[]{:S(2)}, u32[]{:S(2)}) async-start(bf16[16,56,512]{2,1,0:T(8,128)(2,1)} %broadcast_in_dim.34), calls=%async_computation.4 | async-start | bytes 1835008 | tf_op jit(solution)/shard_map/all_to_all | solution.py:24
  116.9 36.2 %copy-start.6 = (bf16[512,512]{1,0:T(8,128)(2,1)}, bf16[512,512]{1,0:T(8,128)(2,1)S(1)}, u32[]{:S(2)}) copy-start(bf16[512,512]{1,0:T(8,128)(2,1)S(1)} %fusion.21) | copy-start | bytes 1572868
  116.9 21.4 %collective-permute-start.6 = (bf16[512,512]{1,0:T(8,128)(2,1)S(1)}, bf16[512,512]{1,0:T(8,128)(2,1)S(1)}, u32[]{:S(2)}, u32[]{:S(2)}) collective-permute-start(bf16[512,512]{1,0:T(8,128)(2,1)S(1)} %fusion.21), channel_id=1, source_target_pairs={{0,1},{1,0},{2,3},{3,2},{4,5},{5,4},{6,7},{7,6},{8,9},{9,8},{10,11... | collective-permute-start | bytes 1572872 | tf_op jit(solution)/shard_map/ppermute | solution.py:32
  140.4 16.5 %all-to-all-start.6 = ((bf16[16,56,512]{2,1,0:T(8,128)(2,1)}), bf16[16,56,512]{2,1,0:T(8,128)(2,1)S(1)}, u32[]{:S(2)}, u32[]{:S(2)}) async-start(bf16[16,56,512]{2,1,0:T(8,128)(2,1)} %bitcast.15), calls=%async_computation.6 | async-start | bytes 1835008 | tf_op jit(solution)/shard_map/all_to_all | solution.py:24
  156.8 18.5 %all-to-all-start.5 = ((bf16[16,64,512]{2,1,0:T(8,128)(2,1)}), bf16[16,64,512]{2,1,0:T(8,128)(2,1)S(1)}, u32[]{:S(2)}, u32[]{:S(2)}) async-start(bf16[16,64,512]{2,1,0:T(8,128)(2,1)} %pad_maximum_fusion.3), calls=%async_computation.5 | async-start | bytes 2097152 | tf_op jit(solution)/shard_map/all_to_all | solution.py:24
  163.5 17.3 %copy-start.7 = (bf16[512,512]{1,0:T(8,128)(2,1)S(1)}, bf16[512,512]{1,0:T(8,128)(2,1)}, u32[]{:S(2)}) copy-start(bf16[512,512]{1,0:T(8,128)(2,1)} %copy-done.6) | copy-start | bytes 1572868
  177.0 16.1 %all-to-all-start.7 = ((bf16[16,52,128]{2,1,0:T(8,128)(2,1)}), bf16[16,52,128]{2,1,0:T(8,128)(2,1)S(1)}, u32[]{:S(2)}, u32[]{:S(2)}) async-start(bf16[16,52,128]{2,1,0:T(8,128)(2,1)} %pad_maximum_fusion.7), calls=%async_computation.7 | async-start | bytes 458752 | tf_op jit(solution)/shard_map/all_to_all | solution.py:24
  197.6 14.1 %collective-permute-start.9 = (f32[512,512]{1,0:T(8,128)}, f32[512,512]{1,0:T(8,128)S(1)}, u32[]{:S(2)}, u32[]{:S(2)}) collective-permute-start(f32[512,512]{1,0:T(8,128)} %fusion.11), channel_id=1, source_target_pairs={{0,1},{1,0},{2,3},{3,2},{4,5},{5,4},{6,7},{7,6},{8,9},{9,8},{10,11... | collective-permute-start | bytes 3145736 | tf_op jit(solution)/shard_map/ppermute | solution.py:32
  (8 other events, 34.3 us)

commit v8 on v7

--- a/solution.py
+++ b/solution.py
@@ -15,7 +15,6 @@
 NZ, NX, NY, NC = 16, 4, 4, 2
 XY = ("x", "y")
 SWAP = [(0, 1), (1, 0)]
-NEAR = [(0, 1), (1, 0), (2, 3), (3, 2)]
 f32 = jnp.float32
 bf16 = jnp.bfloat16
 
@@ -100,25 +99,23 @@
     emb = proj_out.shape[1]
     cen = centres.shape[0]
     images = NX * NY * rows
-    lanes = emb // 4
     zi, xi, yi, ci = (lax.axis_index(a) for a in ("z", "x", "y", "c"))
 
     from_left = shift(features, "x", 1)
     from_right = shift(features, "x", 3)
     own_cols = proj_in.T
-    own_out = spread(lax.dynamic_slice_in_dim(proj_out, ci * (emb // 2) + lax.rem(yi, 2) * lanes, lanes, 1), "z", NZ)
-    own_cols = jnp.concatenate([own_cols, lax.ppermute(own_cols, "y", NEAR)], axis=0)
+    own_out = spread(lax.dynamic_slice_in_dim(proj_out, ci * (emb // 2), emb // 2, 1), "z", NZ)
+    own_cols = jnp.concatenate([own_cols, lax.ppermute(own_cols, "y", [(0, 1), (1, 0), (2, 3), (3, 2)])], axis=0)
     own_cols = jnp.concatenate([own_cols, lax.ppermute(own_cols, "y", [(0, 3), (3, 0), (1, 2), (2, 1)])], axis=0)
     from_far = shift(from_left, "x", 1)
     other_cols = partner(own_cols)
     seat = jnp.stack([xi, yi, ci]).astype(jnp.int32)
     part = partial_hidden(seat, (features, from_left, from_right, from_far), own_cols, other_cols, cols)
-    part = exchange(part, "x").reshape(NZ, cols, 128)
-    part, labels = lax.optimization_barrier((part, labels))
     all_labels = lax.dynamic_update_slice_in_dim(jnp.zeros(NY * rows, jnp.int32), labels, yi * rows, 0)
     all_labels = lax.psum(all_labels, "y")
     all_labels = lax.dynamic_update_slice_in_dim(jnp.zeros(images, jnp.int32), all_labels, xi * NY * rows, 0)
     all_labels = lax.psum(all_labels, "x")
+    part = exchange(part, "x").reshape(NZ, cols, 128)
 
     all_labels = all_labels.reshape(images, 1)
     wide = centres.astype(f32)
@@ -131,9 +128,6 @@
     position = jnp.concatenate([(chip + ci) * cen + step, (chip + 1 - ci) * cen + step])
     target = all_labels == position[None, :]
 
-    beside_out = lax.ppermute(own_out, "y", NEAR)
-    even = lax.rem(yi, 2) == 0
-    own_out = jnp.concatenate([jnp.where(even, own_out, beside_out), jnp.where(even, beside_out, own_out)], axis=2)
     other_out = partner(own_out)
     hidden = jnp.sum(exchange(part, "z").astype(f32), axis=0).astype(bf16)
     hidden = spread(hidden, "z", NZ).reshape(NZ * cols, 128)

time: 217 us -> 238 us (1.097)
  the two profiles are of different devices: /device:TPU:1 before, /device:TPU:6 now
where the time goes in v8:
time: 238 us; the launch traced here: 234 us
  starting transfers between devices  67.6 us (28%)
  waiting for transfers between devices  65.1 us (27%)
  blocking collectives  55.7 us (23%)
  matrix products  20.8 us (9%)
  other arithmetic  8.54 us (4%)
  local copies, waits for them, and re-layouts  8.21 us (3%)
  Pallas kernels  6.44 us (3%)
    all_to_all x7, waiting for transfers between devices, exchange(): return lax.all_to_all(blocks, axis, 0, 0)  47.2 us
    all_to_all x7, starting transfers between devices, exchange(): return lax.all_to_all(blocks, axis, 0, 0)  40.5 us
    all_to_all x1, blocking collectives, exchange(): return lax.all_to_all(blocks, axis, 0, 0)  36.9 us
    psum x1, blocking collectives, step_of(): all_labels = lax.psum(all_labels, 'y')  11 us
    ppermute x3, starting transfers between devices, shift(): return lax.ppermute(block, axis, [(i, (i + by) % 4) for i in range(4)])  10.9 us
    ppermute x3, waiting for transfers between devices, shift(): return lax.ppermute(block, axis, [(i, (i + by) % 4) for i in range(4)])  9.09 us
    psum x1, blocking collectives, step_of(): all_labels = lax.psum(all_labels, 'x')  7.8 us
    ppermute x4, starting transfers between devices, partner(): return lax.ppermute(block, 'c', SWAP)  7.67 us
  transfers between devices with their start and end apart: 16, of which 9 were waited for; matrix products, arithmetic and copies ran while one was open for 11% of the time, Pallas kernels for 0%

profile of v8, /device:TPU:6, one launch (start us, length us, event | category | flops | bytes accessed | tf_op | source)
XLA Modules:
  0.0 233.8 jit_solution(12459952636491489572)
XLA Ops:
  0.7 3.6 %collective-permute-start.4 = (bf16[24,3840]{1,0:T(8,128)(2,1)}, bf16[24,3840]{1,0:T(8,128)(2,1)S(1)}, u32[]{:S(2)}, u32[]{:S(2)}) collective-permute-start(bf16[24,3840]{1,0:T(8,128)(2,1)} %bitcast.61), channel_id=1, source_target_pairs={{0,2},{2,0},{4,6},{6,4},{1,3},{3,1},{5,7},{7,5},{8,10},{10,8},{12,... | collective-permute-start | bytes 552968 | tf_op jit(solution)/shard_map/ppermute | solution.py:108
  4.3 5.0 %collective-permute-done.4 = bf16[24,3840]{1,0:T(8,128)(2,1)S(1)} collective-permute-done((bf16[24,3840]{1,0:T(8,128)(2,1)}, bf16[24,3840]{1,0:T(8,128)(2,1)S(1)}, u32[]{:S(2)}, u32[]{:S(2)}) %collective-permute-start.4) | collective-permute-done | bytes 184352 | tf_op jit(solution)/shard_map/ppermute | solution.py:108
  10.2 4.9 %collective-permute-start.5 = (bf16[48,3840]{1,0:T(8,128)(2,1)S(1)}, bf16[48,3840]{1,0:T(8,128)(2,1)S(1)}, u32[]{:S(2)}, u32[]{:S(2)}) collective-permute-start(bf16[48,3840]{1,0:T(8,128)(2,1)S(1)} %pad_maximum_fusion.5), channel_id=1, source_target_pairs={{0,6},{6,0},{2,4},{4,2},{1,7},{7,1},{3,5},{5,3},{8,14},{14,8},{10,... | collective-permute-start | bytes 1105928 | tf_op jit(solution)/shard_map/ppermute | solution.py:109
  15.2 3.9 %collective-permute-start.1 = (bf16[56,3840]{1,0:T(8,128)(2,1)}, bf16[56,3840]{1,0:T(8,128)(2,1)S(1)}, u32[]{:S(2)}, u32[]{:S(2)}) collective-permute-start(bf16[56,3840]{1,0:T(8,128)(2,1)} %mine.1), channel_id=1, source_target_pairs={{0,8},{8,16},{16,24},{24,0},{1,9},{9,17},{17,25},{25,1},{2,10},{10... | collective-permute-start | bytes 1290248 | tf_op jit(solution)/shard_map/ppermute | solution.py:35
  19.1 3.8 %collective-permute-done.5 = bf16[48,3840]{1,0:T(8,128)(2,1)S(1)} collective-permute-done((bf16[48,3840]{1,0:T(8,128)(2,1)S(1)}, bf16[48,3840]{1,0:T(8,128)(2,1)S(1)}, u32[]{:S(2)}, u32[]{:S(2)}) %collective-permute-start.5) | collective-permute-done | bytes 368672 | tf_op jit(solution)/shard_map/ppermute | solution.py:109
  28.6 4.3 %collective-permute-start.3 = (bf16[56,3840]{1,0:T(8,128)(2,1)S(1)}, bf16[56,3840]{1,0:T(8,128)(2,1)}, u32[]{:S(2)}, u32[]{:S(2)}) collective-permute-start(bf16[56,3840]{1,0:T(8,128)(2,1)S(1)} %collective-permute-done.1.left), channel_id=1, source_target_pairs={{0,8},{8,16},{16,24},{24,0},{1,9},{9,17},{17,25},{25,1},{2,10},{10... | collective-permute-start | bytes 1290248 | tf_op jit(solution)/shard_map/ppermute | solution.py:35
  33.5 7.9 %collective-permute-done.2.right = bf16[56,3840]{1,0:T(8,128)(2,1)S(1)} collective-permute-done((bf16[56,3840]{1,0:T(8,128)(2,1)}, bf16[56,3840]{1,0:T(8,128)(2,1)S(1)}, u32[]{:S(2)}, u32[]{:S(2)}) %collective-permute-start.2) | collective-permute-done | bytes 430112 | tf_op jit(solution)/shard_map/ppermute | solution.py:35
  46.9 7.5 %all-to-all-start = ((bf16[4,4,24,128]{3,2,1,0:T(8,128)(2,1)}), bf16[4,4,24,128]{3,2,1,0:T(8,128)(2,1)}, u32[]{:S(2)}, u32[]{:S(2)}) async-start(bf16[4,4,24,128]{3,2,1,0:T(8,128)(2,1)} %shard_map.68), calls=%async_computation | async-start | bytes 196608 | tf_op jit(solution)/shard_map/all_to_all | solution.py:23
  54.4 3.8 %all-to-all-done = bf16[4,4,24,128]{3,2,1,0:T(8,128)(2,1)} async-done(((bf16[4,4,24,128]{3,2,1,0:T(8,128)(2,1)}), bf16[4,4,24,128]{3,2,1,0:T(8,128)(2,1)}, u32[]{:S(2)}, u32[]{:S(2)}) %all-to-all-start) | async-done | bytes 98336 | tf_op jit(solution)/shard_map/all_to_all | solution.py:23
  58.2 36.9 %all_to_all.40 = bf16[16,48,256]{2,1,0:T(8,128)(2,1)S(1)} all-to-all(bf16[16,48,256]{2,1,0:T(8,128)(2,1)S(1)} %broadcast_in_dim.33), channel_id=1, replica_groups=mesh['z'=16,'x'=4,'y'=4,'c'=2] {'z'}, dimensions={0} | all-to-all | bytes 786432 | tf_op jit(solution)/shard_map/all_to_all | solution.py:23
  95.2 6.3 %all-to-all-start.1 = ((bf16[16,24,128]{2,1,0:T(8,128)(2,1)}), bf16[16,24,128]{2,1,0:T(8,128)(2,1)S(1)}, u32[]{:S(2)}, u32[]{:S(2)}) async-start(bf16[16,24,128]{2,1,0:T(8,128)(2,1)} %bitcast.4), calls=%async_computation.1 | async-start | bytes 196608 | tf_op jit(solution)/shard_map/all_to_all | solution.py:23
  103.6 11.1 %all-to-all-done.1 = bf16[16,24,128]{2,1,0:T(8,128)(2,1)S(1)} async-done(((bf16[16,24,128]{2,1,0:T(8,128)(2,1)}), bf16[16,24,128]{2,1,0:T(8,128)(2,1)S(1)}, u32[]{:S(2)}, u32[]{:S(2)}) %all-to-all-start.1) | async-done | bytes 98336 | tf_op jit(solution)/shard_map/all_to_all | solution.py:23
  115.4 3.5 %all-to-all-start.2 = ((bf16[16,24,128]{2,1,0:T(8,128)(2,1)}), bf16[16,24,128]{2,1,0:T(8,128)(2,1)S(1)}, u32[]{:S(2)}, u32[]{:S(2)}) async-start(bf16[16,24,128]{2,1,0:T(8,128)(2,1)} %broadcast_in_dim.32), calls=%async_computation.2 | async-start | bytes 196608 | tf_op jit(solution)/shard_map/all_to_all | solution.py:23
  119.0 13.0 %all-to-all-done.2 = bf16[16,24,128]{2,1,0:T(8,128)(2,1)S(1)} async-done(((bf16[16,24,128]{2,1,0:T(8,128)(2,1)}), bf16[16,24,128]{2,1,0:T(8,128)(2,1)S(1)}, u32[]{:S(2)}, u32[]{:S(2)}) %all-to-all-start.2) | async-done | bytes 98336 | tf_op jit(solution)/shard_map/all_to_all | solution.py:23
  134.2 6.9 %all-to-all-start.4 = ((bf16[16,56,512]{2,1,0:T(8,128)(2,1)}), bf16[16,56,512]{2,1,0:T(8,128)(2,1)S(1)}, u32[]{:S(2)}, u32[]{:S(2)}) async-start(bf16[16,56,512]{2,1,0:T(8,128)(2,1)} %broadcast_in_dim.34), calls=%async_computation.4 | async-start | bytes 1835008 | tf_op jit(solution)/shard_map/all_to_all | solution.py:23
  143.5 11.0 %psum.14 = s32[224]{0:T(256)S(1)} all-reduce(s32[224]{0:T(256)S(1)} %dynamic_update_slice.6), channel_id=1, replica_groups=mesh['z'=16,'x'=4,'y'=4,'c'=2] {'y'}, use_global_device_ids=true, to_apply=%region_0.0 | all-reduce | flops 224 | bytes 1792 | tf_op jit(solution)/shard_map/psum | solution.py:115
  154.7 7.8 %psum.15 = s32[896]{0:T(1024)S(1)} all-reduce(s32[896]{0:T(1024)S(1)} %dynamic_update_slice.7), channel_id=1, replica_groups=mesh['z'=16,'x'=4,'y'=4,'c'=2] {'x'}, use_global_device_ids=true, to_apply=%region_1.0 | all-reduce | flops 896 | bytes 7168 | tf_op jit(solution)/shard_map/psum | solution.py:117
  164.6 5.4 %all-to-all-start.6 = ((bf16[16,56,512]{2,1,0:T(8,128)(2,1)}), bf16[16,56,512]{2,1,0:T(8,128)(2,1)S(1)}, u32[]{:S(2)}, u32[]{:S(2)}) async-start(bf16[16,56,512]{2,1,0:T(8,128)(2,1)} %bitcast.15), calls=%async_computation.6 | async-start | bytes 1835008 | tf_op jit(solution)/shard_map/all_to_all | solution.py:23
  170.0 6.9 %fusion.6 = (f32[896]{0:T(1024)S(1)}, f32[896]{0:T(1024)S(1)}, f32[896]{0:T(1024)S(1)}, f32[896]{0:T(1024)S(1)}, f32[896]{0:T(1024)S(1)}, /*index=5*/bf16[896,1024]{1,0:T(8,128)(2,1)}) fusion(s32[1024]{0:T(1024)S(1)} %pad_add_fusion, s32[896]{0:T(1024)S(1)} %psum.15, bf16[896,512]{1,0:T(8,128)(2,1)S(1)} %bitcast.47, ...), kind=kOutput, calls=%fused_computation.13 | convolution fusion | flops 966389376 | bytes 3826688 | tf_op jit(solution)/shard_map/dot_general | solution.py:155
  181.5 7.2 %all-to-all-start.5 = ((bf16[16,64,512]{2,1,0:T(8,128)(2,1)}), bf16[16,64,512]{2,1,0:T(8,128)(2,1)S(1)}, u32[]{:S(2)}, u32[]{:S(2)}) async-start(bf16[16,64,512]{2,1,0:T(8,128)(2,1)} %pad_maximum_fusion.3), calls=%async_computation.5 | async-start | bytes 2097152 | tf_op jit(solution)/shard_map/all_to_all | solution.py:23
  189.3 10.4 %all-to-all-done.5 = bf16[16,64,512]{2,1,0:T(8,128)(2,1)S(1)} async-done(((bf16[16,64,512]{2,1,0:T(8,128)(2,1)}), bf16[16,64,512]{2,1,0:T(8,128)(2,1)S(1)}, u32[]{:S(2)}, u32[]{:S(2)}) %all-to-all-start.5) | async-done | bytes 1048608 | tf_op jit(solution)/shard_map/all_to_all | solution.py:23
  201.3 3.6 %all-to-all-start.7 = ((bf16[16,52,128]{2,1,0:T(8,128)(2,1)}), bf16[16,52,128]{2,1,0:T(8,128)(2,1)S(1)}, u32[]{:S(2)}, u32[]{:S(2)}) async-start(bf16[16,52,128]{2,1,0:T(8,128)(2,1)} %pad_maximum_fusion.6), calls=%async_computation.7 | async-start | bytes 458752 | tf_op jit(solution)/shard_map/all_to_all | solution.py:23
  210.0 8.8 %all-to-all-done.7 = bf16[16,52,128]{2,1,0:T(8,128)(2,1)S(1)} async-done(((bf16[16,52,128]{2,1,0:T(8,128)(2,1)}), bf16[16,52,128]{2,1,0:T(8,128)(2,1)S(1)}, u32[]{:S(2)}, u32[]{:S(2)}) %all-to-all-start.7) | async-done | bytes 213024 | tf_op jit(solution)/shard_map/all_to_all | solution.py:23
  226.1 3.6 %fusion.13.own = f32[512,512]{1,0:T(8,128)} fusion(bf16[1792,512]{1,0:T(8,128)(2,1)S(1)} %pad_maximum_fusion.1, bf16[1024,1792]{0,1:T(8,128)(2,1)} %pad_maximum_fusion), kind=kOutput, calls=%fused_computation.28 | convolution fusion | flops 939524096 | bytes 4718592 | tf_op jit(solution)/shard_map/dot_general | solution.py:218
  (119 shorter events, 45.1 us)
Async XLA Ops:
  0.6 53.8 %copy-start = (bf16[48,512]{1,0:T(8,128)(2,1)S(1)}, bf16[48,512]{1,0:T(8,128)(2,1)}, u32[]{:S(2)}) copy-start(bf16[48,512]{1,0:T(8,128)(2,1)} %param.7) | copy-start | bytes 147460
  0.6 100.8 %copy-start.2 = (bf16[512,512]{1,0:T(8,128)(2,1)S(1)}, bf16[512,512]{1,0:T(8,128)(2,1)}, u32[]{:S(2)}) copy-start(bf16[512,512]{1,0:T(8,128)(2,1)} %centres.1) | copy-start | bytes 1572868
  0.7 8.6 %collective-permute-start.4 = (bf16[24,3840]{1,0:T(8,128)(2,1)}, bf16[24,3840]{1,0:T(8,128)(2,1)S(1)}, u32[]{:S(2)}, u32[]{:S(2)}) collective-permute-start(bf16[24,3840]{1,0:T(8,128)(2,1)} %bitcast.61), channel_id=1, source_target_pairs={{0,2},{2,0},{4,6},{6,4},{1,3},{3,1},{5,7},{7,5},{8,10},{10,8},{12,... | collective-permute-start | bytes 552968 | tf_op jit(solution)/shard_map/ppermute | solution.py:108
  10.2 12.6 %collective-permute-start.5 = (bf16[48,3840]{1,0:T(8,128)(2,1)S(1)}, bf16[48,3840]{1,0:T(8,128)(2,1)S(1)}, u32[]{:S(2)}, u32[]{:S(2)}) collective-permute-start(bf16[48,3840]{1,0:T(8,128)(2,1)S(1)} %pad_maximum_fusion.5), channel_id=1, source_target_pairs={{0,6},{6,0},{2,4},{4,2},{1,7},{7,1},{3,5},{5,3},{8,14},{14,8},{10,... | collective-permute-start | bytes 1105928 | tf_op jit(solution)/shard_map/ppermute | solution.py:109
  15.2 13.4 %collective-permute-start.1 = (bf16[56,3840]{1,0:T(8,128)(2,1)}, bf16[56,3840]{1,0:T(8,128)(2,1)S(1)}, u32[]{:S(2)}, u32[]{:S(2)}) collective-permute-start(bf16[56,3840]{1,0:T(8,128)(2,1)} %mine.1), channel_id=1, source_target_pairs={{0,8},{8,16},{16,24},{24,0},{1,9},{9,17},{17,25},{25,1},{2,10},{10... | collective-permute-start | bytes 1290248 | tf_op jit(solution)/shard_map/ppermute | solution.py:35
  23.8 18.7 %copy-start.3 = (bf16[96,3840]{1,0:T(8,128)(2,1)}, bf16[96,3840]{1,0:T(8,128)(2,1)S(1)}, u32[]{:S(2)}) copy-start(bf16[96,3840]{1,0:T(8,128)(2,1)S(1)} %pad_maximum_fusion.4.own_cols) | copy-start | bytes 2211844
  23.9 18.7 %collective-permute-start.6 = (bf16[96,3840]{1,0:T(8,128)(2,1)S(1)}, bf16[96,3840]{1,0:T(8,128)(2,1)S(1)}, u32[]{:S(2)}, u32[]{:S(2)}) collective-permute-start(bf16[96,3840]{1,0:T(8,128)(2,1)S(1)} %pad_maximum_fusion.4.own_cols), channel_id=1, source_target_pairs={{0,1},{1,0},{2,3},{3,2},{4,5},{5,4},{6,7},{7,6},{8,9},{9,8},{10,11... | collective-permute-start | bytes 2211848 | tf_op jit(solution)/shard_map/ppermute | solution.py:31
  25.8 15.6 %collective-permute-start.2 = (bf16[56,3840]{1,0:T(8,128)(2,1)}, bf16[56,3840]{1,0:T(8,128)(2,1)S(1)}, u32[]{:S(2)}, u32[]{:S(2)}) collective-permute-start(bf16[56,3840]{1,0:T(8,128)(2,1)} %mine.1), channel_id=1, source_target_pairs={{0,24},{8,0},{16,8},{24,16},{1,25},{9,1},{17,9},{25,17},{2,26},{10... | collective-permute-start | bytes 1290248 | tf_op jit(solution)/shard_map/ppermute | solution.py:35
  28.5 14.0 %copy-start.7 = (bf16[56,3840]{1,0:T(8,128)(2,1)}, bf16[56,3840]{1,0:T(8,128)(2,1)S(1)}, u32[]{:S(2)}) copy-start(bf16[56,3840]{1,0:T(8,128)(2,1)S(1)} %collective-permute-done.1.left) | copy-start | bytes 1290244
  28.6 14.0 %collective-permute-start.3 = (bf16[56,3840]{1,0:T(8,128)(2,1)S(1)}, bf16[56,3840]{1,0:T(8,128)(2,1)}, u32[]{:S(2)}, u32[]{:S(2)}) collective-permute-start(bf16[56,3840]{1,0:T(8,128)(2,1)S(1)} %collective-permute-done.1.left), channel_id=1, source_target_pairs={{0,8},{8,16},{16,24},{24,0},{1,9},{9,17},{17,25},{25,1},{2,10},{10... | collective-permute-start | bytes 1290248 | tf_op jit(solution)/shard_map/ppermute | solution.py:35
  46.9 11.3 %all-to-all-start = ((bf16[4,4,24,128]{3,2,1,0:T(8,128)(2,1)}), bf16[4,4,24,128]{3,2,1,0:T(8,128)(2,1)}, u32[]{:S(2)}, u32[]{:S(2)}) async-start(bf16[4,4,24,128]{3,2,1,0:T(8,128)(2,1)} %shard_map.68), calls=%async_computation | async-start | bytes 196608 | tf_op jit(solution)/shard_map/all_to_all | solution.py:23
  95.2 19.6 %all-to-all-start.1 = ((bf16[16,24,128]{2,1,0:T(8,128)(2,1)}), bf16[16,24,128]{2,1,0:T(8,128)(2,1)S(1)}, u32[]{:S(2)}, u32[]{:S(2)}) async-start(bf16[16,24,128]{2,1,0:T(8,128)(2,1)} %bitcast.4), calls=%async_computation.1 | async-start | bytes 196608 | tf_op jit(solution)/shard_map/all_to_all | solution.py:23
  101.7 17.3 %collective-permute-start.7 = (bf16[16,48,256]{2,1,0:T(8,128)(2,1)S(1)}, bf16[16,48,256]{2,1,0:T(8,128)(2,1)S(1)}, u32[]{:S(2)}, u32[]{:S(2)}) collective-permute-start(bf16[16,48,256]{2,1,0:T(8,128)(2,1)S(1)} %all_to_all.40), channel_id=1, source_target_pairs={{0,1},{1,0},{2,3},{3,2},{4,5},{5,4},{6,7},{7,6},{8,9},{9,8},{10,11... | collective-permute-start | bytes 1179656 | tf_op jit(solution)/shard_map/ppermute | solution.py:31
  115.4 16.6 %all-to-all-start.2 = ((bf16[16,24,128]{2,1,0:T(8,128)(2,1)}), bf16[16,24,128]{2,1,0:T(8,128)(2,1)S(1)}, u32[]{:S(2)}, u32[]{:S(2)}) async-start(bf16[16,24,128]{2,1,0:T(8,128)(2,1)} %broadcast_in_dim.32), calls=%async_computation.2 | async-start | bytes 196608 | tf_op jit(solution)/shard_map/all_to_all | solution.py:23
  118.9 24.3 %copy-start.10 = (s32[56]{0:T(128)S(1)}, s32[56]{0:T(128)}, u32[]{:S(2)}) copy-start(s32[56]{0:T(128)} %param.9) | copy-start | bytes 676
  134.2 30.4 %all-to-all-start.4 = ((bf16[16,56,512]{2,1,0:T(8,128)(2,1)}), bf16[16,56,512]{2,1,0:T(8,128)(2,1)S(1)}, u32[]{:S(2)}, u32[]{:S(2)}) async-start(bf16[16,56,512]{2,1,0:T(8,128)(2,1)} %broadcast_in_dim.34), calls=%async_computation.4 | async-start | bytes 1835008 | tf_op jit(solution)/shard_map/all_to_all | solution.py:23
  141.3 36.5 %copy-start.6 = (bf16[512,512]{1,0:T(8,128)(2,1)}, bf16[512,512]{1,0:T(8,128)(2,1)S(1)}, u32[]{:S(2)}) copy-start(bf16[512,512]{1,0:T(8,128)(2,1)S(1)} %fusion.21) | copy-start | bytes 1572868
  141.3 21.2 %collective-permute-start = (bf16[512,512]{1,0:T(8,128)(2,1)S(1)}, bf16[512,512]{1,0:T(8,128)(2,1)S(1)}, u32[]{:S(2)}, u32[]{:S(2)}) collective-permute-start(bf16[512,512]{1,0:T(8,128)(2,1)S(1)} %fusion.21), channel_id=1, source_target_pairs={{0,1},{1,0},{2,3},{3,2},{4,5},{5,4},{6,7},{7,6},{8,9},{9,8},{10,11... | collective-permute-start | bytes 1572872 | tf_op jit(solution)/shard_map/ppermute | solution.py:31
  162.5 15.3 %copy-start.9 = (bf16[512,512]{1,0:T(8,128)(2,1)}, bf16[512,512]{1,0:T(8,128)(2,1)S(1)}, u32[]{:S(2)}) copy-start(bf16[512,512]{1,0:T(8,128)(2,1)S(1)} %collective-permute-done) | copy-start | bytes 1572868
  164.6 16.9 %all-to-all-start.6 = ((bf16[16,56,512]{2,1,0:T(8,128)(2,1)}), bf16[16,56,512]{2,1,0:T(8,128)(2,1)S(1)}, u32[]{:S(2)}, u32[]{:S(2)}) async-start(bf16[16,56,512]{2,1,0:T(8,128)(2,1)} %bitcast.15), calls=%async_computation.6 | async-start | bytes 1835008 | tf_op jit(solution)/shard_map/all_to_all | solution.py:23
  181.5 18.2 %all-to-all-start.5 = ((bf16[16,64,512]{2,1,0:T(8,128)(2,1)}), bf16[16,64,512]{2,1,0:T(8,128)(2,1)S(1)}, u32[]{:S(2)}, u32[]{:S(2)}) async-start(bf16[16,64,512]{2,1,0:T(8,128)(2,1)} %pad_maximum_fusion.3), calls=%async_computation.5 | async-start | bytes 2097152 | tf_op jit(solution)/shard_map/all_to_all | solution.py:23
  201.3 17.5 %all-to-all-start.7 = ((bf16[16,52,128]{2,1,0:T(8,128)(2,1)}), bf16[16,52,128]{2,1,0:T(8,128)(2,1)S(1)}, u32[]{:S(2)}, u32[]{:S(2)}) async-start(bf16[16,52,128]{2,1,0:T(8,128)(2,1)} %pad_maximum_fusion.6), calls=%async_computation.7 | async-start | bytes 458752 | tf_op jit(solution)/shard_map/all_to_all | solution.py:23
  219.2 2.0 copy-start.1
  223.4 6.4 %collective-permute-start.8 = (f32[512,512]{1,0:T(8,128)}, f32[512,512]{1,0:T(8,128)S(1)}, u32[]{:S(2)}, u32[]{:S(2)}) collective-permute-start(f32[512,512]{1,0:T(8,128)} %fusion.11), channel_id=1, source_target_pairs={{0,1},{1,0},{2,3},{3,2},{4,5},{5,4},{6,7},{7,6},{8,9},{9,8},{10,11... | collective-permute-start | bytes 3145736 | tf_op jit(solution)/shard_map/ppermute | solution.py:31
  (3 other events, 3.0 us)
